TPU v7x, 32 devices: a whole 2x2x4 slice. The times are simulated.
32 devices in a mesh: seq: 4 (over x, core), fsdp: 8 (over z, y).
Axes of the slice: x: 2, y: 2, z: 4, core: 2. Of those that a mesh axis runs over, the one named last changes fastest.
Arguments:
- inputs: bfloat16 [4096, 2304], P(('fsdp', 'seq')), may hold values from -6 to 6
- cotangent: bfloat16 [4096, 2304], P(('fsdp', 'seq')), may hold values from -6 to 6
- segments: int32 [4096], replicated, may hold values from 0 to 3, never falling along the last dimension, each value on 1 to 2048 neighbouring positions
- first_gain: bfloat16 [2304], P(('seq', 'fsdp')), may hold values from -0.5 to 0.5
- second_gain: bfloat16 [2304], P(('seq', 'fsdp')), may hold values from -0.5 to 0.5
- third_gain: bfloat16 [2304], P(('seq', 'fsdp')), may hold values from -0.5 to 0.5
- fourth_gain: bfloat16 [2304], P(('seq', 'fsdp')), may hold values from -0.5 to 0.5
- query_weight: bfloat16 [2304, 2048], P(('seq', 'fsdp')), may hold values from -0.125 to 0.125
- key_weight: bfloat16 [2304, 1024], P(('seq', 'fsdp')), may hold values from -0.125 to 0.125
- value_weight: bfloat16 [2304, 1024], P(('seq', 'fsdp')), may hold values from -0.125 to 0.125
- output_weight: bfloat16 [2304, 2048], P(('seq', 'fsdp')), may hold values from -0.125 to 0.125
- gate_weight: bfloat16 [9216, 2304], P(('seq', 'fsdp')), may hold values from -0.125 to 0.125
- up_weight: bfloat16 [9216, 2304], P(('seq', 'fsdp')), may hold values from -0.125 to 0.125
- down_weight: bfloat16 [9216, 2304], P(('seq', 'fsdp')), may hold values from -0.0625 to 0.0625
Outputs:
- layer_out: float32 [4096, 2304], P(('fsdp', 'seq'))
- input_grad: float32 [4096, 2304], P(('fsdp', 'seq'))
- first_grad: float32 [2304], P(('seq', 'fsdp'))
- second_grad: float32 [2304], P(('seq', 'fsdp'))
- third_grad: float32 [2304], P(('seq', 'fsdp'))
- fourth_grad: float32 [2304], P(('seq', 'fsdp'))
- query_grad: float32 [2304, 2048], P(('seq', 'fsdp'))
- key_grad: float32 [2304, 1024], P(('seq', 'fsdp'))
- value_grad: float32 [2304, 1024], P(('seq', 'fsdp'))
- output_grad: float32 [2304, 2048], P(('seq', 'fsdp'))
- gate_grad: float32 [9216, 2304], P(('seq', 'fsdp'))
- up_grad: float32 [9216, 2304], P(('seq', 'fsdp'))
- down_grad: float32 [9216, 2304], P(('seq', 'fsdp'))
Inputs may be any that keep to these rules, and one draw needn't show every extreme that they name: `segments`: document numbers never fall along the batch; every document number appears, each document holds at most 2048 tokens, and one holds exactly 2048.
All inputs are finite; a program needn't handle non-finite values.
Results may differ from a plain program's by a relative error of at most 0.02.
Values may be sent and summed in bfloat16 or wider, within the bound.
No kernel may reach another device: no remote copies, remote signals or barrier semaphores. Data moves between devices by JAX's collectives and lax.ppermute only.
A program may use at most 384 MiB of HBM per device.

v0:
```python
import functools

import jax
import jax.numpy as jnp
from jax import lax
from jax.experimental import pallas as pl
from jax.experimental.pallas import tpu as pltpu
from jax.sharding import PartitionSpec as P


HEAD_DIM = 256


epsilon = 1e-06
softcap = 50.0
rope_base = 10000.0
gelu_coef = 0.7978845608028654
cubic_coef = 0.044715


def rms_forward(values, gain):
    scaling = lax.rsqrt(jnp.mean(values * values, axis=-1, keepdims=True) + epsilon)
    return values * scaling * (1.0 + gain.astype(jnp.float32))


def rms_backward(values, gain, upstream):
    scaling = lax.rsqrt(jnp.mean(values * values, axis=-1, keepdims=True) + epsilon)
    weighted = upstream * (1.0 + gain.astype(jnp.float32))
    inner = jnp.mean(weighted * values, axis=-1, keepdims=True)
    grad_values = scaling * weighted - values * (scaling * scaling * scaling) * inner
    grad_gain = jnp.sum(upstream * values * scaling, axis=0)
    return (grad_values, grad_gain)


def rotation(positions):
    half = HEAD_DIM // 2
    frequency = jnp.power(rope_base, -jnp.arange(half, dtype=jnp.float32) / half)
    angles = positions.astype(jnp.float32)[:, None] * frequency[None, :]
    return (jnp.cos(angles), jnp.sin(angles))


def rope_apply(values, cosine, sine, inverse):
    rows = values.shape[0]
    half = HEAD_DIM // 2
    shaped = values.reshape(rows, -1, HEAD_DIM)
    first = shaped[:, :, :half]
    second = shaped[:, :, half:]
    cosine_row = cosine[:, None, :]
    sine_row = sine[:, None, :]
    if inverse:
        sine_row = -sine_row
    turned = jnp.concatenate(
        [first * cosine_row - second * sine_row, second * cosine_row + first * sine_row], axis=-1
    )
    return turned.reshape(rows, -1)


def gelu_value(gate):
    bent = jnp.tanh(gelu_coef * (gate + cubic_coef * gate * gate * gate))
    return 0.5 * gate * (1.0 + bent)


def gelu_slope(gate):
    bent = jnp.tanh(gelu_coef * (gate + cubic_coef * gate * gate * gate))
    return 0.5 * (1.0 + bent) + 0.5 * gate * (1.0 - bent * bent) * gelu_coef * (
        1.0 + 3.0 * cubic_coef * gate * gate
    )


def contract_rows(left, right):
    return lax.dot_general(
        left, right, (((0,), (0,)), ((), ())), preferred_element_type=jnp.float32
    )


def contract_cols(left, right):
    return lax.dot_general(
        left, right, (((1,), (1,)), ((), ())), preferred_element_type=jnp.float32
    )


def attend_kernel(heads, live_ref, query_ref, pair_ref, at_ref, pos_ref, start_ref, mixed_ref, log_ref, sums, totals):
    step = pl.program_id(0)
    scale = HEAD_DIM ** (-0.5)

    @pl.when(step == 0)
    def _():
        sums[...] = jnp.zeros_like(sums)
        totals[...] = jnp.zeros_like(totals)

    @pl.when(live_ref[step] > 0)
    def _():
        keys = pair_ref[:, :HEAD_DIM]
        turned = pair_ref[:, HEAD_DIM:].T
        allowed = (at_ref[...] >= start_ref[...]) & (at_ref[...] <= pos_ref[...])
        for head in range(heads):
            cols = slice(head * HEAD_DIM, (head + 1) * HEAD_DIM)
            bent = jnp.tanh(contract_cols(keys, query_ref[:, cols]) * (scale / softcap))
            expo = jnp.where(allowed, jnp.exp(softcap * bent), 0.0)
            totals[head : head + 1, :] += jnp.sum(expo, axis=0, keepdims=True)
            sums[head] += jnp.dot(turned, expo.astype(jnp.bfloat16), preferred_element_type=jnp.float32)

    @pl.when(step == pl.num_programs(0) - 1)
    def _():
        log_ref[...] = jnp.log(totals[...])
        for head in range(heads):
            cols = slice(head * HEAD_DIM, (head + 1) * HEAD_DIM)
            mixed = sums[head] / totals[head : head + 1, :]
            mixed_ref[:, cols] = mixed.T.astype(jnp.bfloat16)


def attend(live, query, pairs, key_at, query_pos, query_start, block):
    rows, width = query.shape
    heads = width // HEAD_DIM
    steps = pairs.shape[0] // block
    row = pl.BlockSpec((1, rows), lambda i, live: (0, 0))
    return pl.pallas_call(
        functools.partial(attend_kernel, heads),
        grid_spec=pltpu.PrefetchScalarGridSpec(
            num_scalar_prefetch=1,
            grid=(steps,),
            in_specs=[
                pl.BlockSpec((rows, width), lambda i, live: (0, 0)),
                pl.BlockSpec((block, pairs.shape[1]), lambda i, live: (i, 0)),
                pl.BlockSpec((block, 1), lambda i, live: (i, 0)),
                row,
                row,
            ],
            out_specs=[
                pl.BlockSpec((rows, width), lambda i, live: (0, 0)),
                pl.BlockSpec((heads, rows), lambda i, live: (0, 0)),
            ],
            scratch_shapes=[
                pltpu.VMEM((heads, HEAD_DIM, rows), jnp.float32),
                pltpu.VMEM((heads, rows), jnp.float32),
            ],
        ),
        out_shape=[
            jax.ShapeDtypeStruct((rows, width), jnp.bfloat16),
            jax.ShapeDtypeStruct((heads, rows), jnp.float32),
        ],
        cost_estimate=pl.CostEstimate(
            flops=4 * rows * width * pairs.shape[0],
            bytes_accessed=2 * pairs.size + 4 * query.size,
            transcendentals=2 * rows * heads * pairs.shape[0],
        ),
        name="attend",
    )(live, query, pairs, key_at[:, None], query_pos[None, :], query_start[None, :])


def attend_back_kernel(
    heads, first, last, live_ref, query_ref, grad_ref, pair_ref, at_ref, pos_ref, start_ref, log_ref,
    delta_ref, carry_ref, query_grad_ref, pair_grad_ref, sums,
):
    step = pl.program_id(0)
    scale = HEAD_DIM ** (-0.5)

    @pl.when(step == 0)
    def _():
        sums[...] = carry_ref[...]

    @pl.when(live_ref[step + first] == 0)
    def _():
        pair_grad_ref[...] = jnp.zeros_like(pair_grad_ref)

    @pl.when(live_ref[step + first] > 0)
    def _():
        keys = pair_ref[:, :HEAD_DIM]
        values = pair_ref[:, HEAD_DIM:]
        allowed = (at_ref[...] >= start_ref[...]) & (at_ref[...] <= pos_ref[...])
        key_grad = None
        value_grad = None
        for head in range(heads):
            cols = slice(head * HEAD_DIM, (head + 1) * HEAD_DIM)
            query = query_ref[:, cols]
            grad = grad_ref[:, cols]
            bent = jnp.tanh(contract_cols(keys, query) * (scale / softcap))
            probs = jnp.where(allowed, jnp.exp(softcap * bent - log_ref[head : head + 1, :]), 0.0)
            value_part = jnp.dot(probs.astype(jnp.bfloat16), grad, preferred_element_type=jnp.float32)
            slope = contract_cols(values, grad) - delta_ref[head : head + 1, :]
            score = (probs * slope * (1.0 - bent * bent)).astype(jnp.bfloat16)
            key_part = jnp.dot(score, query, preferred_element_type=jnp.float32)
            sums[:, cols] += contract_rows(score, keys)
            key_grad = key_part if key_grad is None else key_grad + key_part
            value_grad = value_part if value_grad is None else value_grad + value_part
        pair_grad_ref[:, :HEAD_DIM] = (key_grad * scale).astype(jnp.bfloat16)
        pair_grad_ref[:, HEAD_DIM:] = value_grad.astype(jnp.bfloat16)

    @pl.when(step == pl.num_programs(0) - 1)
    def _():
        query_grad_ref[...] = sums[...] * scale if last else sums[...]


def attend_back(
    live, query, grad, pairs, key_at, query_pos, query_start, log_totals, delta, carry, block, first, steps
):
    rows, width = query.shape
    heads = width // HEAD_DIM
    row = pl.BlockSpec((1, rows), lambda i, live: (0, 0))
    head_row = pl.BlockSpec((heads, rows), lambda i, live: (0, 0))
    full = pl.BlockSpec((rows, width), lambda i, live: (0, 0))
    pair_spec = pl.BlockSpec((block, pairs.shape[1]), lambda i, live: (i + first, 0))
    out_spec = pl.BlockSpec((block, pairs.shape[1]), lambda i, live: (i, 0))
    return pl.pallas_call(
        functools.partial(attend_back_kernel, heads, first, first == 0),
        grid_spec=pltpu.PrefetchScalarGridSpec(
            num_scalar_prefetch=1,
            grid=(steps,),
            in_specs=[
                full,
                full,
                pair_spec,
                pl.BlockSpec((block, 1), lambda i, live: (i + first, 0)),
                row,
                row,
                head_row,
                head_row,
                full,
            ],
            out_specs=[full, out_spec],
            scratch_shapes=[pltpu.VMEM((rows, width), jnp.float32)],
        ),
        out_shape=[
            jax.ShapeDtypeStruct((rows, width), jnp.float32),
            jax.ShapeDtypeStruct((steps * block, pairs.shape[1]), jnp.bfloat16),
        ],
        cost_estimate=pl.CostEstimate(
            flops=10 * rows * width * steps * block,
            bytes_accessed=4 * steps * block * width + 8 * query.size,
            transcendentals=2 * rows * heads * steps * block,
        ),
        name="attend_back",
    )(live, query, grad, pairs, key_at[:, None], query_pos[None, :], query_start[None, :], log_totals, delta, carry)


def after(value, *others):
    return lax.optimization_barrier((value,) + others)[0]


def layer(
    inputs,
    cotangent,
    segments,
    first_gain,
    second_gain,
    third_gain,
    fourth_gain,
    query_weight,
    key_weight,
    value_weight,
    output_weight,
    gate_weight,
    up_weight,
    down_weight,
):
    tokens = inputs.shape[0]
    width = inputs.shape[1]
    own_rows = query_weight.shape[0]
    seq_count = lax.axis_size("seq")
    count = lax.axis_size("fsdp")
    seq_rank = lax.axis_index("seq")
    fsdp_rank = lax.axis_index("fsdp")
    half = count // 2
    bf16 = jnp.bfloat16
    head_rows = tokens * seq_count
    query_cols = query_weight.shape[1] // seq_count
    key_cols = key_weight.shape[1] // seq_count

    cycle = [2 * i for i in range(half)] + [2 * i + 1 for i in reversed(range(half))]
    ahead = [(cycle[i], cycle[(i + 1) % count]) for i in range(count)]
    behind = [(b, a) for a, b in ahead]
    place = jnp.where(fsdp_rank % 2 == 0, fsdp_rank // 2, count - 1 - fsdp_rank // 2)

    def rank_at(step):
        spot = lax.rem(place + step + count, count)
        return jnp.where(spot < half, 2 * spot, 2 * (count - 1 - spot) + 1)

    def flip(value, bits):
        return lax.ppermute(value, "seq", [(i, i ^ bits) for i in range(seq_count)])

    def hop(value, pairs):
        return lax.ppermute(value, "fsdp", pairs)

    def ring_gather(value, axis):
        groups = [[value]]
        from_behind = value
        from_ahead = value
        for _ in range(1, half):
            from_behind = hop(from_behind, ahead)
            from_ahead = hop(from_ahead, behind)
            groups.append([from_behind, from_ahead])
        cut = value.shape[axis] // 2
        low = lax.slice_in_dim(from_behind, 0, cut, axis=axis)
        high = lax.slice_in_dim(from_ahead, cut, value.shape[axis], axis=axis)
        low = hop(low, ahead)
        high = hop(high, behind)
        groups.append([jnp.concatenate([low, high], axis=axis)])
        return groups

    def ring_scatter(part_at, axis):
        far = part_at(half)
        cut = far.shape[axis] // 2
        low = lax.slice_in_dim(far, 0, cut, axis=axis).astype(bf16)
        high = lax.slice_in_dim(far, cut, far.shape[axis], axis=axis).astype(bf16)
        low, high = lax.optimization_barrier((hop(low, ahead), hop(high, behind)))
        low = low.astype(jnp.float32)
        high = high.astype(jnp.float32)
        blank = jnp.zeros_like(low)
        onward = jnp.concatenate([low, blank], axis=axis)
        back = jnp.concatenate([blank, high], axis=axis)
        for step in range(half - 1, 0, -1):
            onward = (part_at(step) + onward).astype(bf16)
            back = (part_at(-step) + back).astype(bf16)
            onward, back = lax.optimization_barrier((hop(onward, ahead), hop(back, behind)))
            onward = onward.astype(jnp.float32)
            back = back.astype(jnp.float32)
        return part_at(0) + onward + back

    def seq_gather(value):
        across = flip(value, 2)
        beside = flip(value, 1)
        return [value, beside, across, flip(across, 1)]

    def seq_scatter(parts):
        near = flip(parts[1].astype(bf16), 1).astype(jnp.float32)
        far = flip(parts[3].astype(bf16), 1).astype(jnp.float32)
        across = flip((parts[2] + far).astype(bf16), 2).astype(jnp.float32)
        return parts[0] + near + across

    def turn(value, step):
        return hop(value, [(i, (i + step) % count) for i in range(count)])

    packed = jnp.stack([first_gain, second_gain, third_gain, fourth_gain])
    row = jnp.zeros((seq_count, 4, own_rows), bf16)
    for j in range(seq_count):
        piece = flip(packed, j) if j else packed
        row = lax.dynamic_update_slice(row, piece[None], (seq_rank ^ j, 0, 0))
    gains = jnp.zeros((count, seq_count, 4, own_rows), bf16)
    for step in range(count):
        piece = turn(row, step) if step else row
        gains = lax.dynamic_update_slice(
            gains, piece[None], (lax.rem(fsdp_rank - step + count, count), 0, 0, 0)
        )
    gains = jnp.transpose(gains, (2, 1, 0, 3)).reshape(4, width)
    gain_one, gain_two, gain_three, gain_four = gains[0], gains[1], gains[2], gains[3]

    def columns(weight, rank, size):
        return lax.dynamic_slice_in_dim(weight, rank * size, size, 1)

    def head_columns(rank):
        return jnp.concatenate(
            [
                columns(query_weight, rank, query_cols),
                columns(key_weight, rank, key_cols),
                columns(value_weight, rank, key_cols),
            ],
            axis=1,
        )

    def exchange(pick):
        pieces = [pick(seq_rank)] + [
            flip(pick(seq_rank ^ j), j) for j in range(1, seq_count)
        ]
        chunk = jnp.zeros((seq_count,) + pieces[0].shape, bf16)
        for j, piece in enumerate(pieces):
            chunk = lax.dynamic_update_slice(chunk, piece[None], (seq_rank ^ j, 0, 0))
        return chunk

    def assemble(groups):
        cols = groups[0][0].shape[2]
        whole_weight = jnp.zeros((seq_count, count, own_rows, cols), bf16)
        for step, group in enumerate(groups):
            for rank, piece in zip((rank_at(-step), rank_at(step)), group):
                whole_weight = lax.dynamic_update_slice(
                    whole_weight, piece[:, None], (0, rank, 0, 0)
                )
        return whole_weight.reshape(width, cols)

    head_chunk = exchange(head_columns)
    rows_in = seq_gather(after(inputs, head_chunk))
    out_chunk = exchange(lambda rank: columns(output_weight, rank, query_cols))
    head_groups = ring_gather(head_chunk, 2)
    in_full = assemble(head_groups)

    def block_pos(rank):
        return jnp.concatenate(
            [
                (rank * seq_count + (seq_rank ^ j)) * tokens + jnp.arange(tokens, dtype=jnp.int32)
                for j in range(seq_count)
            ]
        )

    head_pos = block_pos(fsdp_rank)
    head_seg = jnp.concatenate(
        [
            lax.dynamic_slice_in_dim(
                segments, (fsdp_rank * seq_count + (seq_rank ^ j)) * tokens, tokens, 0
            )
            for j in range(seq_count)
        ]
    )
    head_start = jnp.sum((segments[None, :] < head_seg[:, None]).astype(jnp.int32), axis=1)

    head_in = jnp.concatenate(rows_in, axis=0).astype(jnp.float32)
    whole = inputs.astype(jnp.float32)
    normed = lax.optimization_barrier(rms_forward(head_in, gain_one).astype(bf16))
    head_cos, head_sin = rotation(head_pos)
    projected = jnp.dot(normed, in_full, preferred_element_type=jnp.float32)
    turned = rope_apply(projected[:, : query_cols + key_cols], head_cos, head_sin, False)
    query_head = turned[:, :query_cols].astype(bf16)
    pair = jnp.concatenate(
        [turned[:, query_cols:], projected[:, query_cols + key_cols :]], axis=1
    ).astype(bf16)

    up_line = [(i, i + 2) for i in range(count - 2)]
    down_line = [(b, a) for a, b in up_line]
    reach = half // 2

    def sideways(step, reverse):
        to_odd = [(2 * i, 2 * i + 1) for i in range(half)]
        to_even = [(2 * i + 1, 2 * i) for i in range(half)]
        pairs = to_odd if step == 0 else to_even if step == reach else to_odd + to_even
        return [(b, a) for a, b in pairs] if reverse else pairs

    line = [pair]
    while len(line) <= reach:
        line.append(hop(line[-1], up_line))
    side = [hop(line[k], sideways(k, False)) for k in range(reach + 1)]
    out_chunk = after(out_chunk, head_groups[-1][0])
    out_groups = ring_gather(out_chunk, 2)
    out_full = assemble(out_groups)

    pieces = []
    places = []
    for k in range(reach + 1):
        pieces += [line[k], side[k]]
        places += [block_pos(fsdp_rank - 2 * k), block_pos((fsdp_rank ^ 1) - 2 * k)]
    pairs_all = jnp.concatenate(pieces, axis=0)
    key_pos = jnp.concatenate(places)
    low_start = jnp.min(head_start)
    ranks = []
    for k in range(reach + 1):
        ranks += [fsdp_rank - 2 * k, (fsdp_rank ^ 1) - 2 * k]
    ranks = jnp.stack(ranks)
    live = (ranks >= 0) & (ranks <= fsdp_rank) & ((ranks + 1) * head_rows > low_start)
    live = live.astype(jnp.int32)
    mixed_head, log_totals = attend(
        live, query_head, pairs_all, key_pos, head_pos, head_start, head_rows
    )
    attended_part = contract_cols(mixed_head, out_full)
    attended = seq_scatter(jnp.split(attended_part, seq_count, axis=0))
    middle = whole + rms_forward(attended, gain_two)
    ffn_in = rms_forward(middle, gain_three).astype(bf16)
    upstream = cotangent.astype(jnp.float32)

    def unit_rows(weight):
        weight = after(weight, rows_in[2])
        across = flip(weight, 2)
        beside = flip(weight, 1)
        both = flip(after(across, line[reach]), 1)
        return jnp.concatenate([weight, across, beside, both], axis=0)

    gate_units, up_units, down_units = (
        unit_rows(weight) for weight in (gate_weight, up_weight, down_weight)
    )

    def joined(groups):
        return [group[0] if len(group) == 1 else jnp.concatenate(group, axis=0) for group in groups]

    def part_of(parts):
        def part_at(step):
            if step == 0:
                return parts[0]
            if abs(step) == half:
                return parts[half]
            part = parts[abs(step)]
            return part[tokens:] if step > 0 else part[:tokens]

        return part_at

    row_groups = joined(ring_gather(ffn_in, 0))
    gates, ups, hiddens, mlp_parts = [], [], [], []
    for rows in row_groups:
        gate = contract_cols(rows, gate_units)
        up = contract_cols(rows, up_units)
        hidden = (gelu_value(gate) * up).astype(bf16)
        gates.append(gate)
        ups.append(up)
        hiddens.append(hidden)
        mlp_parts.append(jnp.dot(hidden, down_units, preferred_element_type=jnp.float32))
    mlp = ring_scatter(part_of(mlp_parts), 0)
    layer_out = middle + rms_forward(mlp, gain_four)
    mlp_grad, fourth_part = rms_backward(mlp, gain_four, upstream)
    mlp_round = mlp_grad.astype(bf16)
    grad_groups = joined(ring_gather(mlp_round, 0))
    gate_deltas, up_deltas, in_parts = [], [], []
    for grads, gate, up in zip(grad_groups, gates, ups):
        hidden_grad = contract_cols(grads, down_units)
        gate_delta = (hidden_grad * up * gelu_slope(gate)).astype(bf16)
        up_delta = (hidden_grad * gelu_value(gate)).astype(bf16)
        gate_deltas.append(gate_delta)
        up_deltas.append(up_delta)
        in_parts.append(
            jnp.dot(gate_delta, gate_units, preferred_element_type=jnp.float32)
            + jnp.dot(up_delta, up_units, preferred_element_type=jnp.float32)
        )
    ffn_in_grad = ring_scatter(part_of(in_parts), 0)

    middle_part, third_part = rms_backward(middle, gain_three, ffn_in_grad)
    middle_grad = upstream + middle_part
    attended_grad, second_part = rms_backward(attended, gain_two, middle_grad)
    attended_round = attended_grad.astype(bf16)
    attended_blocks = seq_gather(attended_round)
    attended_rows = jnp.concatenate(attended_blocks, axis=0)

    all_rows = jnp.concatenate(row_groups, axis=0)
    all_grads = jnp.concatenate(grad_groups, axis=0)

    def unit_grad(left, right):
        full = contract_rows(jnp.concatenate(left, axis=0), right).astype(bf16)
        cut = full.shape[0] // 2
        near = full[:cut].astype(jnp.float32) + flip(full[cut:], 1).astype(jnp.float32)
        across = flip(near[cut // 2 :].astype(bf16), 2)
        return near[: cut // 2] + across.astype(jnp.float32)

    down_grad = unit_grad(hiddens, all_grads)
    gate_grad = unit_grad(gate_deltas, all_rows)
    up_grad = unit_grad(up_deltas, all_rows)

    mixed_grad_head = jnp.dot(
        attended_rows, out_full, preferred_element_type=jnp.float32
    ).astype(bf16)

    def weight_grad(left, right):
        full = contract_rows(left, right).reshape(seq_count, count, own_rows, -1)
        chunk = ring_scatter(
            lambda step: lax.dynamic_slice_in_dim(full, rank_at(step), 1, 1)[:, 0], 2
        )
        chunk = chunk.astype(bf16)
        return [
            flip(lax.dynamic_slice_in_dim(chunk, seq_rank ^ j, 1, 0)[0], j)
            if j
            else lax.dynamic_slice_in_dim(chunk, seq_rank, 1, 0)[0]
            for j in range(seq_count)
        ]

    def spread(pieces):
        cols = pieces[0].shape[1]
        out = jnp.zeros((own_rows, cols * seq_count), jnp.float32)
        for j, piece in enumerate(pieces):
            out = lax.dynamic_update_slice(
                out, piece.astype(jnp.float32), (0, (seq_rank ^ j) * cols)
            )
        return out

    delta = jnp.sum(
        (mixed_grad_head.astype(jnp.float32) * mixed_head.astype(jnp.float32)).reshape(
            head_rows, -1, HEAD_DIM
        ),
        axis=-1,
    ).T
    queries_grad = jnp.zeros(query_head.shape, jnp.float32)
    total = None
    for k in range(reach, -1, -1):
        queries_grad, pair_part = attend_back(
            live,
            query_head,
            mixed_grad_head,
            pairs_all,
            key_pos,
            head_pos,
            head_start,
            log_totals,
            delta,
            queries_grad,
            head_rows,
            2 * k,
            2,
        )
        here = pair_part[:head_rows].astype(jnp.float32) + hop(
            pair_part[head_rows:], sideways(k, True)
        ).astype(jnp.float32)
        if total is not None:
            here = here + hop(total.astype(bf16), down_line).astype(jnp.float32)
        total = here
    query_back = rope_apply(queries_grad, head_cos, head_sin, True).astype(bf16)
    key_back = rope_apply(total[:, :key_cols], head_cos, head_sin, True).astype(bf16)
    value_back = total[:, key_cols:].astype(bf16)
    output_grad = spread(weight_grad(attended_rows, mixed_head))
    query_grad = spread(weight_grad(normed, query_back))
    pair_back = jnp.concatenate([key_back, value_back], axis=1)
    pair_pieces = weight_grad(normed, pair_back)
    key_grad = spread([piece[:, :key_cols] for piece in pair_pieces])
    value_grad = spread([piece[:, key_cols:] for piece in pair_pieces])
    normed_part = contract_cols(jnp.concatenate([query_back, pair_back], axis=1), in_full)
    normed_grad = seq_scatter(jnp.split(normed_part, seq_count, axis=0))
    head_scaling = lax.rsqrt(jnp.mean(head_in * head_in, axis=-1, keepdims=True) + epsilon)
    first_part = jnp.sum(normed_part * head_in * head_scaling, axis=0)
    input_part, _ = rms_backward(whole, gain_one, normed_grad)
    input_grad = middle_grad + input_part

    gain_parts = jnp.stack([first_part, second_part, third_part, fourth_part])
    gain_parts = gain_parts.reshape(4, seq_count, count, own_rows)
    gain_sums = None
    for step in range(count):
        piece = lax.dynamic_slice_in_dim(gain_parts, lax.rem(fsdp_rank + step, count), 1, 2)
        piece = turn(piece, step) if step else piece
        gain_sums = piece if gain_sums is None else gain_sums + piece
    gain_sums = gain_sums[:, :, 0]
    gain_grads = None
    for j in range(seq_count):
        piece = lax.dynamic_slice_in_dim(gain_sums, seq_rank ^ j, 1, 1)[:, 0]
        piece = flip(piece, j) if j else piece
        gain_grads = piece if gain_grads is None else gain_grads + piece
    return (
        layer_out,
        input_grad,
        gain_grads[0],
        gain_grads[1],
        gain_grads[2],
        gain_grads[3],
        query_grad,
        key_grad,
        value_grad,
        output_grad,
        gate_grad,
        up_grad,
        down_grad,
    )


def solution(mesh):
    placed = (
        P(("fsdp", "seq"), None),
        P(("fsdp", "seq"), None),
        P(),
        P(("seq", "fsdp")),
        P(("seq", "fsdp")),
        P(("seq", "fsdp")),
        P(("seq", "fsdp")),
        P(("seq", "fsdp"), None),
        P(("seq", "fsdp"), None),
        P(("seq", "fsdp"), None),
        P(("seq", "fsdp"), None),
        P(("seq", "fsdp"), None),
        P(("seq", "fsdp"), None),
        P(("seq", "fsdp"), None),
    )
    return jax.shard_map(
        layer,
        mesh=mesh,
        in_specs=placed,
        out_specs=(
            P(("fsdp", "seq"), None),
            P(("fsdp", "seq"), None),
            P(("seq", "fsdp")),
            P(("seq", "fsdp")),
            P(("seq", "fsdp")),
            P(("seq", "fsdp")),
            P(("seq", "fsdp"), None),
            P(("seq", "fsdp"), None),
            P(("seq", "fsdp"), None),
            P(("seq", "fsdp"), None),
            P(("seq", "fsdp"), None),
            P(("seq", "fsdp"), None),
            P(("seq", "fsdp"), None),
        ),
        check_vma=False,
    )
```

profile of v0, /device:TPU:0, one launch (start us, length us, event | category | flops | bytes accessed | tf_op | source)
XLA Modules:
  0.0 723.2 jit_solution(7825253198207127814)
XLA Ops:
  45.6 11.0 %collective-permute-done.4 = bf16[128,2304]{1,0:T(8,128)(2,1)S(1)} collective-permute-done((bf16[128,2304]{1,0:T(8,128)(2,1)S(1)}, bf16[128,2304]{1,0:T(8,128)(2,1)S(1)}, u32[]{:S(2)}, u32[]{:S(2)}) %collective-permute-start.4) | collective-permute-done | bytes 589856 | tf_op jit(solution)/shard_map/ppermute | solution.py:279
  63.1 10.7 %collective-permute-done.18 = bf16[4,72,1024]{2,1,0:T(8,128)(2,1)S(1)} collective-permute-done((bf16[4,72,1024]{2,1,0:T(8,128)(2,1)S(1)}, bf16[4,72,1024]{2,1,0:T(8,128)(2,1)S(1)}, u32[]{:S(2)}, u32[]{:S(2)}) %collective-permute-start.18) | collective-permute-done | bytes 589856 | tf_op jit(solution)/shard_map/ppermute | solution.py:282
  80.8 8.3 %collective-permute-done.20 = bf16[4,72,1024]{2,1,0:T(8,128)(2,1)S(1)} collective-permute-done((bf16[4,72,1024]{2,1,0:T(8,128)(2,1)S(1)}, bf16[4,72,1024]{2,1,0:T(8,128)(2,1)S(1)}, u32[]{:S(2)}, u32[]{:S(2)}) %collective-permute-start.20) | collective-permute-done | bytes 589856 | tf_op jit(solution)/shard_map/ppermute | solution.py:282
  95.3 21.8 %collective-permute-done.46 = bf16[288,2304]{1,0:T(8,128)(2,1)S(1)} collective-permute-done((bf16[288,2304]{1,0:T(8,128)(2,1)S(1)}, bf16[288,2304]{1,0:T(8,128)(2,1)S(1)}, u32[]{:S(2)}, u32[]{:S(2)}) %collective-permute-start.46) | collective-permute-done | bytes 1327136 | tf_op jit(solution)/shard_map/ppermute | solution.py:279
  156.7 10.7 %collective-permute-done.36 = bf16[4,72,512]{2,1,0:T(8,128)(2,1)S(1)} collective-permute-done((bf16[4,72,512]{2,1,0:T(8,128)(2,1)S(1)}, bf16[4,72,512]{2,1,0:T(8,128)(2,1)S(1)}, u32[]{:S(2)}, u32[]{:S(2)}) %collective-permute-start.36) | collective-permute-done | bytes 294944 | tf_op jit(solution)/shard_map/ppermute | solution.py:282
  182.2 7.1 attend.1
  200.3 12.1 %collective-permute-done.42 = bf16[128,2304]{1,0:T(8,128)(2,1)S(1)} collective-permute-done((bf16[128,2304]{1,0:T(8,128)(2,1)S(1)}, bf16[128,2304]{1,0:T(8,128)(2,1)S(1)}, u32[]{:S(2)}, u32[]{:S(2)}) %collective-permute-start.42) | collective-permute-done | bytes 589856 | tf_op jit(solution)/shard_map/ppermute | solution.py:279
  222.5 7.6 %collective-permute-done.52 = bf16[128,2304]{1,0:T(8,128)(2,1)S(1)} collective-permute-done((bf16[128,2304]{1,0:T(8,128)(2,1)S(1)}, bf16[128,2304]{1,0:T(8,128)(2,1)S(1)}, u32[]{:S(2)}, u32[]{:S(2)}) %collective-permute-start.52) | collective-permute-done | bytes 589856 | tf_op jit(solution)/shard_map/ppermute | solution.py:282
  239.1 8.8 %collective-permute-done.54 = bf16[128,2304]{1,0:T(8,128)(2,1)S(1)} collective-permute-done((bf16[128,2304]{1,0:T(8,128)(2,1)S(1)}, bf16[128,2304]{1,0:T(8,128)(2,1)S(1)}, u32[]{:S(2)}, u32[]{:S(2)}) %collective-permute-start.54) | collective-permute-done | bytes 589856 | tf_op jit(solution)/shard_map/ppermute | solution.py:282
  255.0 8.6 %collective-permute-done.56 = bf16[128,2304]{1,0:T(8,128)(2,1)S(1)} collective-permute-done((bf16[128,2304]{1,0:T(8,128)(2,1)S(1)}, bf16[128,2304]{1,0:T(8,128)(2,1)S(1)}, u32[]{:S(2)}, u32[]{:S(2)}) %collective-permute-start.56) | collective-permute-done | bytes 589856 | tf_op jit(solution)/shard_map/ppermute | solution.py:282
  281.2 5.5 collective-permute-done.60
  291.0 9.3 %collective-permute-done.62 = bf16[128,2304]{1,0:T(8,128)(2,1)S(1)} collective-permute-done((bf16[128,2304]{1,0:T(8,128)(2,1)S(1)}, bf16[128,2304]{1,0:T(8,128)(2,1)S(1)}, u32[]{:S(2)}, u32[]{:S(2)}) %collective-permute-start.62) | collective-permute-done | bytes 589856 | tf_op jit(solution)/shard_map/ppermute | solution.py:282
  306.2 10.1 %collective-permute-done.64 = bf16[128,2304]{1,0:T(8,128)(2,1)S(1)} collective-permute-done((bf16[128,2304]{1,0:T(8,128)(2,1)S(1)}, bf16[128,2304]{1,0:T(8,128)(2,1)S(1)}, u32[]{:S(2)}, u32[]{:S(2)}) %collective-permute-start.64) | collective-permute-done | bytes 589856 | tf_op jit(solution)/shard_map/ppermute | solution.py:282
  351.7 6.6 constant_dynamic-update-slice_fusion.32
  366.5 7.8 %collective-permute-done.70 = bf16[128,2304]{1,0:T(8,128)(2,1)S(1)} collective-permute-done((bf16[128,2304]{1,0:T(8,128)(2,1)}, bf16[128,2304]{1,0:T(8,128)(2,1)S(1)}, u32[]{:S(2)}, u32[]{:S(2)}) %collective-permute-start.70) | collective-permute-done | bytes 589856 | tf_op jit(solution)/shard_map/ppermute | solution.py:282
  386.9 6.1 collective-permute-done.72
  411.7 5.8 collective-permute-done.76
  420.1 8.9 %collective-permute-done.78 = bf16[128,2304]{1,0:T(8,128)(2,1)S(1)} collective-permute-done((bf16[128,2304]{1,0:T(8,128)(2,1)S(1)}, bf16[128,2304]{1,0:T(8,128)(2,1)S(1)}, u32[]{:S(2)}, u32[]{:S(2)}) %collective-permute-start.78) | collective-permute-done | bytes 589856 | tf_op jit(solution)/shard_map/ppermute | solution.py:282
  431.3 6.3 convolution_convert_fusion
  443.3 6.3 convolution_convert_fusion.1
  461.7 6.2 convolution_convert_fusion.2
  499.2 6.3 attend_back.5
  522.4 5.7 collective-permute-start.89
  536.8 9.9 %collective-permute-done.130 = bf16[4,72,512]{2,1,0:T(8,128)(2,1)S(1)} collective-permute-done((bf16[4,72,512]{2,1,0:T(8,128)(2,1)S(1)}, bf16[4,72,512]{2,1,0:T(8,128)(2,1)S(1)}, u32[]{:S(2)}, u32[]{:S(2)}) %collective-permute-start.130) | collective-permute-done | bytes 294944 | tf_op jit(solution)/shard_map/ppermute | solution.py:282
  559.2 12.9 %collective-permute-done.131 = bf16[4,72,512]{2,1,0:T(8,128)(2,1)S(1)} collective-permute-done((bf16[4,72,512]{2,1,0:T(8,128)(2,1)S(1)}, bf16[4,72,512]{2,1,0:T(8,128)(2,1)S(1)}, u32[]{:S(2)}, u32[]{:S(2)}) %collective-permute-start.131) | collective-permute-done | bytes 294944 | tf_op jit(solution)/shard_map/ppermute | solution.py:282
  580.4 22.7 %collective-permute-done.139 = bf16[288,2304]{1,0:T(8,128)(2,1)S(1)} collective-permute-done((bf16[288,2304]{1,0:T(8,128)(2,1)S(1)}, bf16[288,2304]{1,0:T(8,128)(2,1)S(1)}, u32[]{:S(2)}, u32[]{:S(2)}) %collective-permute-start.139) | collective-permute-done | bytes 1327136 | tf_op jit(solution)/shard_map/ppermute | solution.py:279
  615.7 7.6 %collective-permute-done.111 = bf16[4,72,512]{2,1,0:T(8,128)(2,1)S(1)} collective-permute-done((bf16[4,72,512]{2,1,0:T(8,128)(2,1)S(1)}, bf16[4,72,512]{2,1,0:T(8,128)(2,1)S(1)}, u32[]{:S(2)}, u32[]{:S(2)}) %collective-permute-start.111) | collective-permute-done | bytes 294944 | tf_op jit(solution)/shard_map/ppermute | solution.py:282
  636.5 12.5 %collective-permute-done.91 = bf16[512,512]{1,0:T(8,128)(2,1)S(1)} collective-permute-done((bf16[512,512]{1,0:T(8,128)(2,1)S(1)}, bf16[512,512]{1,0:T(8,128)(2,1)S(1)}, u32[]{:S(2)}, u32[]{:S(2)}) %collective-permute-start.91) | collective-permute-done | bytes 524320 | tf_op jit(solution)/shard_map/ppermute | solution.py:282
  657.5 6.7 fusion.4
  679.5 6.9 collective-permute-done.118
  692.2 7.1 collective-permute-done.120
  714.5 6.4 collective-permute-done.125
  (783 shorter events, 429.0 us)
Async XLA Ops:
  56.6 35.0 %collective-permute-start.43 = (bf16[288,2304]{1,0:T(8,128)(2,1)S(1)}, bf16[288,2304]{1,0:T(8,128)(2,1)}, u32[]{:S(2)}, u32[]{:S(2)}) collective-permute-start(bf16[288,2304]{1,0:T(8,128)(2,1)S(1)} %copy-done.36), channel_id=1, source_target_pairs={{0,16},{8,24},{16,0},{24,8},{1,17},{9,25},{17,1},{25,9},{2,18},{10... | collective-permute-start | bytes 3981320 | tf_op jit(solution)/shard_map/ppermute | solution.py:279
  63.1 30.4 %collective-permute-start.44 = (bf16[288,2304]{1,0:T(8,128)(2,1)S(1)}, bf16[288,2304]{1,0:T(8,128)(2,1)S(1)}, u32[]{:S(2)}, u32[]{:S(2)}) collective-permute-start(bf16[288,2304]{1,0:T(8,128)(2,1)S(1)} %copy-done.36), channel_id=1, source_target_pairs={{0,8},{8,0},{16,24},{24,16},{1,9},{9,1},{17,25},{25,17},{2,10},{10... | collective-permute-start | bytes 3981320 | tf_op jit(solution)/shard_map/ppermute | solution.py:279
  73.8 43.2 %collective-permute-start.46 = (bf16[288,2304]{1,0:T(8,128)(2,1)S(1)}, bf16[288,2304]{1,0:T(8,128)(2,1)S(1)}, u32[]{:S(2)}, u32[]{:S(2)}) collective-permute-start(bf16[288,2304]{1,0:T(8,128)(2,1)S(1)} %copy-done.37), channel_id=1, source_target_pairs={{0,16},{8,24},{16,0},{24,8},{1,17},{9,25},{17,1},{25,9},{2,18},{10... | collective-permute-start | bytes 3981320 | tf_op jit(solution)/shard_map/ppermute | solution.py:279
  89.1 28.0 %collective-permute-start.47 = (bf16[288,2304]{1,0:T(8,128)(2,1)S(1)}, bf16[288,2304]{1,0:T(8,128)(2,1)S(1)}, u32[]{:S(2)}, u32[]{:S(2)}) collective-permute-start(bf16[288,2304]{1,0:T(8,128)(2,1)S(1)} %copy-done.37), channel_id=1, source_target_pairs={{0,8},{8,0},{16,24},{24,16},{1,9},{9,1},{17,25},{25,17},{2,10},{10... | collective-permute-start | bytes 3981320 | tf_op jit(solution)/shard_map/ppermute | solution.py:279
  90.0 102.1 %collective-permute-start.49 = (bf16[288,2304]{1,0:T(8,128)(2,1)}, bf16[288,2304]{1,0:T(8,128)(2,1)}, u32[]{:S(2)}, u32[]{:S(2)}) collective-permute-start(bf16[288,2304]{1,0:T(8,128)(2,1)} %param.27), channel_id=1, source_target_pairs={{0,16},{8,24},{16,0},{24,8},{1,17},{9,25},{17,1},{25,9},{2,18},{10... | collective-permute-start | bytes 3981320 | tf_op jit(solution)/shard_map/ppermute | solution.py:279
  91.6 25.6 %collective-permute-start.22 = (bf16[4,72,512]{2,1,0:T(8,128)(2,1)S(1)}, bf16[4,72,512]{2,1,0:T(8,128)(2,1)S(1)}, u32[]{:S(2)}, u32[]{:S(2)}) collective-permute-start(bf16[4,72,512]{2,1,0:T(8,128)(2,1)S(1)} %slice.326), channel_id=1, source_target_pairs={{0,2},{2,4},{4,6},{6,7},{7,5},{5,3},{3,1},{1,0},{8,10},{10,12},{12... | collective-permute-start | bytes 884744 | tf_op jit(solution)/shard_map/ppermute | solution.py:282
  93.5 23.8 %collective-permute-start.23 = (bf16[4,72,512]{2,1,0:T(8,128)(2,1)S(1)}, bf16[4,72,512]{2,1,0:T(8,128)(2,1)S(1)}, u32[]{:S(2)}, u32[]{:S(2)}) collective-permute-start(bf16[4,72,512]{2,1,0:T(8,128)(2,1)S(1)} %slice.327), channel_id=1, source_target_pairs={{2,0},{4,2},{6,4},{7,6},{5,7},{3,5},{1,3},{0,1},{10,8},{12,10},{14... | collective-permute-start | bytes 884744 | tf_op jit(solution)/shard_map/ppermute | solution.py:282
  117.3 21.4 %collective-permute-start.32 = (bf16[4,72,512]{2,1,0:T(8,128)(2,1)}, bf16[4,72,512]{2,1,0:T(8,128)(2,1)}, u32[]{:S(2)}, u32[]{:S(2)}) collective-permute-start(bf16[4,72,512]{2,1,0:T(8,128)(2,1)} %bitcast_dynamic-update-slice_fusion.18), channel_id=1, source_target_pairs={{0,2},{2,4},{4,6},{6,7},{7,5},{5,3},{3,1},{1,0},{8,10},{10,12},{12... | collective-permute-start | bytes 884744 | tf_op jit(solution)/shard_map/ppermute | solution.py:282
  117.9 20.9 %collective-permute-start.33 = (bf16[4,72,512]{2,1,0:T(8,128)(2,1)}, bf16[4,72,512]{2,1,0:T(8,128)(2,1)}, u32[]{:S(2)}, u32[]{:S(2)}) collective-permute-start(bf16[4,72,512]{2,1,0:T(8,128)(2,1)} %bitcast_dynamic-update-slice_fusion.18), channel_id=1, source_target_pairs={{2,0},{4,2},{6,4},{7,6},{5,7},{3,5},{1,3},{0,1},{10,8},{12,10},{14... | collective-permute-start | bytes 884744 | tf_op jit(solution)/shard_map/ppermute | solution.py:282
  127.2 19.2 %collective-permute-start.24 = (bf16[512,512]{1,0:T(8,128)(2,1)}, bf16[512,512]{1,0:T(8,128)(2,1)}, u32[]{:S(2)}, u32[]{:S(2)}) collective-permute-start(bf16[512,512]{1,0:T(8,128)(2,1)} %get-tuple-element.243), channel_id=1, source_target_pairs={{0,1},{2,3},{4,5},{6,7},{8,9},{10,11},{12,13},{14,15},{16,17},{18,... | collective-permute-start | bytes 1572872 | tf_op jit(solution)/shard_map/ppermute | solution.py:282
  146.4 28.9 %collective-permute-start.26 = (bf16[512,512]{1,0:T(8,128)(2,1)}, bf16[512,512]{1,0:T(8,128)(2,1)S(1)}, u32[]{:S(2)}, u32[]{:S(2)}) collective-permute-start(bf16[512,512]{1,0:T(8,128)(2,1)} %collective-permute-done.25), channel_id=1, source_target_pairs={{0,1},{2,3},{4,5},{6,7},{1,0},{3,2},{5,4},{7,6},{8,9},{10,11},{12,... | collective-permute-start | bytes 1572872 | tf_op jit(solution)/shard_map/ppermute | solution.py:282
  146.4 23.7 %collective-permute-start.27 = (bf16[512,512]{1,0:T(8,128)(2,1)}, bf16[512,512]{1,0:T(8,128)(2,1)S(1)}, u32[]{:S(2)}, u32[]{:S(2)}) collective-permute-start(bf16[512,512]{1,0:T(8,128)(2,1)} %collective-permute-done.25), channel_id=1, source_target_pairs={{0,2},{1,3},{2,4},{3,5},{4,6},{5,7},{8,10},{9,11},{10,12},{11,13},... | collective-permute-start | bytes 1572872 | tf_op jit(solution)/shard_map/ppermute | solution.py:282
  174.2 20.4 %collective-permute-start.50 = (bf16[288,2304]{1,0:T(8,128)(2,1)}, bf16[288,2304]{1,0:T(8,128)(2,1)}, u32[]{:S(2)}, u32[]{:S(2)}) collective-permute-start(bf16[288,2304]{1,0:T(8,128)(2,1)} %param.27), channel_id=1, source_target_pairs={{0,8},{8,0},{16,24},{24,16},{1,9},{9,1},{17,25},{25,17},{2,10},{10... | collective-permute-start | bytes 3981320 | tf_op jit(solution)/shard_map/ppermute | solution.py:279
  175.2 23.2 %collective-permute-start.45 = (bf16[288,2304]{1,0:T(8,128)(2,1)}, bf16[288,2304]{1,0:T(8,128)(2,1)}, u32[]{:S(2)}, u32[]{:S(2)}) collective-permute-start(bf16[288,2304]{1,0:T(8,128)(2,1)} %collective-permute-done.43), channel_id=1, source_target_pairs={{0,8},{8,0},{16,24},{24,16},{1,9},{9,1},{17,25},{25,17},{2,10},{10... | collective-permute-start | bytes 3981320 | tf_op jit(solution)/shard_map/ppermute | solution.py:279
  440.8 34.5 %collective-permute-start.142 = (bf16[576,2304]{1,0:T(8,128)(2,1)}, bf16[576,2304]{1,0:T(8,128)(2,1)}, u32[]{:S(2)}, u32[]{:S(2)}) collective-permute-start(bf16[576,2304]{1,0:T(8,128)(2,1)} %slice.388), channel_id=1, source_target_pairs={{0,8},{8,0},{16,24},{24,16},{1,9},{9,1},{17,25},{25,17},{2,10},{10... | collective-permute-start | bytes 7962632 | tf_op jit(solution)/shard_map/ppermute | solution.py:279
  452.9 64.9 %collective-permute-start.140 = (bf16[576,2304]{1,0:T(8,128)(2,1)}, bf16[576,2304]{1,0:T(8,128)(2,1)}, u32[]{:S(2)}, u32[]{:S(2)}) collective-permute-start(bf16[576,2304]{1,0:T(8,128)(2,1)} %slice.384), channel_id=1, source_target_pairs={{0,8},{8,0},{16,24},{24,16},{1,9},{9,1},{17,25},{25,17},{2,10},{10... | collective-permute-start | bytes 7962632 | tf_op jit(solution)/shard_map/ppermute | solution.py:279
  471.1 57.2 %collective-permute-start.138 = (bf16[576,2304]{1,0:T(8,128)(2,1)}, bf16[576,2304]{1,0:T(8,128)(2,1)}, u32[]{:S(2)}, u32[]{:S(2)}) collective-permute-start(bf16[576,2304]{1,0:T(8,128)(2,1)} %slice.380), channel_id=1, source_target_pairs={{0,8},{8,0},{16,24},{24,16},{1,9},{9,1},{17,25},{25,17},{2,10},{10... | collective-permute-start | bytes 7962632 | tf_op jit(solution)/shard_map/ppermute | solution.py:279
  479.6 73.7 %collective-permute-start.143 = (bf16[288,2304]{1,0:T(8,128)(2,1)}, bf16[288,2304]{1,0:T(8,128)(2,1)}, u32[]{:S(2)}, u32[]{:S(2)}) collective-permute-start(bf16[288,2304]{1,0:T(8,128)(2,1)} %slice.470), channel_id=1, source_target_pairs={{0,16},{8,24},{16,0},{24,8},{1,17},{9,25},{17,1},{25,9},{2,18},{10... | collective-permute-start | bytes 3981320 | tf_op jit(solution)/shard_map/ppermute | solution.py:279
  483.5 28.0 %collective-permute-start.127 = (bf16[4,72,256]{2,1,0:T(8,128)(2,1)}, bf16[4,72,256]{2,1,0:T(8,128)(2,1)S(1)}, u32[]{:S(2)}, u32[]{:S(2)}) collective-permute-start(bf16[4,72,256]{2,1,0:T(8,128)(2,1)} %get-tuple-element.253), channel_id=1, source_target_pairs={{0,2},{2,4},{4,6},{6,7},{7,5},{5,3},{3,1},{1,0},{8,10},{10,12},{12... | collective-permute-start | bytes 442376 | tf_op jit(solution)/shard_map/ppermute | solution.py:282
  483.6 32.8 %collective-permute-start.128 = (bf16[4,72,256]{2,1,0:T(8,128)(2,1)}, bf16[4,72,256]{2,1,0:T(8,128)(2,1)}, u32[]{:S(2)}, u32[]{:S(2)}) collective-permute-start(bf16[4,72,256]{2,1,0:T(8,128)(2,1)} %get-tuple-element.252), channel_id=1, source_target_pairs={{2,0},{4,2},{6,4},{7,6},{5,7},{3,5},{1,3},{0,1},{10,8},{12,10},{14... | collective-permute-start | bytes 442376 | tf_op jit(solution)/shard_map/ppermute | solution.py:282
  522.4 30.7 %collective-permute-start.89 = (bf16[512,512]{1,0:T(8,128)(2,1)S(1)}, bf16[512,512]{1,0:T(8,128)(2,1)S(1)}, u32[]{:S(2)}, u32[]{:S(2)}) collective-permute-start(bf16[512,512]{1,0:T(8,128)(2,1)S(1)} %slice.290), channel_id=1, source_target_pairs={{0,1},{2,3},{4,5},{6,7},{8,9},{10,11},{12,13},{14,15},{16,17},{18,... | collective-permute-start | bytes 1572872 | tf_op jit(solution)/shard_map/ppermute | solution.py:282
  530.4 21.0 %collective-permute-start.108 = (bf16[4,72,512]{2,1,0:T(8,128)(2,1)S(1)}, bf16[4,72,512]{2,1,0:T(8,128)(2,1)S(1)}, u32[]{:S(2)}, u32[]{:S(2)}) collective-permute-start(bf16[4,72,512]{2,1,0:T(8,128)(2,1)S(1)} %get-tuple-element.190), channel_id=1, source_target_pairs={{2,0},{4,2},{6,4},{7,6},{5,7},{3,5},{1,3},{0,1},{10,8},{12,10},{14... | collective-permute-start | bytes 884744 | tf_op jit(solution)/shard_map/ppermute | solution.py:282
  546.7 32.0 %collective-permute-start.141 = (bf16[288,2304]{1,0:T(8,128)(2,1)S(1)}, bf16[288,2304]{1,0:T(8,128)(2,1)S(1)}, u32[]{:S(2)}, u32[]{:S(2)}) collective-permute-start(bf16[288,2304]{1,0:T(8,128)(2,1)S(1)} %slice.471), channel_id=1, source_target_pairs={{0,16},{8,24},{16,0},{24,8},{1,17},{9,25},{17,1},{25,9},{2,18},{10... | collective-permute-start | bytes 3981320 | tf_op jit(solution)/shard_map/ppermute | solution.py:279
  547.2 55.9 %collective-permute-start.139 = (bf16[288,2304]{1,0:T(8,128)(2,1)S(1)}, bf16[288,2304]{1,0:T(8,128)(2,1)S(1)}, u32[]{:S(2)}, u32[]{:S(2)}) collective-permute-start(bf16[288,2304]{1,0:T(8,128)(2,1)S(1)} %slice.472), channel_id=1, source_target_pairs={{0,16},{8,24},{16,0},{24,8},{1,17},{9,25},{17,1},{25,9},{2,18},{10... | collective-permute-start | bytes 3981320 | tf_op jit(solution)/shard_map/ppermute | solution.py:279
  551.4 85.1 %collective-permute-start.87 = (bf16[512,512]{1,0:T(8,128)(2,1)S(1)}, bf16[512,512]{1,0:T(8,128)(2,1)S(1)}, u32[]{:S(2)}, u32[]{:S(2)}) collective-permute-start(bf16[512,512]{1,0:T(8,128)(2,1)S(1)} %slice.286), channel_id=1, source_target_pairs={{1,0},{3,2},{5,4},{7,6},{9,8},{11,10},{13,12},{15,14},{17,16},{19,... | collective-permute-start | bytes 1572872 | tf_op jit(solution)/shard_map/ppermute | solution.py:282
  572.1 35.3 %collective-permute-start.109 = (bf16[4,72,512]{2,1,0:T(8,128)(2,1)S(1)}, bf16[4,72,512]{2,1,0:T(8,128)(2,1)S(1)}, u32[]{:S(2)}, u32[]{:S(2)}) collective-permute-start(bf16[4,72,512]{2,1,0:T(8,128)(2,1)S(1)} %get-tuple-element.189), channel_id=1, source_target_pairs={{0,2},{2,4},{4,6},{6,7},{7,5},{5,3},{3,1},{1,0},{8,10},{10,12},{12... | collective-permute-start | bytes 884744 | tf_op jit(solution)/shard_map/ppermute | solution.py:282
  572.1 35.3 %collective-permute-start.110 = (bf16[4,72,512]{2,1,0:T(8,128)(2,1)S(1)}, bf16[4,72,512]{2,1,0:T(8,128)(2,1)S(1)}, u32[]{:S(2)}, u32[]{:S(2)}) collective-permute-start(bf16[4,72,512]{2,1,0:T(8,128)(2,1)S(1)} %get-tuple-element.188), channel_id=1, source_target_pairs={{2,0},{4,2},{6,4},{7,6},{5,7},{3,5},{1,3},{0,1},{10,8},{12,10},{14... | collective-permute-start | bytes 884744 | tf_op jit(solution)/shard_map/ppermute | solution.py:282
  578.7 30.2 %collective-permute-start.133 = (bf16[4,72,512]{2,1,0:T(8,128)(2,1)S(1)}, bf16[4,72,512]{2,1,0:T(8,128)(2,1)S(1)}, u32[]{:S(2)}, u32[]{:S(2)}) collective-permute-start(bf16[4,72,512]{2,1,0:T(8,128)(2,1)S(1)} %get-tuple-element.175), channel_id=1, source_target_pairs={{0,2},{2,4},{4,6},{6,7},{7,5},{5,3},{3,1},{1,0},{8,10},{10,12},{12... | collective-permute-start | bytes 884744 | tf_op jit(solution)/shard_map/ppermute | solution.py:282
  607.3 20.5 %collective-permute-start.88 = (bf16[512,512]{1,0:T(8,128)(2,1)S(1)}, bf16[512,512]{1,0:T(8,128)(2,1)S(1)}, u32[]{:S(2)}, u32[]{:S(2)}) collective-permute-start(bf16[512,512]{1,0:T(8,128)(2,1)S(1)} %slice.288), channel_id=1, source_target_pairs={{1,0},{3,2},{5,4},{7,6},{0,1},{2,3},{4,5},{6,7},{9,8},{11,10},{13,... | collective-permute-start | bytes 1572872 | tf_op jit(solution)/shard_map/ppermute | solution.py:282
  607.4 20.6 %collective-permute-start.90 = (bf16[512,512]{1,0:T(8,128)(2,1)S(1)}, bf16[512,512]{1,0:T(8,128)(2,1)S(1)}, u32[]{:S(2)}, u32[]{:S(2)}) collective-permute-start(bf16[512,512]{1,0:T(8,128)(2,1)S(1)} %add_convert_fusion.1), channel_id=1, source_target_pairs={{2,0},{3,1},{4,2},{5,3},{6,4},{7,5},{10,8},{11,9},{12,10},{13,11},... | collective-permute-start | bytes 1572872 | tf_op jit(solution)/shard_map/ppermute | solution.py:282
  676.2 27.7 %collective-permute-start.93 = (bf16[128,2304]{1,0:T(8,128)(2,1)S(1)}, bf16[128,2304]{1,0:T(8,128)(2,1)S(1)}, u32[]{:S(2)}, u32[]{:S(2)}) collective-permute-start(bf16[128,2304]{1,0:T(8,128)(2,1)S(1)} %get-tuple-element.195), channel_id=1, source_target_pairs={{0,8},{8,0},{16,24},{24,16},{1,9},{9,1},{17,25},{25,17},{2,10},{10... | collective-permute-start | bytes 1769480 | tf_op jit(solution)/shard_map/ppermute | solution.py:279
  676.3 44.7 %collective-permute-start.92 = (bf16[128,2304]{1,0:T(8,128)(2,1)S(1)}, bf16[128,2304]{1,0:T(8,128)(2,1)S(1)}, u32[]{:S(2)}, u32[]{:S(2)}) collective-permute-start(bf16[128,2304]{1,0:T(8,128)(2,1)S(1)} %get-tuple-element.194), channel_id=1, source_target_pairs={{0,8},{8,0},{16,24},{24,16},{1,9},{9,1},{17,25},{25,17},{2,10},{10... | collective-permute-start | bytes 1769480 | tf_op jit(solution)/shard_map/ppermute | solution.py:279
  (214 other events, 2517.4 us)
where the time goes:
time: 733 us; the launch traced here: 723 us
  waiting for transfers between devices  303 us (41%)
  starting transfers between devices  160 us (22%)
  matrix products  113 us (15%)
  local copies, waits for them, and re-layouts  70.4 us (10%)
  other arithmetic  51.1 us (7%)
  Pallas kernels  21.7 us (3%)
    ppermute x96, waiting for transfers between devices, hop(): return lax.ppermute(value, 'fsdp', pairs)  214 us
    ppermute x96, starting transfers between devices, hop(): return lax.ppermute(value, 'fsdp', pairs)  132 us
    ppermute x48, waiting for transfers between devices, flip(): return lax.ppermute(value, 'seq', [(i, i ^ bits) for i in range(seq_count)])  89.4 us
    dot_general x17, matrix products, contract_cols(): lax.dot_general(left, right, (((1,), (1,)), ((), ())), preferred_element_...  54.3 us
    ppermute x48, starting transfers between devices, flip(): return lax.ppermute(value, 'seq', [(i, i ^ bits) for i in range(seq_count)])  27.9 us
    unnamed x235, local copies, waits for them, and re-layouts  27.1 us
    dot_general x6, matrix products, contract_rows(): lax.dot_general(left, right, (((0,), (0,)), ((), ())), preferred_element_...  25.4 us
  transfers between devices with their start and end apart: 144, of which 60 were waited for; matrix products, arithmetic and copies ran while one was open for 25% of the time, Pallas kernels for 3%

commit v1 on v0

--- a/solution.py
+++ b/solution.py
@@ -148,23 +148,30 @@
     )(live, query, pairs, key_at[:, None], query_pos[None, :], query_start[None, :])
 
 
-def attend_back_kernel(
-    heads, first, last, live_ref, query_ref, grad_ref, pair_ref, at_ref, pos_ref, start_ref, log_ref,
-    delta_ref, carry_ref, query_grad_ref, pair_grad_ref, sums,
-):
+def attend_back_kernel(heads, first, begins, ends, *refs):
+    live_ref, query_ref, grad_ref, mixed_ref, pair_ref, at_ref, pos_ref, start_ref, log_ref = refs[:9]
+    refs = refs[9:]
+    if not begins:
+        carry_ref, refs = refs[0], refs[1:]
+    if ends:
+        cos_ref, sin_ref, refs = refs[0], refs[1], refs[2:]
+    query_grad_ref, line_ref, side_ref, sums, delta = refs
     step = pl.program_id(0)
     scale = HEAD_DIM ** (-0.5)
 
     @pl.when(step == 0)
     def _():
-        sums[...] = carry_ref[...]
-
-    @pl.when(live_ref[step + first] == 0)
-    def _():
-        pair_grad_ref[...] = jnp.zeros_like(pair_grad_ref)
-
-    @pl.when(live_ref[step + first] > 0)
-    def _():
+        sums[...] = jnp.zeros_like(sums) if begins else carry_ref[...]
+        ones = jnp.ones((8, HEAD_DIM), jnp.bfloat16)
+        for head in range(heads):
+            cols = slice(head * HEAD_DIM, (head + 1) * HEAD_DIM)
+            grad = grad_ref[:, cols].astype(jnp.float32)
+            product = grad * mixed_ref[:, cols].astype(jnp.float32)
+            high = product.astype(jnp.bfloat16)
+            low = (product - high.astype(jnp.float32)).astype(jnp.bfloat16)
+            delta[head * 8 : head * 8 + 8, :] = contract_cols(ones, high) + contract_cols(ones, low)
+
+    def work(out_ref):
         keys = pair_ref[:, :HEAD_DIM]
         values = pair_ref[:, HEAD_DIM:]
         allowed = (at_ref[...] >= start_ref[...]) & (at_ref[...] <= pos_ref[...])
@@ -175,62 +182,175 @@
             query = query_ref[:, cols]
             grad = grad_ref[:, cols]
             bent = jnp.tanh(contract_cols(keys, query) * (scale / softcap))
-            probs = jnp.where(allowed, jnp.exp(softcap * bent - log_ref[head : head + 1, :]), 0.0)
-            value_part = jnp.dot(probs.astype(jnp.bfloat16), grad, preferred_element_type=jnp.float32)
-            slope = contract_cols(values, grad) - delta_ref[head : head + 1, :]
+            probs = jnp.where(
+                allowed, jnp.exp(softcap * bent - log_ref[head : head + 1, :]), 0.0
+            )
+            value_part = jnp.dot(
+                probs.astype(jnp.bfloat16), grad, preferred_element_type=jnp.float32
+            )
+            slope = contract_cols(values, grad) - delta[head * 8 : head * 8 + 1, :]
             score = (probs * slope * (1.0 - bent * bent)).astype(jnp.bfloat16)
             key_part = jnp.dot(score, query, preferred_element_type=jnp.float32)
             sums[:, cols] += contract_rows(score, keys)
             key_grad = key_part if key_grad is None else key_grad + key_part
             value_grad = value_part if value_grad is None else value_grad + value_part
-        pair_grad_ref[:, :HEAD_DIM] = (key_grad * scale).astype(jnp.bfloat16)
-        pair_grad_ref[:, HEAD_DIM:] = value_grad.astype(jnp.bfloat16)
-
-    @pl.when(step == pl.num_programs(0) - 1)
-    def _():
-        query_grad_ref[...] = sums[...] * scale if last else sums[...]
+        out_ref[:, :HEAD_DIM] = (key_grad * scale).astype(jnp.bfloat16)
+        out_ref[:, HEAD_DIM:] = value_grad.astype(jnp.bfloat16)
+
+    @pl.when(step == 0)
+    def _():
+        line_ref[...] = jnp.zeros_like(line_ref)
+        side_ref[...] = jnp.zeros_like(side_ref)
+
+    @pl.when((step == 0) & (live_ref[first] > 0))
+    def _():
+        work(line_ref)
+
+    @pl.when((step == 1) & (live_ref[first + 1] > 0))
+    def _():
+        work(side_ref)
+
+    @pl.when(step == 1)
+    def _():
+        if not ends:
+            query_grad_ref[...] = sums[...]
+            return
+        half = HEAD_DIM // 2
+        for head in range(heads):
+            near = slice(head * HEAD_DIM, head * HEAD_DIM + half)
+            far = slice(head * HEAD_DIM + half, (head + 1) * HEAD_DIM)
+            one = sums[:, near] * scale
+            two = sums[:, far] * scale
+            query_grad_ref[:, near] = (one * cos_ref[...] + two * sin_ref[...]).astype(jnp.bfloat16)
+            query_grad_ref[:, far] = (two * cos_ref[...] - one * sin_ref[...]).astype(jnp.bfloat16)
 
 
 def attend_back(
-    live, query, grad, pairs, key_at, query_pos, query_start, log_totals, delta, carry, block, first, steps
+    live, query, grad, mixed, pairs, key_at, query_pos, query_start, log_totals, carry, turns, first
 ):
     rows, width = query.shape
     heads = width // HEAD_DIM
+    block = rows
     row = pl.BlockSpec((1, rows), lambda i, live: (0, 0))
     head_row = pl.BlockSpec((heads, rows), lambda i, live: (0, 0))
     full = pl.BlockSpec((rows, width), lambda i, live: (0, 0))
-    pair_spec = pl.BlockSpec((block, pairs.shape[1]), lambda i, live: (i + first, 0))
-    out_spec = pl.BlockSpec((block, pairs.shape[1]), lambda i, live: (i, 0))
+    part = pl.BlockSpec((block, pairs.shape[1]), lambda i, live: (0, 0))
+    more_specs = []
+    more = []
+    if carry is not None:
+        more_specs.append(full)
+        more.append(carry)
+    if turns is not None:
+        turn_spec = pl.BlockSpec((rows, HEAD_DIM // 2), lambda i, live: (0, 0))
+        more_specs += [turn_spec, turn_spec]
+        more += list(turns)
+    part_shape = jax.ShapeDtypeStruct((block, pairs.shape[1]), jnp.bfloat16)
     return pl.pallas_call(
-        functools.partial(attend_back_kernel, heads, first, first == 0),
+        functools.partial(attend_back_kernel, heads, first, carry is None, turns is not None),
         grid_spec=pltpu.PrefetchScalarGridSpec(
             num_scalar_prefetch=1,
-            grid=(steps,),
+            grid=(2,),
             in_specs=[
                 full,
                 full,
-                pair_spec,
+                full,
+                pl.BlockSpec((block, pairs.shape[1]), lambda i, live: (i + first, 0)),
                 pl.BlockSpec((block, 1), lambda i, live: (i + first, 0)),
                 row,
                 row,
                 head_row,
-                head_row,
-                full,
+                *more_specs,
             ],
-            out_specs=[full, out_spec],
-            scratch_shapes=[pltpu.VMEM((rows, width), jnp.float32)],
+            out_specs=[full, part, part],
+            scratch_shapes=[
+                pltpu.VMEM((rows, width), jnp.float32),
+                pltpu.VMEM((heads * 8, rows), jnp.float32),
+            ],
         ),
         out_shape=[
-            jax.ShapeDtypeStruct((rows, width), jnp.float32),
-            jax.ShapeDtypeStruct((steps * block, pairs.shape[1]), jnp.bfloat16),
+            jax.ShapeDtypeStruct(
+                (rows, width), jnp.float32 if turns is None else jnp.bfloat16
+            ),
+            part_shape,
+            part_shape,
         ],
         cost_estimate=pl.CostEstimate(
-            flops=10 * rows * width * steps * block,
-            bytes_accessed=4 * steps * block * width + 8 * query.size,
-            transcendentals=2 * rows * heads * steps * block,
+            flops=20 * rows * width * block,
+            bytes_accessed=8 * block * width + 8 * query.size,
+            transcendentals=4 * rows * heads * block,
         ),
         name="attend_back",
-    )(live, query, grad, pairs, key_at[:, None], query_pos[None, :], query_start[None, :], log_totals, delta, carry)
+    )(
+        live,
+        query,
+        grad,
+        mixed,
+        pairs,
+        key_at[:, None],
+        query_pos[None, :],
+        query_start[None, :],
+        log_totals,
+        *more,
+    )
+
+
+def project_kernel(turned, split, rows_ref, weight_ref, cos_ref, sin_ref, query_ref, pair_ref):
+    step = pl.program_id(0)
+    half = HEAD_DIM // 2
+    product = jnp.dot(rows_ref[...], weight_ref[...], preferred_element_type=jnp.float32)
+
+    def store(out_ref, turn):
+        one = product[:, :half]
+        two = product[:, half:]
+        if turn:
+            cosine = cos_ref[...]
+            sine = sin_ref[...]
+            one, two = one * cosine - two * sine, two * cosine + one * sine
+        out_ref[:, :half] = one.astype(jnp.bfloat16)
+        out_ref[:, half:] = two.astype(jnp.bfloat16)
+
+    @pl.when(step < split)
+    def _():
+        store(query_ref, True)
+
+    @pl.when((step >= split) & (step < turned))
+    def _():
+        store(pair_ref, True)
+
+    @pl.when(step >= turned)
+    def _():
+        store(pair_ref, False)
+
+
+def project(rows, weight, cosine, sine, query_cols, key_cols):
+    count = rows.shape[0]
+    split = query_cols // HEAD_DIM
+    steps = weight.shape[1] // HEAD_DIM
+    turn_spec = pl.BlockSpec((count, HEAD_DIM // 2), lambda i: (0, 0))
+    return pl.pallas_call(
+        functools.partial(project_kernel, split + key_cols // HEAD_DIM, split),
+        grid=(steps,),
+        in_specs=[
+            pl.BlockSpec(rows.shape, lambda i: (0, 0)),
+            pl.BlockSpec((weight.shape[0], HEAD_DIM), lambda i: (0, i)),
+            turn_spec,
+            turn_spec,
+        ],
+        out_specs=[
+            pl.BlockSpec((count, HEAD_DIM), lambda i: (0, jnp.minimum(i, split - 1))),
+            pl.BlockSpec((count, HEAD_DIM), lambda i: (0, jnp.maximum(i - split, 0))),
+        ],
+        out_shape=[
+            jax.ShapeDtypeStruct((count, query_cols), jnp.bfloat16),
+            jax.ShapeDtypeStruct((count, 2 * key_cols), jnp.bfloat16),
+        ],
+        cost_estimate=pl.CostEstimate(
+            flops=2 * rows.size * weight.shape[1],
+            bytes_accessed=2 * (rows.size + weight.size + count * weight.shape[1]),
+            transcendentals=0,
+        ),
+        name="project",
+    )(rows, weight, cosine, sine)
 
 
 def after(value, *others):
@@ -327,21 +447,20 @@
         across = flip((parts[2] + far).astype(bf16), 2).astype(jnp.float32)
         return parts[0] + near + across
 
-    def turn(value, step):
-        return hop(value, [(i, (i + step) % count) for i in range(count)])
-
+    def sum_all(value):
+        bits = 1
+        while bits < seq_count:
+            value = value + flip(value, bits)
+            bits *= 2
+        bits = 1
+        while bits < count:
+            value = value + hop(value, [(i, i ^ bits) for i in range(count)])
+            bits *= 2
+        return value
+
+    own_start = (seq_rank * count + fsdp_rank) * own_rows
     packed = jnp.stack([first_gain, second_gain, third_gain, fourth_gain])
-    row = jnp.zeros((seq_count, 4, own_rows), bf16)
-    for j in range(seq_count):
-        piece = flip(packed, j) if j else packed
-        row = lax.dynamic_update_slice(row, piece[None], (seq_rank ^ j, 0, 0))
-    gains = jnp.zeros((count, seq_count, 4, own_rows), bf16)
-    for step in range(count):
-        piece = turn(row, step) if step else row
-        gains = lax.dynamic_update_slice(
-            gains, piece[None], (lax.rem(fsdp_rank - step + count, count), 0, 0, 0)
-        )
-    gains = jnp.transpose(gains, (2, 1, 0, 3)).reshape(4, width)
+    gains = sum_all(lax.dynamic_update_slice(jnp.zeros((4, width), bf16), packed, (0, own_start)))
     gain_one, gain_two, gain_three, gain_four = gains[0], gains[1], gains[2], gains[3]
 
     def columns(weight, rank, size):
@@ -405,12 +524,7 @@
     whole = inputs.astype(jnp.float32)
     normed = lax.optimization_barrier(rms_forward(head_in, gain_one).astype(bf16))
     head_cos, head_sin = rotation(head_pos)
-    projected = jnp.dot(normed, in_full, preferred_element_type=jnp.float32)
-    turned = rope_apply(projected[:, : query_cols + key_cols], head_cos, head_sin, False)
-    query_head = turned[:, :query_cols].astype(bf16)
-    pair = jnp.concatenate(
-        [turned[:, query_cols:], projected[:, query_cols + key_cols :]], axis=1
-    ).astype(bf16)
+    query_head, pair = project(normed, in_full, head_cos, head_sin, query_cols, key_cols)
 
     up_line = [(i, i + 2) for i in range(count - 2)]
     down_line = [(b, a) for a, b in up_line]
@@ -453,15 +567,18 @@
     ffn_in = rms_forward(middle, gain_three).astype(bf16)
     upstream = cotangent.astype(jnp.float32)
 
+    blank = jnp.zeros((-2 * gate_weight.shape[0] % 128, width), bf16)
+
     def unit_rows(weight):
         weight = after(weight, rows_in[2])
         across = flip(weight, 2)
         beside = flip(weight, 1)
         both = flip(after(across, line[reach]), 1)
-        return jnp.concatenate([weight, across, beside, both], axis=0)
+        return jnp.concatenate([weight, across, blank, beside, both, blank], axis=0)
 
     gate_units, up_units, down_units = (
-        unit_rows(weight) for weight in (gate_weight, up_weight, down_weight)
+        unit_rows(weight)
+        for weight in (gate_weight, up_weight, down_weight)
     )
 
     def joined(groups):
@@ -517,11 +634,20 @@
     all_grads = jnp.concatenate(grad_groups, axis=0)
 
     def unit_grad(left, right):
-        full = contract_rows(jnp.concatenate(left, axis=0), right).astype(bf16)
-        cut = full.shape[0] // 2
-        near = full[:cut].astype(jnp.float32) + flip(full[cut:], 1).astype(jnp.float32)
-        across = flip(near[cut // 2 :].astype(bf16), 2)
-        return near[: cut // 2] + across.astype(jnp.float32)
+        units = gate_weight.shape[0]
+        left = jnp.concatenate(left, axis=0)
+        cut = left.shape[1] // 2
+        far = contract_rows(left[:, cut:], right).astype(bf16)
+        near = contract_rows(left[:, :cut], right).astype(bf16)
+        beside = flip(far, 1)
+
+        def both(begin):
+            return near[begin : begin + units].astype(jnp.float32) + beside[
+                begin : begin + units
+            ].astype(jnp.float32)
+
+        across = flip(both(units).astype(bf16), 2)
+        return both(0) + across.astype(jnp.float32)
 
     down_grad = unit_grad(hiddens, all_grads)
     gate_grad = unit_grad(gate_deltas, all_rows)
@@ -533,10 +659,11 @@
 
     def weight_grad(left, right):
         full = contract_rows(left, right).reshape(seq_count, count, own_rows, -1)
-        chunk = ring_scatter(
+        return ring_scatter(
             lambda step: lax.dynamic_slice_in_dim(full, rank_at(step), 1, 1)[:, 0], 2
-        )
-        chunk = chunk.astype(bf16)
+        ).astype(bf16)
+
+    def to_owners(chunk):
         return [
             flip(lax.dynamic_slice_in_dim(chunk, seq_rank ^ j, 1, 0)[0], j)
             if j
@@ -553,43 +680,37 @@
             )
         return out
 
-    delta = jnp.sum(
-        (mixed_grad_head.astype(jnp.float32) * mixed_head.astype(jnp.float32)).reshape(
-            head_rows, -1, HEAD_DIM
-        ),
-        axis=-1,
-    ).T
-    queries_grad = jnp.zeros(query_head.shape, jnp.float32)
+    carry = None
     total = None
     for k in range(reach, -1, -1):
-        queries_grad, pair_part = attend_back(
+        carry, line_part, side_part = attend_back(
             live,
             query_head,
             mixed_grad_head,
+            mixed_head,
             pairs_all,
             key_pos,
             head_pos,
             head_start,
             log_totals,
-            delta,
-            queries_grad,
-            head_rows,
+            carry,
+            None if k else (head_cos, head_sin),
             2 * k,
-            2,
         )
-        here = pair_part[:head_rows].astype(jnp.float32) + hop(
-            pair_part[head_rows:], sideways(k, True)
-        ).astype(jnp.float32)
+        here = line_part.astype(jnp.float32) + hop(side_part, sideways(k, True)).astype(jnp.float32)
         if total is not None:
             here = here + hop(total.astype(bf16), down_line).astype(jnp.float32)
         total = here
-    query_back = rope_apply(queries_grad, head_cos, head_sin, True).astype(bf16)
+    query_back = carry
     key_back = rope_apply(total[:, :key_cols], head_cos, head_sin, True).astype(bf16)
     value_back = total[:, key_cols:].astype(bf16)
-    output_grad = spread(weight_grad(attended_rows, mixed_head))
-    query_grad = spread(weight_grad(normed, query_back))
+    output_chunk = weight_grad(attended_rows, mixed_head)
+    query_chunk = weight_grad(normed, query_back)
+    both_pieces = to_owners(jnp.concatenate([output_chunk, query_chunk], axis=2))
+    output_grad = spread([piece[:, :query_cols] for piece in both_pieces])
+    query_grad = spread([piece[:, query_cols:] for piece in both_pieces])
     pair_back = jnp.concatenate([key_back, value_back], axis=1)
-    pair_pieces = weight_grad(normed, pair_back)
+    pair_pieces = to_owners(weight_grad(normed, pair_back))
     key_grad = spread([piece[:, :key_cols] for piece in pair_pieces])
     value_grad = spread([piece[:, key_cols:] for piece in pair_pieces])
     normed_part = contract_cols(jnp.concatenate([query_back, pair_back], axis=1), in_full)
@@ -600,18 +721,7 @@
     input_grad = middle_grad + input_part
 
     gain_parts = jnp.stack([first_part, second_part, third_part, fourth_part])
-    gain_parts = gain_parts.reshape(4, seq_count, count, own_rows)
-    gain_sums = None
-    for step in range(count):
-        piece = lax.dynamic_slice_in_dim(gain_parts, lax.rem(fsdp_rank + step, count), 1, 2)
-        piece = turn(piece, step) if step else piece
-        gain_sums = piece if gain_sums is None else gain_sums + piece
-    gain_sums = gain_sums[:, :, 0]
-    gain_grads = None
-    for j in range(seq_count):
-        piece = lax.dynamic_slice_in_dim(gain_sums, seq_rank ^ j, 1, 1)[:, 0]
-        piece = flip(piece, j) if j else piece
-        gain_grads = piece if gain_grads is None else gain_grads + piece
+    gain_grads = lax.dynamic_slice_in_dim(sum_all(gain_parts), own_start, own_rows, 1)
     return (
         layer_out,
         input_grad,

time: 733 us -> 765 us (1.044)
  matrix products: 113 us -> 189 us
  local copies, waits for them, and re-layouts: 70.4 us -> 54.9 us
  waiting for transfers between devices: 303 us -> 289 us
  starting transfers between devices: 160 us -> 147 us
  other arithmetic: 51.1 us -> 40.7 us
  Pallas kernels: 21.7 us -> 30.3 us
    dot_general x17, matrix products: 54.3 us -> 86.3 us  [contract_cols(): lax.dot_general(left, right, (((1,), (1,)), ((), ())), preferred_element_...]
    ppermute x96 -> x88, waiting for transfers between devices: 214 us -> 193 us  [hop(): return lax.ppermute(value, 'fsdp', pairs)]
    dot_general x5, matrix products: 7.4 us -> 21.5 us  [layer(): jnp.dot(gate_delta, gate_units, preferred_element_type=jnp.float32)]
    ppermute x96 -> x88, starting transfers between devices: 132 us -> 120 us  [hop(): return lax.ppermute(value, 'fsdp', pairs)]
    dot_general x5, matrix products: 10.2 us -> 21.7 us  [layer(): jnp.dot(hidden, down_units, preferred_element_type=jnp.float32)]
    dot_general x5, matrix products: 10.8 us -> 21.6 us  [layer(): jnp.dot(up_delta, up_units, preferred_element_type=jnp.float32)]
    slice x14 -> x0, local copies, waits for them, and re-layouts: 9.04 us -> none  [the longest x3 5.31 us: unit_grad(): full[cut:]]
    pallas_call x3 -> x4, Pallas kernels: 14.6 us -> 23.3 us  [the longest x3 16.4 us: attend_back(): pl.pallas_call(functools.partial(attend_back_kernel, heads, first, carry...]
  transfers between devices with their start and end apart: 144 -> 131, of which waited for: 60 -> 68; matrix products, arithmetic and copies ran while one was open for 25% -> 29% of each run, Pallas kernels for 3% -> 4%
where the time goes in v1:
time: 765 us; the launch traced here: 755 us
  waiting for transfers between devices  289 us (38%)
  matrix products  189 us (25%)
  starting transfers between devices  147 us (19%)
  local copies, waits for them, and re-layouts  54.9 us (7%)
  other arithmetic  40.7 us (5%)
  Pallas kernels  30.3 us (4%)
    ppermute x88, waiting for transfers between devices, hop(): return lax.ppermute(value, 'fsdp', pairs)  193 us
    ppermute x88, starting transfers between devices, hop(): return lax.ppermute(value, 'fsdp', pairs)  120 us
    ppermute x43, waiting for transfers between devices, flip(): return lax.ppermute(value, 'seq', [(i, i ^ bits) for i in range(seq_count)])  96.4 us
    dot_general x17, matrix products, contract_cols(): lax.dot_general(left, right, (((1,), (1,)), ((), ())), preferred_element_...  86.3 us
    dot_general x9, matrix products, contract_rows(): lax.dot_general(left, right, (((0,), (0,)), ((), ())), preferred_element_...  34 us
    unnamed x209, local copies, waits for them, and re-layouts  27.2 us
    ppermute x43, starting transfers between devices, flip(): return lax.ppermute(value, 'seq', [(i, i ^ bits) for i in range(seq_count)])  26.5 us
    dot_general x5, matrix products, layer(): jnp.dot(hidden, down_units, preferred_element_type=jnp.float32)  21.7 us
  transfers between devices with their start and end apart: 131, of which 68 were waited for; matrix products, arithmetic and copies ran while one was open for 29% of the time, Pallas kernels for 4%

profile of v1, /device:TPU:0, one launch (start us, length us, event | category | flops | bytes accessed | tf_op | source)
XLA Modules:
  0.0 754.6 jit_solution(16420369110821383785)
XLA Ops:
  39.2 9.6 %collective-permute-done.4 = bf16[128,2304]{1,0:T(8,128)(2,1)S(1)} collective-permute-done((bf16[128,2304]{1,0:T(8,128)(2,1)S(1)}, bf16[128,2304]{1,0:T(8,128)(2,1)S(1)}, u32[]{:S(2)}, u32[]{:S(2)}) %collective-permute-start.4) | collective-permute-done | bytes 589856 | tf_op jit(solution)/shard_map/ppermute | solution.py:399
  57.4 8.5 %collective-permute-done.13 = bf16[4,72,1024]{2,1,0:T(8,128)(2,1)S(1)} collective-permute-done((bf16[4,72,1024]{2,1,0:T(8,128)(2,1)S(1)}, bf16[4,72,1024]{2,1,0:T(8,128)(2,1)S(1)}, u32[]{:S(2)}, u32[]{:S(2)}) %collective-permute-start.13) | collective-permute-done | bytes 589856 | tf_op jit(solution)/shard_map/ppermute | solution.py:402
  87.9 21.3 %collective-permute-done.41 = bf16[288,2304]{1,0:T(8,128)(2,1)S(1)} collective-permute-done((bf16[288,2304]{1,0:T(8,128)(2,1)S(1)}, bf16[288,2304]{1,0:T(8,128)(2,1)S(1)}, u32[]{:S(2)}, u32[]{:S(2)}) %collective-permute-start.41) | collective-permute-done | bytes 1327136 | tf_op jit(solution)/shard_map/ppermute | solution.py:399
  116.2 20.3 %collective-permute-done.44 = bf16[288,2304]{1,0:T(8,128)(2,1)S(1)} collective-permute-done((bf16[288,2304]{1,0:T(8,128)(2,1)S(1)}, bf16[288,2304]{1,0:T(8,128)(2,1)S(1)}, u32[]{:S(2)}, u32[]{:S(2)}) %collective-permute-start.44) | collective-permute-done | bytes 1327136 | tf_op jit(solution)/shard_map/ppermute | solution.py:399
  140.8 6.9 project.1
  159.9 6.4 collective-permute-done.20
  176.5 10.8 %collective-permute-done.31 = bf16[4,72,512]{2,1,0:T(8,128)(2,1)S(1)} collective-permute-done((bf16[4,72,512]{2,1,0:T(8,128)(2,1)S(1)}, bf16[4,72,512]{2,1,0:T(8,128)(2,1)S(1)}, u32[]{:S(2)}, u32[]{:S(2)}) %collective-permute-start.31) | collective-permute-done | bytes 294944 | tf_op jit(solution)/shard_map/ppermute | solution.py:402
  195.9 7.9 %collective-permute-done.23 = bf16[512,512]{1,0:T(8,128)(2,1)S(1)} collective-permute-done((bf16[512,512]{1,0:T(8,128)(2,1)S(1)}, bf16[512,512]{1,0:T(8,128)(2,1)S(1)}, u32[]{:S(2)}, u32[]{:S(2)}) %collective-permute-start.23) | collective-permute-done | bytes 524320 | tf_op jit(solution)/shard_map/ppermute | solution.py:402
  205.5 7.0 attend.1
  229.5 6.4 collective-permute-done.37
  247.0 5.6 constant_dynamic-update-slice_fusion.52
  263.5 5.5 constant_dynamic-update-slice_fusion.51
  269.1 5.8 collective-permute-done.49
  282.1 5.6 constant_dynamic-update-slice_fusion.50
  287.6 5.8 collective-permute-done.51
  300.2 6.0 constant_dynamic-update-slice_fusion.49
  306.3 6.4 fusion.195
  312.8 5.6 constant_dynamic-update-slice_fusion.48
  340.3 7.3 collective-permute-done.57
  354.7 7.3 collective-permute-done.59
  365.7 8.6 %collective-permute-done.61 = bf16[128,2304]{1,0:T(8,128)(2,1)} collective-permute-done((bf16[128,2304]{1,0:T(8,128)(2,1)}, bf16[128,2304]{1,0:T(8,128)(2,1)}, u32[]{:S(2)}, u32[]{:S(2)}) %collective-permute-start.61) | collective-permute-done | bytes 589856 | tf_op jit(solution)/shard_map/ppermute | solution.py:402
  442.9 5.3 fusion.199
  459.5 5.6 constant_dynamic-update-slice_fusion.29
  491.3 9.2 %collective-permute-done.73 = bf16[128,2304]{1,0:T(8,128)(2,1)S(1)} collective-permute-done((bf16[128,2304]{1,0:T(8,128)(2,1)S(1)}, bf16[128,2304]{1,0:T(8,128)(2,1)S(1)}, u32[]{:S(2)}, u32[]{:S(2)}) %collective-permute-start.73) | collective-permute-done | bytes 589856 | tf_op jit(solution)/shard_map/ppermute | solution.py:402
  509.2 6.4 collective-permute-done.75
  565.3 7.2 attend_back.5
  575.3 6.2 collective-permute-start.103
  604.2 12.5 %collective-permute-done.106 = bf16[4,72,512]{2,1,0:T(8,128)(2,1)S(1)} collective-permute-done((bf16[4,72,512]{2,1,0:T(8,128)(2,1)S(1)}, bf16[4,72,512]{2,1,0:T(8,128)(2,1)S(1)}, u32[]{:S(2)}, u32[]{:S(2)}) %collective-permute-start.106) | collective-permute-done | bytes 294944 | tf_op jit(solution)/shard_map/ppermute | solution.py:402
  650.3 9.0 %collective-permute-done.128 = bf16[288,2304]{1,0:T(8,128)(2,1)S(1)} collective-permute-done((bf16[288,2304]{1,0:T(8,128)(2,1)S(1)}, bf16[288,2304]{1,0:T(8,128)(2,1)S(1)}, u32[]{:S(2)}, u32[]{:S(2)}) %collective-permute-start.128) | collective-permute-done | bytes 1327136 | tf_op jit(solution)/shard_map/ppermute | solution.py:399
  662.5 17.3 %collective-permute-done.126 = bf16[288,2304]{1,0:T(8,128)(2,1)S(1)} collective-permute-done((bf16[288,2304]{1,0:T(8,128)(2,1)S(1)}, bf16[288,2304]{1,0:T(8,128)(2,1)S(1)}, u32[]{:S(2)}, u32[]{:S(2)}) %collective-permute-start.126) | collective-permute-done | bytes 1327136 | tf_op jit(solution)/shard_map/ppermute | solution.py:399
  685.5 14.1 %collective-permute-done.86 = bf16[512,512]{1,0:T(8,128)(2,1)S(1)} collective-permute-done((bf16[512,512]{1,0:T(8,128)(2,1)S(1)}, bf16[512,512]{1,0:T(8,128)(2,1)S(1)}, u32[]{:S(2)}, u32[]{:S(2)}) %collective-permute-start.86) | collective-permute-done | bytes 524320 | tf_op jit(solution)/shard_map/ppermute | solution.py:402
  746.6 5.7 collective-permute-done.123
  (673 shorter events, 478.0 us)
Async XLA Ops:
  2.7 29.0 %collective-permute-start = (bf16[72,1024]{1,0:T(8,128)(2,1)S(1)}, bf16[72,1024]{1,0:T(8,128)(2,1)S(1)}, u32[]{:S(2)}, u32[]{:S(2)}) collective-permute-start(bf16[72,1024]{1,0:T(8,128)(2,1)S(1)} %pad_maximum_fusion.4), channel_id=1, source_target_pairs={{0,8},{8,0},{16,24},{24,16},{1,9},{9,1},{17,25},{25,17},{2,10},{10... | collective-permute-start | bytes 442376 | tf_op jit(solution)/shard_map/ppermute | solution.py:399
  3.3 28.4 %collective-permute-start.1 = (bf16[72,1024]{1,0:T(8,128)(2,1)S(1)}, bf16[72,1024]{1,0:T(8,128)(2,1)S(1)}, u32[]{:S(2)}, u32[]{:S(2)}) collective-permute-start(bf16[72,1024]{1,0:T(8,128)(2,1)S(1)} %pad_maximum_fusion.5), channel_id=1, source_target_pairs={{0,16},{8,24},{16,0},{24,8},{1,17},{9,25},{17,1},{25,9},{2,18},{10... | collective-permute-start | bytes 442376 | tf_op jit(solution)/shard_map/ppermute | solution.py:399
  5.9 25.9 %collective-permute-start.2 = (bf16[72,1024]{1,0:T(8,128)(2,1)S(1)}, bf16[72,1024]{1,0:T(8,128)(2,1)S(1)}, u32[]{:S(2)}, u32[]{:S(2)}) collective-permute-start(bf16[72,1024]{1,0:T(8,128)(2,1)S(1)} %pad_maximum_fusion.6), channel_id=1, source_target_pairs={{0,24},{8,16},{16,8},{24,0},{1,25},{9,17},{17,9},{25,1},{2,26},{10... | collective-permute-start | bytes 442376 | tf_op jit(solution)/shard_map/ppermute | solution.py:399
  35.5 21.9 %collective-permute-start.3 = (bf16[128,2304]{1,0:T(8,128)(2,1)S(1)}, bf16[128,2304]{1,0:T(8,128)(2,1)S(1)}, u32[]{:S(2)}, u32[]{:S(2)}) collective-permute-start(bf16[128,2304]{1,0:T(8,128)(2,1)S(1)} %copy-done.3), channel_id=1, source_target_pairs={{0,8},{8,0},{16,24},{24,16},{1,9},{9,1},{17,25},{25,17},{2,10},{10... | collective-permute-start | bytes 1769480 | tf_op jit(solution)/shard_map/ppermute | solution.py:399
  48.8 36.6 %collective-permute-start.38 = (bf16[288,2304]{1,0:T(8,128)(2,1)S(1)}, bf16[288,2304]{1,0:T(8,128)(2,1)}, u32[]{:S(2)}, u32[]{:S(2)}) collective-permute-start(bf16[288,2304]{1,0:T(8,128)(2,1)S(1)} %copy-done.16), channel_id=1, source_target_pairs={{0,16},{8,24},{16,0},{24,8},{1,17},{9,25},{17,1},{25,9},{2,18},{10... | collective-permute-start | bytes 3981320 | tf_op jit(solution)/shard_map/ppermute | solution.py:399
  57.3 54.8 %collective-permute-start.39 = (bf16[288,2304]{1,0:T(8,128)(2,1)S(1)}, bf16[288,2304]{1,0:T(8,128)(2,1)S(1)}, u32[]{:S(2)}, u32[]{:S(2)}) collective-permute-start(bf16[288,2304]{1,0:T(8,128)(2,1)S(1)} %copy-done.16), channel_id=1, source_target_pairs={{0,8},{8,0},{16,24},{24,16},{1,9},{9,1},{17,25},{25,17},{2,10},{10... | collective-permute-start | bytes 3981320 | tf_op jit(solution)/shard_map/ppermute | solution.py:399
  65.9 43.3 %collective-permute-start.41 = (bf16[288,2304]{1,0:T(8,128)(2,1)S(1)}, bf16[288,2304]{1,0:T(8,128)(2,1)S(1)}, u32[]{:S(2)}, u32[]{:S(2)}) collective-permute-start(bf16[288,2304]{1,0:T(8,128)(2,1)S(1)} %copy-done.17), channel_id=1, source_target_pairs={{0,16},{8,24},{16,0},{24,8},{1,17},{9,25},{17,1},{25,9},{2,18},{10... | collective-permute-start | bytes 3981320 | tf_op jit(solution)/shard_map/ppermute | solution.py:399
  81.3 33.8 %collective-permute-start.42 = (bf16[288,2304]{1,0:T(8,128)(2,1)S(1)}, bf16[288,2304]{1,0:T(8,128)(2,1)S(1)}, u32[]{:S(2)}, u32[]{:S(2)}) collective-permute-start(bf16[288,2304]{1,0:T(8,128)(2,1)S(1)} %copy-done.17), channel_id=1, source_target_pairs={{0,8},{8,0},{16,24},{24,16},{1,9},{9,1},{17,25},{25,17},{2,10},{10... | collective-permute-start | bytes 3981320 | tf_op jit(solution)/shard_map/ppermute | solution.py:399
  83.2 53.3 %collective-permute-start.44 = (bf16[288,2304]{1,0:T(8,128)(2,1)S(1)}, bf16[288,2304]{1,0:T(8,128)(2,1)S(1)}, u32[]{:S(2)}, u32[]{:S(2)}) collective-permute-start(bf16[288,2304]{1,0:T(8,128)(2,1)S(1)} %copy-done.18), channel_id=1, source_target_pairs={{0,16},{8,24},{16,0},{24,8},{1,17},{9,25},{17,1},{25,9},{2,18},{10... | collective-permute-start | bytes 3981320 | tf_op jit(solution)/shard_map/ppermute | solution.py:399
  85.4 131.3 %collective-permute-start.45 = (bf16[288,2304]{1,0:T(8,128)(2,1)S(1)}, bf16[288,2304]{1,0:T(8,128)(2,1)}, u32[]{:S(2)}, u32[]{:S(2)}) collective-permute-start(bf16[288,2304]{1,0:T(8,128)(2,1)S(1)} %copy-done.18), channel_id=1, source_target_pairs={{0,8},{8,0},{16,24},{24,16},{1,9},{9,1},{17,25},{25,17},{2,10},{10... | collective-permute-start | bytes 3981320 | tf_op jit(solution)/shard_map/ppermute | solution.py:399
  109.2 28.6 %collective-permute-start.17 = (bf16[4,72,512]{2,1,0:T(8,128)(2,1)S(1)}, bf16[4,72,512]{2,1,0:T(8,128)(2,1)S(1)}, u32[]{:S(2)}, u32[]{:S(2)}) collective-permute-start(bf16[4,72,512]{2,1,0:T(8,128)(2,1)S(1)} %slice.316), channel_id=1, source_target_pairs={{0,2},{2,4},{4,6},{6,7},{7,5},{5,3},{3,1},{1,0},{8,10},{10,12},{12... | collective-permute-start | bytes 884744 | tf_op jit(solution)/shard_map/ppermute | solution.py:402
  112.2 25.6 %collective-permute-start.18 = (bf16[4,72,512]{2,1,0:T(8,128)(2,1)S(1)}, bf16[4,72,512]{2,1,0:T(8,128)(2,1)S(1)}, u32[]{:S(2)}, u32[]{:S(2)}) collective-permute-start(bf16[4,72,512]{2,1,0:T(8,128)(2,1)S(1)} %slice.317), channel_id=1, source_target_pairs={{2,0},{4,2},{6,4},{7,6},{5,7},{3,5},{1,3},{0,1},{10,8},{12,10},{14... | collective-permute-start | bytes 884744 | tf_op jit(solution)/shard_map/ppermute | solution.py:402
  138.0 19.7 %collective-permute-start.28 = (bf16[4,72,512]{2,1,0:T(8,128)(2,1)S(1)}, bf16[4,72,512]{2,1,0:T(8,128)(2,1)S(1)}, u32[]{:S(2)}, u32[]{:S(2)}) collective-permute-start(bf16[4,72,512]{2,1,0:T(8,128)(2,1)S(1)} %bitcast_dynamic-update-slice_fusion.18), channel_id=1, source_target_pairs={{2,0},{4,2},{6,4},{7,6},{5,7},{3,5},{1,3},{0,1},{10,8},{12,10},{14... | collective-permute-start | bytes 884744 | tf_op jit(solution)/shard_map/ppermute | solution.py:402
  166.3 29.5 %collective-permute-start.21 = (bf16[512,512]{1,0:T(8,128)(2,1)S(1)}, bf16[512,512]{1,0:T(8,128)(2,1)S(1)}, u32[]{:S(2)}, u32[]{:S(2)}) collective-permute-start(bf16[512,512]{1,0:T(8,128)(2,1)S(1)} %collective-permute-done.20), channel_id=1, source_target_pairs={{0,1},{2,3},{4,5},{6,7},{1,0},{3,2},{5,4},{7,6},{8,9},{10,11},{12,... | collective-permute-start | bytes 1572872 | tf_op jit(solution)/shard_map/ppermute | solution.py:402
  166.3 24.4 %collective-permute-start.22 = (bf16[512,512]{1,0:T(8,128)(2,1)S(1)}, bf16[512,512]{1,0:T(8,128)(2,1)S(1)}, u32[]{:S(2)}, u32[]{:S(2)}) collective-permute-start(bf16[512,512]{1,0:T(8,128)(2,1)S(1)} %collective-permute-done.20), channel_id=1, source_target_pairs={{0,2},{1,3},{2,4},{3,5},{4,6},{5,7},{8,10},{9,11},{10,12},{11,13},... | collective-permute-start | bytes 1572872 | tf_op jit(solution)/shard_map/ppermute | solution.py:402
  195.8 26.5 %collective-permute-start.40 = (bf16[288,2304]{1,0:T(8,128)(2,1)}, bf16[288,2304]{1,0:T(8,128)(2,1)}, u32[]{:S(2)}, u32[]{:S(2)}) collective-permute-start(bf16[288,2304]{1,0:T(8,128)(2,1)} %collective-permute-done.38), channel_id=1, source_target_pairs={{0,8},{8,0},{16,24},{24,16},{1,9},{9,1},{17,25},{25,17},{2,10},{10... | collective-permute-start | bytes 3981320 | tf_op jit(solution)/shard_map/ppermute | solution.py:399
  459.5 88.9 %collective-permute-start.129 = (bf16[640,2304]{1,0:T(8,128)(2,1)}, bf16[640,2304]{1,0:T(8,128)(2,1)S(1)}, u32[]{:S(2)}, u32[]{:S(2)}) collective-permute-start(bf16[640,2304]{1,0:T(8,128)(2,1)} %convolution_convert_fusion), channel_id=1, source_target_pairs={{0,8},{8,0},{16,24},{24,16},{1,9},{9,1},{17,25},{25,17},{2,10},{10... | collective-permute-start | bytes 8847368 | tf_op jit(solution)/shard_map/ppermute | solution.py:399
  481.4 108.3 %collective-permute-start.127 = (bf16[640,2304]{1,0:T(8,128)(2,1)}, bf16[640,2304]{1,0:T(8,128)(2,1)}, u32[]{:S(2)}, u32[]{:S(2)}) collective-permute-start(bf16[640,2304]{1,0:T(8,128)(2,1)} %convolution_convert_fusion.2), channel_id=1, source_target_pairs={{0,8},{8,0},{16,24},{24,16},{1,9},{9,1},{17,25},{25,17},{2,10},{10... | collective-permute-start | bytes 8847368 | tf_op jit(solution)/shard_map/ppermute | solution.py:399
  524.0 74.4 %collective-permute-start.125 = (bf16[640,2304]{1,0:T(8,128)(2,1)}, bf16[640,2304]{1,0:T(8,128)(2,1)}, u32[]{:S(2)}, u32[]{:S(2)}) collective-permute-start(bf16[640,2304]{1,0:T(8,128)(2,1)} %convolution_convert_fusion.4), channel_id=1, source_target_pairs={{0,8},{8,0},{16,24},{24,16},{1,9},{9,1},{17,25},{25,17},{2,10},{10... | collective-permute-start | bytes 8847368 | tf_op jit(solution)/shard_map/ppermute | solution.py:399
  550.1 85.7 %collective-permute-start.130 = (bf16[288,2304]{1,0:T(8,128)(2,1)}, bf16[288,2304]{1,0:T(8,128)(2,1)}, u32[]{:S(2)}, u32[]{:S(2)}) collective-permute-start(bf16[288,2304]{1,0:T(8,128)(2,1)} %add_convert_fusion), channel_id=1, source_target_pairs={{0,16},{8,24},{16,0},{24,8},{1,17},{9,25},{17,1},{25,9},{2,18},{10... | collective-permute-start | bytes 3981320 | tf_op jit(solution)/shard_map/ppermute | solution.py:399
  594.2 31.6 %collective-permute-start.84 = (bf16[512,512]{1,0:T(8,128)(2,1)S(1)}, bf16[512,512]{1,0:T(8,128)(2,1)S(1)}, u32[]{:S(2)}, u32[]{:S(2)}) collective-permute-start(bf16[512,512]{1,0:T(8,128)(2,1)S(1)} %copy-done.71), channel_id=1, source_target_pairs={{0,1},{2,3},{4,5},{6,7},{8,9},{10,11},{12,13},{14,15},{16,17},{18,... | collective-permute-start | bytes 1572872 | tf_op jit(solution)/shard_map/ppermute | solution.py:402
  598.4 18.6 %collective-permute-start.97 = (bf16[4,72,512]{2,1,0:T(8,128)(2,1)S(1)}, bf16[4,72,512]{2,1,0:T(8,128)(2,1)S(1)}, u32[]{:S(2)}, u32[]{:S(2)}) collective-permute-start(bf16[4,72,512]{2,1,0:T(8,128)(2,1)S(1)} %get-tuple-element.203), channel_id=1, source_target_pairs={{0,2},{2,4},{4,6},{6,7},{7,5},{5,3},{3,1},{1,0},{8,10},{10,12},{12... | collective-permute-start | bytes 884744 | tf_op jit(solution)/shard_map/ppermute | solution.py:402
  600.5 22.5 %collective-permute-start.98 = (bf16[4,72,512]{2,1,0:T(8,128)(2,1)S(1)}, bf16[4,72,512]{2,1,0:T(8,128)(2,1)S(1)}, u32[]{:S(2)}, u32[]{:S(2)}) collective-permute-start(bf16[4,72,512]{2,1,0:T(8,128)(2,1)S(1)} %get-tuple-element.202), channel_id=1, source_target_pairs={{2,0},{4,2},{6,4},{7,6},{5,7},{3,5},{1,3},{0,1},{10,8},{12,10},{14... | collective-permute-start | bytes 884744 | tf_op jit(solution)/shard_map/ppermute | solution.py:402
  627.3 32.0 %collective-permute-start.128 = (bf16[288,2304]{1,0:T(8,128)(2,1)S(1)}, bf16[288,2304]{1,0:T(8,128)(2,1)S(1)}, u32[]{:S(2)}, u32[]{:S(2)}) collective-permute-start(bf16[288,2304]{1,0:T(8,128)(2,1)S(1)} %add_convert_fusion.1), channel_id=1, source_target_pairs={{0,16},{8,24},{16,0},{24,8},{1,17},{9,25},{17,1},{25,9},{2,18},{10... | collective-permute-start | bytes 3981320 | tf_op jit(solution)/shard_map/ppermute | solution.py:399
  641.8 38.0 %collective-permute-start.126 = (bf16[288,2304]{1,0:T(8,128)(2,1)S(1)}, bf16[288,2304]{1,0:T(8,128)(2,1)S(1)}, u32[]{:S(2)}, u32[]{:S(2)}) collective-permute-start(bf16[288,2304]{1,0:T(8,128)(2,1)S(1)} %add_convert_fusion.2), channel_id=1, source_target_pairs={{0,16},{8,24},{16,0},{24,8},{1,17},{9,25},{17,1},{25,9},{2,18},{10... | collective-permute-start | bytes 3981320 | tf_op jit(solution)/shard_map/ppermute | solution.py:399
  642.5 42.9 %collective-permute-start.82 = (bf16[512,512]{1,0:T(8,128)(2,1)S(1)}, bf16[512,512]{1,0:T(8,128)(2,1)S(1)}, u32[]{:S(2)}, u32[]{:S(2)}) collective-permute-start(bf16[512,512]{1,0:T(8,128)(2,1)S(1)} %copy-done.69), channel_id=1, source_target_pairs={{1,0},{3,2},{5,4},{7,6},{9,8},{11,10},{13,12},{15,14},{17,16},{19,... | collective-permute-start | bytes 1572872 | tf_op jit(solution)/shard_map/ppermute | solution.py:402
  645.1 38.3 %collective-permute-start.83 = (bf16[512,512]{1,0:T(8,128)(2,1)S(1)}, bf16[512,512]{1,0:T(8,128)(2,1)S(1)}, u32[]{:S(2)}, u32[]{:S(2)}) collective-permute-start(bf16[512,512]{1,0:T(8,128)(2,1)S(1)} %copy-done.70), channel_id=1, source_target_pairs={{1,0},{3,2},{5,4},{7,6},{0,1},{2,3},{4,5},{6,7},{9,8},{11,10},{13,... | collective-permute-start | bytes 1572872 | tf_op jit(solution)/shard_map/ppermute | solution.py:402
  648.8 34.7 %collective-permute-start.85 = (bf16[512,512]{1,0:T(8,128)(2,1)S(1)}, bf16[512,512]{1,0:T(8,128)(2,1)S(1)}, u32[]{:S(2)}, u32[]{:S(2)}) collective-permute-start(bf16[512,512]{1,0:T(8,128)(2,1)S(1)} %add_convert_fusion.4), channel_id=1, source_target_pairs={{2,0},{3,1},{4,2},{5,3},{6,4},{7,5},{10,8},{11,9},{12,10},{13,11},... | collective-permute-start | bytes 1572872 | tf_op jit(solution)/shard_map/ppermute | solution.py:402
  659.3 26.0 %collective-permute-start.111 = (bf16[72,1024]{1,0:T(8,128)(2,1)S(1)}, bf16[72,1024]{1,0:T(8,128)(2,1)S(1)}, u32[]{:S(2)}, u32[]{:S(2)}) collective-permute-start(bf16[72,1024]{1,0:T(8,128)(2,1)S(1)} %get-tuple-element.247), channel_id=1, source_target_pairs={{0,8},{8,0},{16,24},{24,16},{1,9},{9,1},{17,25},{25,17},{2,10},{10... | collective-permute-start | bytes 442376 | tf_op jit(solution)/shard_map/ppermute | solution.py:399
  683.4 32.2 %collective-permute-start.113 = (bf16[72,1024]{1,0:T(8,128)(2,1)S(1)}, bf16[72,1024]{1,0:T(8,128)(2,1)S(1)}, u32[]{:S(2)}, u32[]{:S(2)}) collective-permute-start(bf16[72,1024]{1,0:T(8,128)(2,1)S(1)} %get-tuple-element.245), channel_id=1, source_target_pairs={{0,24},{8,16},{16,8},{24,0},{1,25},{9,17},{17,9},{25,1},{2,26},{10... | collective-permute-start | bytes 442376 | tf_op jit(solution)/shard_map/ppermute | solution.py:399
  720.4 19.1 %collective-permute-start.88 = (bf16[128,2304]{1,0:T(8,128)(2,1)S(1)}, bf16[128,2304]{1,0:T(8,128)(2,1)S(1)}, u32[]{:S(2)}, u32[]{:S(2)}) collective-permute-start(bf16[128,2304]{1,0:T(8,128)(2,1)S(1)} %get-tuple-element.213), channel_id=1, source_target_pairs={{0,8},{8,0},{16,24},{24,16},{1,9},{9,1},{17,25},{25,17},{2,10},{10... | collective-permute-start | bytes 1769480 | tf_op jit(solution)/shard_map/ppermute | solution.py:399
  720.5 31.9 %collective-permute-start.87 = (bf16[128,2304]{1,0:T(8,128)(2,1)S(1)}, bf16[128,2304]{1,0:T(8,128)(2,1)S(1)}, u32[]{:S(2)}, u32[]{:S(2)}) collective-permute-start(bf16[128,2304]{1,0:T(8,128)(2,1)S(1)} %get-tuple-element.212), channel_id=1, source_target_pairs={{0,8},{8,0},{16,24},{24,16},{1,9},{9,1},{17,25},{25,17},{2,10},{10... | collective-permute-start | bytes 1769480 | tf_op jit(solution)/shard_map/ppermute | solution.py:399
  (186 other events, 2009.8 us)

commit v2 on v1

--- a/solution.py
+++ b/solution.py
@@ -449,12 +449,12 @@
 
     def sum_all(value):
         bits = 1
+        while bits < count:
+            value = value + hop(value, [(i, i ^ bits) for i in range(count)])
+            bits *= 2
+        bits = 1
         while bits < seq_count:
             value = value + flip(value, bits)
-            bits *= 2
-        bits = 1
-        while bits < count:
-            value = value + hop(value, [(i, i ^ bits) for i in range(count)])
             bits *= 2
         return value
 
@@ -705,15 +705,14 @@
     key_back = rope_apply(total[:, :key_cols], head_cos, head_sin, True).astype(bf16)
     value_back = total[:, key_cols:].astype(bf16)
     output_chunk = weight_grad(attended_rows, mixed_head)
-    query_chunk = weight_grad(normed, query_back)
-    both_pieces = to_owners(jnp.concatenate([output_chunk, query_chunk], axis=2))
-    output_grad = spread([piece[:, :query_cols] for piece in both_pieces])
-    query_grad = spread([piece[:, query_cols:] for piece in both_pieces])
-    pair_back = jnp.concatenate([key_back, value_back], axis=1)
-    pair_pieces = to_owners(weight_grad(normed, pair_back))
-    key_grad = spread([piece[:, :key_cols] for piece in pair_pieces])
-    value_grad = spread([piece[:, key_cols:] for piece in pair_pieces])
-    normed_part = contract_cols(jnp.concatenate([query_back, pair_back], axis=1), in_full)
+    output_grad = spread(to_owners(output_chunk))
+    head_back = jnp.concatenate([query_back, key_back, value_back], axis=1)
+    head_pieces = to_owners(weight_grad(normed, head_back))
+    value_begin = query_cols + key_cols
+    query_grad = spread([piece[:, :query_cols] for piece in head_pieces])
+    key_grad = spread([piece[:, query_cols:value_begin] for piece in head_pieces])
+    value_grad = spread([piece[:, value_begin:] for piece in head_pieces])
+    normed_part = contract_cols(head_back, in_full)
     normed_grad = seq_scatter(jnp.split(normed_part, seq_count, axis=0))
     head_scaling = lax.rsqrt(jnp.mean(head_in * head_in, axis=-1, keepdims=True) + epsilon)
     first_part = jnp.sum(normed_part * head_in * head_scaling, axis=0)

time: 765 us -> 739 us (0.966)
  starting transfers between devices: 147 us -> 129 us
    ppermute x43, waiting for transfers between devices: 96.4 us -> 80.8 us  [flip(): return lax.ppermute(value, 'seq', [(i, i ^ bits) for i in range(seq_count)])]
    ppermute x88 -> x80, starting transfers between devices: 120 us -> 107 us  [hop(): return lax.ppermute(value, 'fsdp', pairs)]
    ppermute x88 -> x80, waiting for transfers between devices: 193 us -> 202 us  [hop(): return lax.ppermute(value, 'fsdp', pairs)]
    dot_general x9 -> x8, matrix products: 34 us -> 27.5 us  [contract_rows(): lax.dot_general(left, right, (((0,), (0,)), ((), ())), preferred_element_...]
    unnamed x209 -> x193, local copies, waits for them, and re-layouts: 27.2 us -> 27.5 us
  transfers between devices with their start and end apart: 131 -> 123, of which waited for: 68 -> 62; matrix products, arithmetic and copies ran while one was open for 29% -> 30% of each run, Pallas kernels for 4% -> 4%
where the time goes in v2:
time: 739 us; the launch traced here: 729 us
  waiting for transfers between devices  283 us (38%)
  matrix products  183 us (25%)
  starting transfers between devices  129 us (17%)
  local copies, waits for them, and re-layouts  55.2 us (7%)
  other arithmetic  46 us (6%)
  Pallas kernels  29.9 us (4%)
    ppermute x80, waiting for transfers between devices, hop(): return lax.ppermute(value, 'fsdp', pairs)  202 us
    ppermute x80, starting transfers between devices, hop(): return lax.ppermute(value, 'fsdp', pairs)  107 us
    dot_general x17, matrix products, contract_cols(): lax.dot_general(left, right, (((1,), (1,)), ((), ())), preferred_element_...  86.3 us
    ppermute x43, waiting for transfers between devices, flip(): return lax.ppermute(value, 'seq', [(i, i ^ bits) for i in range(seq_count)])  80.8 us
    dot_general x8, matrix products, contract_rows(): lax.dot_general(left, right, (((0,), (0,)), ((), ())), preferred_element_...  27.5 us
    unnamed x193, local copies, waits for them, and re-layouts  27.5 us
    ppermute x43, starting transfers between devices, flip(): return lax.ppermute(value, 'seq', [(i, i ^ bits) for i in range(seq_count)])  22.7 us
    dot_general x5, matrix products, layer(): jnp.dot(hidden, down_units, preferred_element_type=jnp.float32)  21.7 us
  transfers between devices with their start and end apart: 123, of which 62 were waited for; matrix products, arithmetic and copies ran while one was open for 30% of the time, Pallas kernels for 4%

profile of v2, /device:TPU:0, one launch (start us, length us, event | category | flops | bytes accessed | tf_op | source)
XLA Modules:
  0.0 729.2 jit_solution(3491676055464416355)
XLA Ops:
  37.6 9.1 %collective-permute-done.4 = bf16[128,2304]{1,0:T(8,128)(2,1)S(1)} collective-permute-done((bf16[128,2304]{1,0:T(8,128)(2,1)S(1)}, bf16[128,2304]{1,0:T(8,128)(2,1)S(1)}, u32[]{:S(2)}, u32[]{:S(2)}) %collective-permute-start.4) | collective-permute-done | bytes 589856 | tf_op jit(solution)/shard_map/ppermute | solution.py:399
  54.7 8.5 %collective-permute-done.13 = bf16[4,72,1024]{2,1,0:T(8,128)(2,1)S(1)} collective-permute-done((bf16[4,72,1024]{2,1,0:T(8,128)(2,1)S(1)}, bf16[4,72,1024]{2,1,0:T(8,128)(2,1)S(1)}, u32[]{:S(2)}, u32[]{:S(2)}) %collective-permute-start.13) | collective-permute-done | bytes 589856 | tf_op jit(solution)/shard_map/ppermute | solution.py:402
  73.4 5.7 collective-permute-done.15
  87.0 20.1 %collective-permute-done.41 = bf16[288,2304]{1,0:T(8,128)(2,1)S(1)} collective-permute-done((bf16[288,2304]{1,0:T(8,128)(2,1)S(1)}, bf16[288,2304]{1,0:T(8,128)(2,1)S(1)}, u32[]{:S(2)}, u32[]{:S(2)}) %collective-permute-start.41) | collective-permute-done | bytes 1327136 | tf_op jit(solution)/shard_map/ppermute | solution.py:399
  114.2 18.2 %collective-permute-done.44 = bf16[288,2304]{1,0:T(8,128)(2,1)S(1)} collective-permute-done((bf16[288,2304]{1,0:T(8,128)(2,1)S(1)}, bf16[288,2304]{1,0:T(8,128)(2,1)S(1)}, u32[]{:S(2)}, u32[]{:S(2)}) %collective-permute-start.44) | collective-permute-done | bytes 1327136 | tf_op jit(solution)/shard_map/ppermute | solution.py:399
  136.6 6.9 project.1
  155.0 6.5 collective-permute-done.20
  171.6 10.5 %collective-permute-done.31 = bf16[4,72,512]{2,1,0:T(8,128)(2,1)S(1)} collective-permute-done((bf16[4,72,512]{2,1,0:T(8,128)(2,1)S(1)}, bf16[4,72,512]{2,1,0:T(8,128)(2,1)S(1)}, u32[]{:S(2)}, u32[]{:S(2)}) %collective-permute-start.31) | collective-permute-done | bytes 294944 | tf_op jit(solution)/shard_map/ppermute | solution.py:402
  190.7 5.9 collective-permute-done.23
  198.2 7.0 attend.1
  221.2 7.2 collective-permute-done.37
  239.7 5.6 constant_dynamic-update-slice_fusion.52
  261.5 5.6 collective-permute-done.49
  274.2 5.6 constant_dynamic-update-slice_fusion.50
  279.8 5.8 collective-permute-done.51
  292.4 6.0 constant_dynamic-update-slice_fusion.49
  298.5 6.4 fusion.169
  304.9 5.6 constant_dynamic-update-slice_fusion.48
  333.5 7.9 %collective-permute-done.57 = bf16[128,2304]{1,0:T(8,128)(2,1)S(1)} collective-permute-done((bf16[128,2304]{1,0:T(8,128)(2,1)S(1)}, bf16[128,2304]{1,0:T(8,128)(2,1)S(1)}, u32[]{:S(2)}, u32[]{:S(2)}) %collective-permute-start.57) | collective-permute-done | bytes 589856 | tf_op jit(solution)/shard_map/ppermute | solution.py:402
  348.4 7.8 %collective-permute-done.59 = bf16[128,2304]{1,0:T(8,128)(2,1)S(1)} collective-permute-done((bf16[128,2304]{1,0:T(8,128)(2,1)S(1)}, bf16[128,2304]{1,0:T(8,128)(2,1)S(1)}, u32[]{:S(2)}, u32[]{:S(2)}) %collective-permute-start.59) | collective-permute-done | bytes 589856 | tf_op jit(solution)/shard_map/ppermute | solution.py:402
  360.4 9.2 %collective-permute-done.61 = bf16[128,2304]{1,0:T(8,128)(2,1)} collective-permute-done((bf16[128,2304]{1,0:T(8,128)(2,1)}, bf16[128,2304]{1,0:T(8,128)(2,1)}, u32[]{:S(2)}, u32[]{:S(2)}) %collective-permute-start.61) | collective-permute-done | bytes 589856 | tf_op jit(solution)/shard_map/ppermute | solution.py:402
  485.8 9.2 %collective-permute-done.73 = bf16[128,2304]{1,0:T(8,128)(2,1)S(1)} collective-permute-done((bf16[128,2304]{1,0:T(8,128)(2,1)S(1)}, bf16[128,2304]{1,0:T(8,128)(2,1)S(1)}, u32[]{:S(2)}, u32[]{:S(2)}) %collective-permute-start.73) | collective-permute-done | bytes 589856 | tf_op jit(solution)/shard_map/ppermute | solution.py:402
  501.8 8.1 %collective-permute-done.75 = bf16[128,2304]{1,0:T(8,128)(2,1)S(1)} collective-permute-done((bf16[128,2304]{1,0:T(8,128)(2,1)S(1)}, bf16[128,2304]{1,0:T(8,128)(2,1)S(1)}, u32[]{:S(2)}, u32[]{:S(2)}) %collective-permute-start.75) | collective-permute-done | bytes 589856 | tf_op jit(solution)/shard_map/ppermute | solution.py:402
  516.4 6.7 collective-permute-done.77
  535.2 5.7 collective-permute-done.80
  586.6 7.2 attend_back.5
  610.5 9.1 %collective-permute-done.83 = bf16[512,512]{1,0:T(8,128)(2,1)S(1)} collective-permute-done((bf16[512,512]{1,0:T(8,128)(2,1)}, bf16[512,512]{1,0:T(8,128)(2,1)S(1)}, u32[]{:S(2)}, u32[]{:S(2)}) %collective-permute-start.83) | collective-permute-done | bytes 524320 | tf_op jit(solution)/shard_map/ppermute | solution.py:402
  621.0 10.7 %collective-permute-done.118 = bf16[288,2304]{1,0:T(8,128)(2,1)S(1)} collective-permute-done((bf16[288,2304]{1,0:T(8,128)(2,1)}, bf16[288,2304]{1,0:T(8,128)(2,1)S(1)}, u32[]{:S(2)}, u32[]{:S(2)}) %collective-permute-start.118) | collective-permute-done | bytes 1327136 | tf_op jit(solution)/shard_map/ppermute | solution.py:399
  637.2 9.4 %collective-permute-done.86 = bf16[512,512]{1,0:T(8,128)(2,1)S(1)} collective-permute-done((bf16[512,512]{1,0:T(8,128)(2,1)S(1)}, bf16[512,512]{1,0:T(8,128)(2,1)S(1)}, u32[]{:S(2)}, u32[]{:S(2)}) %collective-permute-start.86) | collective-permute-done | bytes 524320 | tf_op jit(solution)/shard_map/ppermute | solution.py:402
  677.9 11.0 %collective-permute-done.97 = bf16[4,72,1024]{2,1,0:T(8,128)(2,1)S(1)} collective-permute-done((bf16[4,72,1024]{2,1,0:T(8,128)(2,1)S(1)}, bf16[4,72,1024]{2,1,0:T(8,128)(2,1)S(1)}, u32[]{:S(2)}, u32[]{:S(2)}) %collective-permute-start.97) | collective-permute-done | bytes 589856 | tf_op jit(solution)/shard_map/ppermute | solution.py:402
  691.9 11.7 %collective-permute-done.100 = bf16[4,72,1024]{2,1,0:T(8,128)(2,1)S(1)} collective-permute-done((bf16[4,72,1024]{2,1,0:T(8,128)(2,1)S(1)}, bf16[4,72,1024]{2,1,0:T(8,128)(2,1)S(1)}, u32[]{:S(2)}, u32[]{:S(2)}) %collective-permute-start.100) | collective-permute-done | bytes 589856 | tf_op jit(solution)/shard_map/ppermute | solution.py:402
  708.7 9.3 %collective-permute-done.101 = bf16[4,72,1024]{2,1,0:T(8,128)(2,1)S(1)} collective-permute-done((bf16[4,72,1024]{2,1,0:T(8,128)(2,1)S(1)}, bf16[4,72,1024]{2,1,0:T(8,128)(2,1)S(1)}, u32[]{:S(2)}, u32[]{:S(2)}) %collective-permute-start.101) | collective-permute-done | bytes 589856 | tf_op jit(solution)/shard_map/ppermute | solution.py:402
  (637 shorter events, 456.8 us)
Async XLA Ops:
  2.7 28.3 %collective-permute-start = (bf16[72,1024]{1,0:T(8,128)(2,1)S(1)}, bf16[72,1024]{1,0:T(8,128)(2,1)S(1)}, u32[]{:S(2)}, u32[]{:S(2)}) collective-permute-start(bf16[72,1024]{1,0:T(8,128)(2,1)S(1)} %pad_maximum_fusion.7), channel_id=1, source_target_pairs={{0,8},{8,0},{16,24},{24,16},{1,9},{9,1},{17,25},{25,17},{2,10},{10... | collective-permute-start | bytes 442376 | tf_op jit(solution)/shard_map/ppermute | solution.py:399
  3.3 27.8 %collective-permute-start.1 = (bf16[72,1024]{1,0:T(8,128)(2,1)S(1)}, bf16[72,1024]{1,0:T(8,128)(2,1)S(1)}, u32[]{:S(2)}, u32[]{:S(2)}) collective-permute-start(bf16[72,1024]{1,0:T(8,128)(2,1)S(1)} %pad_maximum_fusion.8), channel_id=1, source_target_pairs={{0,16},{8,24},{16,0},{24,8},{1,17},{9,25},{17,1},{25,9},{2,18},{10... | collective-permute-start | bytes 442376 | tf_op jit(solution)/shard_map/ppermute | solution.py:399
  5.9 25.2 %collective-permute-start.2 = (bf16[72,1024]{1,0:T(8,128)(2,1)S(1)}, bf16[72,1024]{1,0:T(8,128)(2,1)S(1)}, u32[]{:S(2)}, u32[]{:S(2)}) collective-permute-start(bf16[72,1024]{1,0:T(8,128)(2,1)S(1)} %pad_maximum_fusion.9), channel_id=1, source_target_pairs={{0,24},{8,16},{16,8},{24,0},{1,25},{9,17},{17,9},{25,1},{2,26},{10... | collective-permute-start | bytes 442376 | tf_op jit(solution)/shard_map/ppermute | solution.py:399
  7.0 19.6 %collective-permute-start.24 = (bf16[72,512]{1,0:T(8,128)(2,1)S(1)}, bf16[72,512]{1,0:T(8,128)(2,1)S(1)}, u32[]{:S(2)}, u32[]{:S(2)}) collective-permute-start(bf16[72,512]{1,0:T(8,128)(2,1)S(1)} %get-tuple-element.245), channel_id=1, source_target_pairs={{0,8},{8,0},{16,24},{24,16},{1,9},{9,1},{17,25},{25,17},{2,10},{10... | collective-permute-start | bytes 221192 | tf_op jit(solution)/shard_map/ppermute | solution.py:399
  34.0 20.7 %collective-permute-start.3 = (bf16[128,2304]{1,0:T(8,128)(2,1)S(1)}, bf16[128,2304]{1,0:T(8,128)(2,1)S(1)}, u32[]{:S(2)}, u32[]{:S(2)}) collective-permute-start(bf16[128,2304]{1,0:T(8,128)(2,1)S(1)} %copy-done.2), channel_id=1, source_target_pairs={{0,8},{8,0},{16,24},{24,16},{1,9},{9,1},{17,25},{25,17},{2,10},{10... | collective-permute-start | bytes 1769480 | tf_op jit(solution)/shard_map/ppermute | solution.py:399
  46.7 37.9 %collective-permute-start.38 = (bf16[288,2304]{1,0:T(8,128)(2,1)S(1)}, bf16[288,2304]{1,0:T(8,128)(2,1)}, u32[]{:S(2)}, u32[]{:S(2)}) collective-permute-start(bf16[288,2304]{1,0:T(8,128)(2,1)S(1)} %copy-done.19), channel_id=1, source_target_pairs={{0,16},{8,24},{16,0},{24,8},{1,17},{9,25},{17,1},{25,9},{2,18},{10... | collective-permute-start | bytes 3981320 | tf_op jit(solution)/shard_map/ppermute | solution.py:399
  54.7 56.7 %collective-permute-start.39 = (bf16[288,2304]{1,0:T(8,128)(2,1)S(1)}, bf16[288,2304]{1,0:T(8,128)(2,1)S(1)}, u32[]{:S(2)}, u32[]{:S(2)}) collective-permute-start(bf16[288,2304]{1,0:T(8,128)(2,1)S(1)} %copy-done.19), channel_id=1, source_target_pairs={{0,8},{8,0},{16,24},{24,16},{1,9},{9,1},{17,25},{25,17},{2,10},{10... | collective-permute-start | bytes 3981320 | tf_op jit(solution)/shard_map/ppermute | solution.py:399
  63.1 44.0 %collective-permute-start.41 = (bf16[288,2304]{1,0:T(8,128)(2,1)S(1)}, bf16[288,2304]{1,0:T(8,128)(2,1)S(1)}, u32[]{:S(2)}, u32[]{:S(2)}) collective-permute-start(bf16[288,2304]{1,0:T(8,128)(2,1)S(1)} %copy-done.20), channel_id=1, source_target_pairs={{0,16},{8,24},{16,0},{24,8},{1,17},{9,25},{17,1},{25,9},{2,18},{10... | collective-permute-start | bytes 3981320 | tf_op jit(solution)/shard_map/ppermute | solution.py:399
  79.2 33.8 %collective-permute-start.42 = (bf16[288,2304]{1,0:T(8,128)(2,1)S(1)}, bf16[288,2304]{1,0:T(8,128)(2,1)S(1)}, u32[]{:S(2)}, u32[]{:S(2)}) collective-permute-start(bf16[288,2304]{1,0:T(8,128)(2,1)S(1)} %copy-done.20), channel_id=1, source_target_pairs={{0,8},{8,0},{16,24},{24,16},{1,9},{9,1},{17,25},{25,17},{2,10},{10... | collective-permute-start | bytes 3981320 | tf_op jit(solution)/shard_map/ppermute | solution.py:399
  81.5 50.8 %collective-permute-start.44 = (bf16[288,2304]{1,0:T(8,128)(2,1)S(1)}, bf16[288,2304]{1,0:T(8,128)(2,1)S(1)}, u32[]{:S(2)}, u32[]{:S(2)}) collective-permute-start(bf16[288,2304]{1,0:T(8,128)(2,1)S(1)} %copy-done.21), channel_id=1, source_target_pairs={{0,16},{8,24},{16,0},{24,8},{1,17},{9,25},{17,1},{25,9},{2,18},{10... | collective-permute-start | bytes 3981320 | tf_op jit(solution)/shard_map/ppermute | solution.py:399
  84.6 124.8 %collective-permute-start.45 = (bf16[288,2304]{1,0:T(8,128)(2,1)S(1)}, bf16[288,2304]{1,0:T(8,128)(2,1)}, u32[]{:S(2)}, u32[]{:S(2)}) collective-permute-start(bf16[288,2304]{1,0:T(8,128)(2,1)S(1)} %copy-done.21), channel_id=1, source_target_pairs={{0,8},{8,0},{16,24},{24,16},{1,9},{9,1},{17,25},{25,17},{2,10},{10... | collective-permute-start | bytes 3981320 | tf_op jit(solution)/shard_map/ppermute | solution.py:399
  107.1 26.5 %collective-permute-start.17 = (bf16[4,72,512]{2,1,0:T(8,128)(2,1)S(1)}, bf16[4,72,512]{2,1,0:T(8,128)(2,1)S(1)}, u32[]{:S(2)}, u32[]{:S(2)}) collective-permute-start(bf16[4,72,512]{2,1,0:T(8,128)(2,1)S(1)} %slice.290), channel_id=1, source_target_pairs={{0,2},{2,4},{4,6},{6,7},{7,5},{5,3},{3,1},{1,0},{8,10},{10,12},{12... | collective-permute-start | bytes 884744 | tf_op jit(solution)/shard_map/ppermute | solution.py:402
  111.4 22.3 %collective-permute-start.18 = (bf16[4,72,512]{2,1,0:T(8,128)(2,1)S(1)}, bf16[4,72,512]{2,1,0:T(8,128)(2,1)S(1)}, u32[]{:S(2)}, u32[]{:S(2)}) collective-permute-start(bf16[4,72,512]{2,1,0:T(8,128)(2,1)S(1)} %slice.291), channel_id=1, source_target_pairs={{2,0},{4,2},{6,4},{7,6},{5,7},{3,5},{1,3},{0,1},{10,8},{12,10},{14... | collective-permute-start | bytes 884744 | tf_op jit(solution)/shard_map/ppermute | solution.py:402
  143.6 17.9 %collective-permute-start.19 = (bf16[512,512]{1,0:T(8,128)(2,1)}, bf16[512,512]{1,0:T(8,128)(2,1)S(1)}, u32[]{:S(2)}, u32[]{:S(2)}) collective-permute-start(bf16[512,512]{1,0:T(8,128)(2,1)} %get-tuple-element.68), channel_id=1, source_target_pairs={{0,1},{2,3},{4,5},{6,7},{8,9},{10,11},{12,13},{14,15},{16,17},{18,... | collective-permute-start | bytes 1572872 | tf_op jit(solution)/shard_map/ppermute | solution.py:402
  161.4 29.1 %collective-permute-start.21 = (bf16[512,512]{1,0:T(8,128)(2,1)S(1)}, bf16[512,512]{1,0:T(8,128)(2,1)S(1)}, u32[]{:S(2)}, u32[]{:S(2)}) collective-permute-start(bf16[512,512]{1,0:T(8,128)(2,1)S(1)} %collective-permute-done.20), channel_id=1, source_target_pairs={{0,1},{2,3},{4,5},{6,7},{1,0},{3,2},{5,4},{7,6},{8,9},{10,11},{12,... | collective-permute-start | bytes 1572872 | tf_op jit(solution)/shard_map/ppermute | solution.py:402
  161.4 24.0 %collective-permute-start.22 = (bf16[512,512]{1,0:T(8,128)(2,1)S(1)}, bf16[512,512]{1,0:T(8,128)(2,1)S(1)}, u32[]{:S(2)}, u32[]{:S(2)}) collective-permute-start(bf16[512,512]{1,0:T(8,128)(2,1)S(1)} %collective-permute-done.20), channel_id=1, source_target_pairs={{0,2},{1,3},{2,4},{3,5},{4,6},{5,7},{8,10},{9,11},{10,12},{11,13},... | collective-permute-start | bytes 1572872 | tf_op jit(solution)/shard_map/ppermute | solution.py:402
  190.6 23.5 %collective-permute-start.40 = (bf16[288,2304]{1,0:T(8,128)(2,1)}, bf16[288,2304]{1,0:T(8,128)(2,1)}, u32[]{:S(2)}, u32[]{:S(2)}) collective-permute-start(bf16[288,2304]{1,0:T(8,128)(2,1)} %collective-permute-done.38), channel_id=1, source_target_pairs={{0,8},{8,0},{16,24},{24,16},{1,9},{9,1},{17,25},{25,17},{2,10},{10... | collective-permute-start | bytes 3981320 | tf_op jit(solution)/shard_map/ppermute | solution.py:399
  429.4 17.8 %collective-permute-start.69 = (bf16[64,2304]{1,0:T(8,128)(2,1)S(1)}, bf16[64,2304]{1,0:T(8,128)(2,1)S(1)}, u32[]{:S(2)}, u32[]{:S(2)}) collective-permute-start(bf16[64,2304]{1,0:T(8,128)(2,1)S(1)} %slice.310), channel_id=1, source_target_pairs={{0,2},{2,4},{4,6},{6,7},{7,5},{5,3},{3,1},{1,0},{8,10},{10,12},{12... | collective-permute-start | bytes 884744 | tf_op jit(solution)/shard_map/ppermute | solution.py:402
  453.9 87.1 %collective-permute-start.121 = (bf16[640,2304]{1,0:T(8,128)(2,1)}, bf16[640,2304]{1,0:T(8,128)(2,1)S(1)}, u32[]{:S(2)}, u32[]{:S(2)}) collective-permute-start(bf16[640,2304]{1,0:T(8,128)(2,1)} %convolution_convert_fusion), channel_id=1, source_target_pairs={{0,8},{8,0},{16,24},{24,16},{1,9},{9,1},{17,25},{25,17},{2,10},{10... | collective-permute-start | bytes 8847368 | tf_op jit(solution)/shard_map/ppermute | solution.py:399
  475.7 67.5 %collective-permute-start.119 = (bf16[640,2304]{1,0:T(8,128)(2,1)}, bf16[640,2304]{1,0:T(8,128)(2,1)S(1)}, u32[]{:S(2)}, u32[]{:S(2)}) collective-permute-start(bf16[640,2304]{1,0:T(8,128)(2,1)} %convolution_convert_fusion.2), channel_id=1, source_target_pairs={{0,8},{8,0},{16,24},{24,16},{1,9},{9,1},{17,25},{25,17},{2,10},{10... | collective-permute-start | bytes 8847368 | tf_op jit(solution)/shard_map/ppermute | solution.py:399
  516.3 33.6 %collective-permute-start.117 = (bf16[640,2304]{1,0:T(8,128)(2,1)S(1)}, bf16[640,2304]{1,0:T(8,128)(2,1)S(1)}, u32[]{:S(2)}, u32[]{:S(2)}) collective-permute-start(bf16[640,2304]{1,0:T(8,128)(2,1)S(1)} %convolution_convert_fusion.4), channel_id=1, source_target_pairs={{0,8},{8,0},{16,24},{24,16},{1,9},{9,1},{17,25},{25,17},{2,10},{10... | collective-permute-start | bytes 8847368 | tf_op jit(solution)/shard_map/ppermute | solution.py:399
  542.7 57.3 %collective-permute-start.122 = (bf16[288,2304]{1,0:T(8,128)(2,1)}, bf16[288,2304]{1,0:T(8,128)(2,1)}, u32[]{:S(2)}, u32[]{:S(2)}) collective-permute-start(bf16[288,2304]{1,0:T(8,128)(2,1)} %add_convert_fusion), channel_id=1, source_target_pairs={{0,16},{8,24},{16,0},{24,8},{1,17},{9,25},{17,1},{25,9},{2,18},{10... | collective-permute-start | bytes 3981320 | tf_op jit(solution)/shard_map/ppermute | solution.py:399
  544.8 61.9 %collective-permute-start.120 = (bf16[288,2304]{1,0:T(8,128)(2,1)}, bf16[288,2304]{1,0:T(8,128)(2,1)S(1)}, u32[]{:S(2)}, u32[]{:S(2)}) collective-permute-start(bf16[288,2304]{1,0:T(8,128)(2,1)} %add_convert_fusion.1), channel_id=1, source_target_pairs={{0,16},{8,24},{16,0},{24,8},{1,17},{9,25},{17,1},{25,9},{2,18},{10... | collective-permute-start | bytes 3981320 | tf_op jit(solution)/shard_map/ppermute | solution.py:399
  570.4 23.5 %collective-permute-start.84 = (bf16[512,512]{1,0:T(8,128)(2,1)}, bf16[512,512]{1,0:T(8,128)(2,1)}, u32[]{:S(2)}, u32[]{:S(2)}) collective-permute-start(bf16[512,512]{1,0:T(8,128)(2,1)} %get-tuple-element.102), channel_id=1, source_target_pairs={{0,1},{2,3},{4,5},{6,7},{8,9},{10,11},{12,13},{14,15},{16,17},{18,... | collective-permute-start | bytes 1572872 | tf_op jit(solution)/shard_map/ppermute | solution.py:402
  593.9 37.9 %collective-permute-start.118 = (bf16[288,2304]{1,0:T(8,128)(2,1)}, bf16[288,2304]{1,0:T(8,128)(2,1)S(1)}, u32[]{:S(2)}, u32[]{:S(2)}) collective-permute-start(bf16[288,2304]{1,0:T(8,128)(2,1)} %add_convert_fusion.2), channel_id=1, source_target_pairs={{0,16},{8,24},{16,0},{24,8},{1,17},{9,25},{17,1},{25,9},{2,18},{10... | collective-permute-start | bytes 3981320 | tf_op jit(solution)/shard_map/ppermute | solution.py:399
  595.9 41.3 %collective-permute-start.82 = (bf16[512,512]{1,0:T(8,128)(2,1)}, bf16[512,512]{1,0:T(8,128)(2,1)S(1)}, u32[]{:S(2)}, u32[]{:S(2)}) collective-permute-start(bf16[512,512]{1,0:T(8,128)(2,1)} %get-tuple-element.98), channel_id=1, source_target_pairs={{1,0},{3,2},{5,4},{7,6},{9,8},{11,10},{13,12},{15,14},{17,16},{19,... | collective-permute-start | bytes 1572872 | tf_op jit(solution)/shard_map/ppermute | solution.py:402
  597.2 22.4 %collective-permute-start.83 = (bf16[512,512]{1,0:T(8,128)(2,1)}, bf16[512,512]{1,0:T(8,128)(2,1)S(1)}, u32[]{:S(2)}, u32[]{:S(2)}) collective-permute-start(bf16[512,512]{1,0:T(8,128)(2,1)} %get-tuple-element.100), channel_id=1, source_target_pairs={{1,0},{3,2},{5,4},{7,6},{0,1},{2,3},{4,5},{6,7},{9,8},{11,10},{13,... | collective-permute-start | bytes 1572872 | tf_op jit(solution)/shard_map/ppermute | solution.py:402
  599.9 20.9 %collective-permute-start.85 = (bf16[512,512]{1,0:T(8,128)(2,1)S(1)}, bf16[512,512]{1,0:T(8,128)(2,1)S(1)}, u32[]{:S(2)}, u32[]{:S(2)}) collective-permute-start(bf16[512,512]{1,0:T(8,128)(2,1)S(1)} %add_convert_fusion.4), channel_id=1, source_target_pairs={{2,0},{3,1},{4,2},{5,3},{6,4},{7,5},{10,8},{11,9},{12,10},{13,11},... | collective-permute-start | bytes 1572872 | tf_op jit(solution)/shard_map/ppermute | solution.py:402
  606.7 30.4 %collective-permute-start.114 = (bf16[72,512]{1,0:T(8,128)(2,1)S(1)}, bf16[72,512]{1,0:T(8,128)(2,1)S(1)}, u32[]{:S(2)}, u32[]{:S(2)}) collective-permute-start(bf16[72,512]{1,0:T(8,128)(2,1)S(1)} %get-tuple-element.241), channel_id=1, source_target_pairs={{0,8},{8,0},{16,24},{24,16},{1,9},{9,1},{17,25},{25,17},{2,10},{10... | collective-permute-start | bytes 221192 | tf_op jit(solution)/shard_map/ppermute | solution.py:399
  619.6 46.3 %collective-permute-start.115 = (bf16[72,512]{1,0:T(8,128)(2,1)S(1)}, bf16[72,512]{1,0:T(8,128)(2,1)S(1)}, u32[]{:S(2)}, u32[]{:S(2)}) collective-permute-start(bf16[72,512]{1,0:T(8,128)(2,1)S(1)} %get-tuple-element.240), channel_id=1, source_target_pairs={{0,16},{8,24},{16,0},{24,8},{1,17},{9,25},{17,1},{25,9},{2,18},{10... | collective-permute-start | bytes 221192 | tf_op jit(solution)/shard_map/ppermute | solution.py:399
  620.8 50.6 %collective-permute-start.116 = (bf16[72,512]{1,0:T(8,128)(2,1)S(1)}, bf16[72,512]{1,0:T(8,128)(2,1)S(1)}, u32[]{:S(2)}, u32[]{:S(2)}) collective-permute-start(bf16[72,512]{1,0:T(8,128)(2,1)S(1)} %get-tuple-element.239), channel_id=1, source_target_pairs={{0,24},{8,16},{16,8},{24,0},{1,25},{9,17},{17,9},{25,1},{2,26},{10... | collective-permute-start | bytes 221192 | tf_op jit(solution)/shard_map/ppermute | solution.py:399
  671.5 19.9 %collective-permute-start.87 = (bf16[128,2304]{1,0:T(8,128)(2,1)S(1)}, bf16[128,2304]{1,0:T(8,128)(2,1)S(1)}, u32[]{:S(2)}, u32[]{:S(2)}) collective-permute-start(bf16[128,2304]{1,0:T(8,128)(2,1)S(1)} %get-tuple-element.190), channel_id=1, source_target_pairs={{0,8},{8,0},{16,24},{24,16},{1,9},{9,1},{17,25},{25,17},{2,10},{10... | collective-permute-start | bytes 1769480 | tf_op jit(solution)/shard_map/ppermute | solution.py:399
  (170 other events, 1887.3 us)

commit v3 on v2

--- a/solution.py
+++ b/solution.py
@@ -448,13 +448,13 @@
         return parts[0] + near + across
 
     def sum_all(value):
+        bits = seq_count // 2
+        while bits:
+            value = value + flip(value, bits)
+            bits //= 2
         bits = 1
         while bits < count:
             value = value + hop(value, [(i, i ^ bits) for i in range(count)])
-            bits *= 2
-        bits = 1
-        while bits < seq_count:
-            value = value + flip(value, bits)
             bits *= 2
         return value
 
@@ -477,9 +477,7 @@
         )
 
     def exchange(pick):
-        pieces = [pick(seq_rank)] + [
-            flip(pick(seq_rank ^ j), j) for j in range(1, seq_count)
-        ]
+        pieces = [pick(seq_rank)] + [flip(pick(seq_rank ^ j), j) for j in range(1, seq_count)]
         chunk = jnp.zeros((seq_count,) + pieces[0].shape, bf16)
         for j, piece in enumerate(pieces):
             chunk = lax.dynamic_update_slice(chunk, piece[None], (seq_rank ^ j, 0, 0))
@@ -570,10 +568,11 @@
     blank = jnp.zeros((-2 * gate_weight.shape[0] % 128, width), bf16)
 
     def unit_rows(weight):
-        weight = after(weight, rows_in[2])
         across = flip(weight, 2)
         beside = flip(weight, 1)
         both = flip(after(across, line[reach]), 1)
+        weight, beside = after(weight, rows_in[2]), after(beside, rows_in[2])
+        across = after(across, side[1])
         return jnp.concatenate([weight, across, blank, beside, both, blank], axis=0)
 
     gate_units, up_units, down_units = (
@@ -697,10 +696,13 @@
             None if k else (head_cos, head_sin),
             2 * k,
         )
-        here = line_part.astype(jnp.float32) + hop(side_part, sideways(k, True)).astype(jnp.float32)
-        if total is not None:
-            here = here + hop(total.astype(bf16), down_line).astype(jnp.float32)
-        total = here
+        side_sum = hop(side_part, sideways(k, True))
+        line_sum = None if total is None else hop(total, down_line)
+        total = line_part.astype(jnp.float32) + side_sum.astype(jnp.float32)
+        if line_sum is not None:
+            total = total + line_sum.astype(jnp.float32)
+        if k:
+            total = total.astype(bf16)
     query_back = carry
     key_back = rope_apply(total[:, :key_cols], head_cos, head_sin, True).astype(bf16)
     value_back = total[:, key_cols:].astype(bf16)
@@ -720,7 +722,19 @@
     input_grad = middle_grad + input_part
 
     gain_parts = jnp.stack([first_part, second_part, third_part, fourth_part])
-    gain_grads = lax.dynamic_slice_in_dim(sum_all(gain_parts), own_start, own_rows, 1)
+    gain_parts = gain_parts.reshape(4, seq_count, count, own_rows)
+    gain_sums = gain_parts
+    bits = 1
+    while bits < count:
+        pairs = [(i, i ^ bits) for i in range(count)]
+        gain_sums = gain_sums + hop(gain_sums, pairs)
+        bits *= 2
+    gain_sums = lax.dynamic_slice_in_dim(gain_sums, fsdp_rank, 1, 2)[:, :, 0]
+    gain_grads = None
+    for j in range(seq_count):
+        piece = lax.dynamic_slice_in_dim(gain_sums, seq_rank ^ j, 1, 1)[:, 0]
+        piece = flip(piece, j) if j else piece
+        gain_grads = piece if gain_grads is None else gain_grads + piece
     return (
         layer_out,
         input_grad,

time: 739 us -> 779 us (1.054)
  other arithmetic: 46 us -> 62 us
  local copies, waits for them, and re-layouts: 55.2 us -> 68.8 us
  matrix products: 183 us -> 195 us
    ppermute x43 -> x44, waiting for transfers between devices: 80.8 us -> 55.6 us  [flip(): return lax.ppermute(value, 'seq', [(i, i ^ bits) for i in range(seq_count)])]
    ppermute x80, waiting for transfers between devices: 202 us -> 227 us  [hop(): return lax.ppermute(value, 'fsdp', pairs)]
    unnamed x193 -> x197, local copies, waits for them, and re-layouts: 27.5 us -> 38.3 us
    dot_general x8, matrix products: 27.5 us -> 36 us  [contract_rows(): lax.dot_general(left, right, (((0,), (0,)), ((), ())), preferred_element_...]
    ppermute x43 -> x44, starting transfers between devices: 22.7 us -> 19.8 us  [flip(): return lax.ppermute(value, 'seq', [(i, i ^ bits) for i in range(seq_count)])]
  transfers between devices with their start and end apart: 123 -> 124, of which waited for: 62 -> 63; matrix products, arithmetic and copies ran while one was open for 30% -> 33% of each run, Pallas kernels for 4% -> 4%
where the time goes in v3:
time: 779 us; the launch traced here: 768 us
  waiting for transfers between devices  283 us (36%)
  matrix products  195 us (25%)
  starting transfers between devices  126 us (16%)
  local copies, waits for them, and re-layouts  68.8 us (9%)
  other arithmetic  62 us (8%)
  Pallas kernels  30 us (4%)
    ppermute x80, waiting for transfers between devices, hop(): return lax.ppermute(value, 'fsdp', pairs)  227 us
    ppermute x80, starting transfers between devices, hop(): return lax.ppermute(value, 'fsdp', pairs)  106 us
    dot_general x17, matrix products, contract_cols(): lax.dot_general(left, right, (((1,), (1,)), ((), ())), preferred_element_...  91.6 us
    ppermute x44, waiting for transfers between devices, flip(): return lax.ppermute(value, 'seq', [(i, i ^ bits) for i in range(seq_count)])  55.6 us
    unnamed x197, local copies, waits for them, and re-layouts  38.3 us
    dot_general x8, matrix products, contract_rows(): lax.dot_general(left, right, (((0,), (0,)), ((), ())), preferred_element_...  36 us
    dot_general x5, matrix products, layer(): jnp.dot(hidden, down_units, preferred_element_type=jnp.float32)  21.7 us
    dot_general x5, matrix products, layer(): jnp.dot(gate_delta, gate_units, preferred_element_type=jnp.float32)  21.4 us
  transfers between devices with their start and end apart: 124, of which 63 were waited for; matrix products, arithmetic and copies ran while one was open for 33% of the time, Pallas kernels for 4%

profile of v3, /device:TPU:0, one launch (start us, length us, event | category | flops | bytes accessed | tf_op | source)
XLA Modules:
  0.0 768.1 jit_solution(7961653528743046201)
XLA Ops:
  45.8 7.1 collective-permute-done.4
  59.0 8.1 %collective-permute-done.12 = bf16[4,72,1024]{2,1,0:T(8,128)(2,1)S(1)} collective-permute-done((bf16[4,72,1024]{2,1,0:T(8,128)(2,1)S(1)}, bf16[4,72,1024]{2,1,0:T(8,128)(2,1)S(1)}, u32[]{:S(2)}, u32[]{:S(2)}) %collective-permute-start.12) | collective-permute-done | bytes 589856 | tf_op jit(solution)/shard_map/ppermute | solution.py:402
  71.8 8.6 %collective-permute-done.13 = bf16[4,72,1024]{2,1,0:T(8,128)(2,1)S(1)} collective-permute-done((bf16[4,72,1024]{2,1,0:T(8,128)(2,1)S(1)}, bf16[4,72,1024]{2,1,0:T(8,128)(2,1)S(1)}, u32[]{:S(2)}, u32[]{:S(2)}) %collective-permute-start.13) | collective-permute-done | bytes 589856 | tf_op jit(solution)/shard_map/ppermute | solution.py:402
  94.6 5.8 collective-permute-done.16
  111.3 6.9 project.1
  127.6 5.7 collective-permute-done.19
  142.7 7.5 collective-permute-done.31
  153.6 7.8 %collective-permute-done.33 = bf16[4,72,256]{2,1,0:T(8,128)(2,1)S(1)} collective-permute-done((bf16[4,72,256]{2,1,0:T(8,128)(2,1)S(1)}, bf16[4,72,256]{2,1,0:T(8,128)(2,1)S(1)}, u32[]{:S(2)}, u32[]{:S(2)}) %collective-permute-start.33) | collective-permute-done | bytes 147488 | tf_op jit(solution)/shard_map/ppermute | solution.py:402
  176.0 17.2 %collective-permute-done.44 = bf16[288,2304]{1,0:T(8,128)(2,1)} collective-permute-done((bf16[288,2304]{1,0:T(8,128)(2,1)S(1)}, bf16[288,2304]{1,0:T(8,128)(2,1)}, u32[]{:S(2)}, u32[]{:S(2)}) %collective-permute-start.44) | collective-permute-done | bytes 1327136 | tf_op jit(solution)/shard_map/ppermute | solution.py:399
  199.4 12.4 %collective-permute-done.23 = bf16[512,512]{1,0:T(8,128)(2,1)S(1)} collective-permute-done((bf16[512,512]{1,0:T(8,128)(2,1)S(1)}, bf16[512,512]{1,0:T(8,128)(2,1)S(1)}, u32[]{:S(2)}, u32[]{:S(2)}) %collective-permute-start.23) | collective-permute-done | bytes 524320 | tf_op jit(solution)/shard_map/ppermute | solution.py:402
  213.5 7.0 attend.1
  235.8 5.7 collective-permute-done.37
  243.6 9.6 %collective-permute-start.47 = (bf16[128,2304]{1,0:T(8,128)(2,1)S(1)}, bf16[128,2304]{1,0:T(8,128)(2,1)S(1)}, u32[]{:S(2)}, u32[]{:S(2)}) collective-permute-start(bf16[128,2304]{1,0:T(8,128)(2,1)S(1)} %get-tuple-element.176), channel_id=1, source_target_pairs={{0,2},{2,4},{4,6},{6,7},{7,5},{5,3},{3,1},{1,0},{8,10},{10,12},{12... | collective-permute-start | bytes 1769480 | tf_op jit(solution)/shard_map/ppermute | solution.py:402
  280.1 6.0 collective-permute-done.49
  299.7 5.9 collective-permute-done.51
  312.3 6.0 constant_dynamic-update-slice_fusion.49
  318.5 6.4 fusion.175
  352.7 6.8 collective-permute-done.57
  366.5 6.9 collective-permute-done.59
  377.1 8.2 %collective-permute-done.61 = bf16[128,2304]{1,0:T(8,128)(2,1)} collective-permute-done((bf16[128,2304]{1,0:T(8,128)(2,1)}, bf16[128,2304]{1,0:T(8,128)(2,1)}, u32[]{:S(2)}, u32[]{:S(2)}) %collective-permute-start.61) | collective-permute-done | bytes 589856 | tf_op jit(solution)/shard_map/ppermute | solution.py:402
  394.8 5.9 constant_dynamic-update-slice_fusion.33
  404.8 6.8 constant_dynamic-update-slice_fusion.32
  499.6 7.8 %collective-permute-done.73 = bf16[128,2304]{1,0:T(8,128)(2,1)S(1)} collective-permute-done((bf16[128,2304]{1,0:T(8,128)(2,1)S(1)}, bf16[128,2304]{1,0:T(8,128)(2,1)S(1)}, u32[]{:S(2)}, u32[]{:S(2)}) %collective-permute-start.73) | collective-permute-done | bytes 589856 | tf_op jit(solution)/shard_map/ppermute | solution.py:402
  516.5 6.6 collective-permute-done.75
  600.1 7.2 attend_back.5
  618.7 10.8 %collective-permute-done.113 = bf16[4,72,512]{2,1,0:T(8,128)(2,1)S(1)} collective-permute-done((bf16[4,72,512]{2,1,0:T(8,128)(2,1)S(1)}, bf16[4,72,512]{2,1,0:T(8,128)(2,1)S(1)}, u32[]{:S(2)}, u32[]{:S(2)}) %collective-permute-start.113) | collective-permute-done | bytes 294944 | tf_op jit(solution)/shard_map/ppermute | solution.py:402
  636.4 11.6 %collective-permute-done.119 = bf16[288,2304]{1,0:T(8,128)(2,1)S(1)} collective-permute-done((bf16[288,2304]{1,0:T(8,128)(2,1)}, bf16[288,2304]{1,0:T(8,128)(2,1)S(1)}, u32[]{:S(2)}, u32[]{:S(2)}) %collective-permute-start.119) | collective-permute-done | bytes 1327136 | tf_op jit(solution)/shard_map/ppermute | solution.py:399
  654.7 14.8 %collective-permute-done.86 = bf16[512,512]{1,0:T(8,128)(2,1)S(1)} collective-permute-done((bf16[512,512]{1,0:T(8,128)(2,1)S(1)}, bf16[512,512]{1,0:T(8,128)(2,1)S(1)}, u32[]{:S(2)}, u32[]{:S(2)}) %collective-permute-start.86) | collective-permute-done | bytes 524320 | tf_op jit(solution)/shard_map/ppermute | solution.py:402
  677.7 9.3 %fusion.4 = (f32[2304]{0:T(1024)}, bf16[512,2304]{1,0:T(8,128)(2,1)}, f32[512,2304]{1,0:T(8,128)}) fusion(f32[512]{0:T(512)S(1)} %copy-done.53, bf16[128,2304]{1,0:T(8,128)(2,1)S(1)} %copy-done.16, bf16[128,2304]{1,0:T(8,128)(2,1)S(1)} %copy-done.12, bf16[128,2304]{1,0:T(8,128)(2,1)S(1)} %copy-done.14, bf16[128,2304]{1,0:T(8,128)(2,1)S(1)} %copy-done.3, ...), kind=kOutput, calls=%fused_computation.14 | convolution fusion | flops 2433218304 | bytes 15215616 | tf_op jit(solution)/shard_map/dot_general | solution.py:77
  715.0 11.2 %collective-permute-done.98 = bf16[4,72,1024]{2,1,0:T(8,128)(2,1)S(1)} collective-permute-done((bf16[4,72,1024]{2,1,0:T(8,128)(2,1)S(1)}, bf16[4,72,1024]{2,1,0:T(8,128)(2,1)S(1)}, u32[]{:S(2)}, u32[]{:S(2)}) %collective-permute-start.98) | collective-permute-done | bytes 589856 | tf_op jit(solution)/shard_map/ppermute | solution.py:402
  730.3 11.2 %collective-permute-done.100 = bf16[4,72,1024]{2,1,0:T(8,128)(2,1)S(1)} collective-permute-done((bf16[4,72,1024]{2,1,0:T(8,128)(2,1)S(1)}, bf16[4,72,1024]{2,1,0:T(8,128)(2,1)S(1)}, u32[]{:S(2)}, u32[]{:S(2)}) %collective-permute-start.100) | collective-permute-done | bytes 589856 | tf_op jit(solution)/shard_map/ppermute | solution.py:402
  745.8 10.0 %collective-permute-done.102 = bf16[4,72,1024]{2,1,0:T(8,128)(2,1)S(1)} collective-permute-done((bf16[4,72,1024]{2,1,0:T(8,128)(2,1)S(1)}, bf16[4,72,1024]{2,1,0:T(8,128)(2,1)S(1)}, u32[]{:S(2)}, u32[]{:S(2)}) %collective-permute-start.102) | collective-permute-done | bytes 589856 | tf_op jit(solution)/shard_map/ppermute | solution.py:402
  (644 shorter events, 495.8 us)
Async XLA Ops:
  3.4 29.9 %collective-permute-start = (bf16[72,1024]{1,0:T(8,128)(2,1)}, bf16[72,1024]{1,0:T(8,128)(2,1)}, u32[]{:S(2)}, u32[]{:S(2)}) collective-permute-start(bf16[72,1024]{1,0:T(8,128)(2,1)} %pad_maximum_fusion.7), channel_id=1, source_target_pairs={{0,8},{8,0},{16,24},{24,16},{1,9},{9,1},{17,25},{25,17},{2,10},{10... | collective-permute-start | bytes 442376 | tf_op jit(solution)/shard_map/ppermute | solution.py:399
  3.9 30.5 %collective-permute-start.1 = (bf16[72,1024]{1,0:T(8,128)(2,1)S(1)}, bf16[72,1024]{1,0:T(8,128)(2,1)S(1)}, u32[]{:S(2)}, u32[]{:S(2)}) collective-permute-start(bf16[72,1024]{1,0:T(8,128)(2,1)S(1)} %pad_maximum_fusion.8), channel_id=1, source_target_pairs={{0,16},{8,24},{16,0},{24,8},{1,17},{9,25},{17,1},{25,9},{2,18},{10... | collective-permute-start | bytes 442376 | tf_op jit(solution)/shard_map/ppermute | solution.py:399
  6.5 28.5 %collective-permute-start.2 = (bf16[72,1024]{1,0:T(8,128)(2,1)S(1)}, bf16[72,1024]{1,0:T(8,128)(2,1)S(1)}, u32[]{:S(2)}, u32[]{:S(2)}) collective-permute-start(bf16[72,1024]{1,0:T(8,128)(2,1)S(1)} %pad_maximum_fusion.9), channel_id=1, source_target_pairs={{0,24},{8,16},{16,8},{24,0},{1,25},{9,17},{17,9},{25,1},{2,26},{10... | collective-permute-start | bytes 442376 | tf_op jit(solution)/shard_map/ppermute | solution.py:399
  8.3 19.3 %collective-permute-start.24 = (bf16[72,512]{1,0:T(8,128)(2,1)}, bf16[72,512]{1,0:T(8,128)(2,1)}, u32[]{:S(2)}, u32[]{:S(2)}) collective-permute-start(bf16[72,512]{1,0:T(8,128)(2,1)} %get-tuple-element.257), channel_id=1, source_target_pairs={{0,8},{8,0},{16,24},{24,16},{1,9},{9,1},{17,25},{25,17},{2,10},{10... | collective-permute-start | bytes 221192 | tf_op jit(solution)/shard_map/ppermute | solution.py:399
  31.8 36.8 %collective-permute-start.39 = (bf16[288,2304]{1,0:T(8,128)(2,1)}, bf16[288,2304]{1,0:T(8,128)(2,1)S(1)}, u32[]{:S(2)}, u32[]{:S(2)}) collective-permute-start(bf16[288,2304]{1,0:T(8,128)(2,1)} %param.25), channel_id=1, source_target_pairs={{0,8},{8,0},{16,24},{24,16},{1,9},{9,1},{17,25},{25,17},{2,10},{10... | collective-permute-start | bytes 3981320 | tf_op jit(solution)/shard_map/ppermute | solution.py:399
  33.3 36.6 %collective-permute-start.42 = (bf16[288,2304]{1,0:T(8,128)(2,1)S(1)}, bf16[288,2304]{1,0:T(8,128)(2,1)S(1)}, u32[]{:S(2)}, u32[]{:S(2)}) collective-permute-start(bf16[288,2304]{1,0:T(8,128)(2,1)S(1)} %copy-done.18), channel_id=1, source_target_pairs={{0,8},{8,0},{16,24},{24,16},{1,9},{9,1},{17,25},{25,17},{2,10},{10... | collective-permute-start | bytes 3981320 | tf_op jit(solution)/shard_map/ppermute | solution.py:399
  34.4 36.8 %collective-permute-start.45 = (bf16[288,2304]{1,0:T(8,128)(2,1)}, bf16[288,2304]{1,0:T(8,128)(2,1)S(1)}, u32[]{:S(2)}, u32[]{:S(2)}) collective-permute-start(bf16[288,2304]{1,0:T(8,128)(2,1)} %param.27), channel_id=1, source_target_pairs={{0,8},{8,0},{16,24},{24,16},{1,9},{9,1},{17,25},{25,17},{2,10},{10... | collective-permute-start | bytes 3981320 | tf_op jit(solution)/shard_map/ppermute | solution.py:399
  56.9 25.1 %collective-permute-start.3 = (bf16[128,2304]{1,0:T(8,128)(2,1)S(1)}, bf16[128,2304]{1,0:T(8,128)(2,1)S(1)}, u32[]{:S(2)}, u32[]{:S(2)}) collective-permute-start(bf16[128,2304]{1,0:T(8,128)(2,1)S(1)} %copy-done.2), channel_id=1, source_target_pairs={{0,8},{8,0},{16,24},{24,16},{1,9},{9,1},{17,25},{25,17},{2,10},{10... | collective-permute-start | bytes 1769480 | tf_op jit(solution)/shard_map/ppermute | solution.py:399
  71.2 97.0 %collective-permute-start.38 = (bf16[288,2304]{1,0:T(8,128)(2,1)}, bf16[288,2304]{1,0:T(8,128)(2,1)}, u32[]{:S(2)}, u32[]{:S(2)}) collective-permute-start(bf16[288,2304]{1,0:T(8,128)(2,1)} %param.25), channel_id=1, source_target_pairs={{0,16},{8,24},{16,0},{24,8},{1,17},{9,25},{17,1},{25,9},{2,18},{10... | collective-permute-start | bytes 3981320 | tf_op jit(solution)/shard_map/ppermute | solution.py:399
  133.3 35.0 %collective-permute-start.41 = (bf16[288,2304]{1,0:T(8,128)(2,1)S(1)}, bf16[288,2304]{1,0:T(8,128)(2,1)}, u32[]{:S(2)}, u32[]{:S(2)}) collective-permute-start(bf16[288,2304]{1,0:T(8,128)(2,1)S(1)} %copy-done.19), channel_id=1, source_target_pairs={{0,16},{8,24},{16,0},{24,8},{1,17},{9,25},{17,1},{25,9},{2,18},{10... | collective-permute-start | bytes 3981320 | tf_op jit(solution)/shard_map/ppermute | solution.py:399
  136.1 32.1 %collective-permute-start.21 = (bf16[512,512]{1,0:T(8,128)(2,1)S(1)}, bf16[512,512]{1,0:T(8,128)(2,1)S(1)}, u32[]{:S(2)}, u32[]{:S(2)}) collective-permute-start(bf16[512,512]{1,0:T(8,128)(2,1)S(1)} %collective-permute-done.20), channel_id=1, source_target_pairs={{0,1},{2,3},{4,5},{6,7},{1,0},{3,2},{5,4},{7,6},{8,9},{10,11},{12,... | collective-permute-start | bytes 1572872 | tf_op jit(solution)/shard_map/ppermute | solution.py:402
  150.2 18.0 %collective-permute-start.22 = (bf16[512,512]{1,0:T(8,128)(2,1)S(1)}, bf16[512,512]{1,0:T(8,128)(2,1)S(1)}, u32[]{:S(2)}, u32[]{:S(2)}) collective-permute-start(bf16[512,512]{1,0:T(8,128)(2,1)S(1)} %collective-permute-done.20), channel_id=1, source_target_pairs={{0,2},{1,3},{2,4},{3,5},{4,6},{5,7},{8,10},{9,11},{10,12},{11,13},... | collective-permute-start | bytes 1572872 | tf_op jit(solution)/shard_map/ppermute | solution.py:402
  167.5 25.7 %collective-permute-start.44 = (bf16[288,2304]{1,0:T(8,128)(2,1)S(1)}, bf16[288,2304]{1,0:T(8,128)(2,1)}, u32[]{:S(2)}, u32[]{:S(2)}) collective-permute-start(bf16[288,2304]{1,0:T(8,128)(2,1)S(1)} %copy-done.21), channel_id=1, source_target_pairs={{0,16},{8,24},{16,0},{24,8},{1,17},{9,25},{17,1},{25,9},{2,18},{10... | collective-permute-start | bytes 3981320 | tf_op jit(solution)/shard_map/ppermute | solution.py:399
  168.2 57.8 %collective-permute-start.40 = (bf16[288,2304]{1,0:T(8,128)(2,1)}, bf16[288,2304]{1,0:T(8,128)(2,1)}, u32[]{:S(2)}, u32[]{:S(2)}) collective-permute-start(bf16[288,2304]{1,0:T(8,128)(2,1)} %collective-permute-done.38), channel_id=1, source_target_pairs={{0,8},{8,0},{16,24},{24,16},{1,9},{9,1},{17,25},{25,17},{2,10},{10... | collective-permute-start | bytes 3981320 | tf_op jit(solution)/shard_map/ppermute | solution.py:399
  168.3 61.0 %collective-permute-start.43 = (bf16[288,2304]{1,0:T(8,128)(2,1)}, bf16[288,2304]{1,0:T(8,128)(2,1)}, u32[]{:S(2)}, u32[]{:S(2)}) collective-permute-start(bf16[288,2304]{1,0:T(8,128)(2,1)} %collective-permute-done.41), channel_id=1, source_target_pairs={{0,8},{8,0},{16,24},{24,16},{1,9},{9,1},{17,25},{25,17},{2,10},{10... | collective-permute-start | bytes 3981320 | tf_op jit(solution)/shard_map/ppermute | solution.py:399
  193.2 38.6 %collective-permute-start.46 = (bf16[288,2304]{1,0:T(8,128)(2,1)}, bf16[288,2304]{1,0:T(8,128)(2,1)}, u32[]{:S(2)}, u32[]{:S(2)}) collective-permute-start(bf16[288,2304]{1,0:T(8,128)(2,1)} %collective-permute-done.44), channel_id=1, source_target_pairs={{0,8},{8,0},{16,24},{24,16},{1,9},{9,1},{17,25},{25,17},{2,10},{10... | collective-permute-start | bytes 3981320 | tf_op jit(solution)/shard_map/ppermute | solution.py:399
  243.6 22.0 %collective-permute-start.47 = (bf16[128,2304]{1,0:T(8,128)(2,1)S(1)}, bf16[128,2304]{1,0:T(8,128)(2,1)S(1)}, u32[]{:S(2)}, u32[]{:S(2)}) collective-permute-start(bf16[128,2304]{1,0:T(8,128)(2,1)S(1)} %get-tuple-element.176), channel_id=1, source_target_pairs={{0,2},{2,4},{4,6},{6,7},{7,5},{5,3},{3,1},{1,0},{8,10},{10,12},{12... | collective-permute-start | bytes 1769480 | tf_op jit(solution)/shard_map/ppermute | solution.py:402
  468.8 87.5 %collective-permute-start.122 = (bf16[640,2304]{1,0:T(8,128)(2,1)}, bf16[640,2304]{1,0:T(8,128)(2,1)}, u32[]{:S(2)}, u32[]{:S(2)}) collective-permute-start(bf16[640,2304]{1,0:T(8,128)(2,1)} %convolution_convert_fusion), channel_id=1, source_target_pairs={{0,8},{8,0},{16,24},{24,16},{1,9},{9,1},{17,25},{25,17},{2,10},{10... | collective-permute-start | bytes 8847368 | tf_op jit(solution)/shard_map/ppermute | solution.py:399
  488.6 71.1 %collective-permute-start.120 = (bf16[640,2304]{1,0:T(8,128)(2,1)}, bf16[640,2304]{1,0:T(8,128)(2,1)}, u32[]{:S(2)}, u32[]{:S(2)}) collective-permute-start(bf16[640,2304]{1,0:T(8,128)(2,1)} %convolution_convert_fusion.2), channel_id=1, source_target_pairs={{0,8},{8,0},{16,24},{24,16},{1,9},{9,1},{17,25},{25,17},{2,10},{10... | collective-permute-start | bytes 8847368 | tf_op jit(solution)/shard_map/ppermute | solution.py:399
  532.1 32.3 %collective-permute-start.118 = (bf16[640,2304]{1,0:T(8,128)(2,1)}, bf16[640,2304]{1,0:T(8,128)(2,1)}, u32[]{:S(2)}, u32[]{:S(2)}) collective-permute-start(bf16[640,2304]{1,0:T(8,128)(2,1)} %convolution_convert_fusion.4), channel_id=1, source_target_pairs={{0,8},{8,0},{16,24},{24,16},{1,9},{9,1},{17,25},{25,17},{2,10},{10... | collective-permute-start | bytes 8847368 | tf_op jit(solution)/shard_map/ppermute | solution.py:399
  559.3 54.6 %collective-permute-start.123 = (bf16[288,2304]{1,0:T(8,128)(2,1)}, bf16[288,2304]{1,0:T(8,128)(2,1)}, u32[]{:S(2)}, u32[]{:S(2)}) collective-permute-start(bf16[288,2304]{1,0:T(8,128)(2,1)} %add_convert_fusion), channel_id=1, source_target_pairs={{0,16},{8,24},{16,0},{24,8},{1,17},{9,25},{17,1},{25,9},{2,18},{10... | collective-permute-start | bytes 3981320 | tf_op jit(solution)/shard_map/ppermute | solution.py:399
  562.7 70.0 %collective-permute-start.121 = (bf16[288,2304]{1,0:T(8,128)(2,1)}, bf16[288,2304]{1,0:T(8,128)(2,1)S(1)}, u32[]{:S(2)}, u32[]{:S(2)}) collective-permute-start(bf16[288,2304]{1,0:T(8,128)(2,1)} %add_convert_fusion.1), channel_id=1, source_target_pairs={{0,16},{8,24},{16,0},{24,8},{1,17},{9,25},{17,1},{25,9},{2,18},{10... | collective-permute-start | bytes 3981320 | tf_op jit(solution)/shard_map/ppermute | solution.py:399
  583.6 23.8 %collective-permute-start.84 = (bf16[512,512]{1,0:T(8,128)(2,1)}, bf16[512,512]{1,0:T(8,128)(2,1)}, u32[]{:S(2)}, u32[]{:S(2)}) collective-permute-start(bf16[512,512]{1,0:T(8,128)(2,1)} %get-tuple-element.114), channel_id=1, source_target_pairs={{0,1},{2,3},{4,5},{6,7},{8,9},{10,11},{12,13},{14,15},{16,17},{18,... | collective-permute-start | bytes 1572872 | tf_op jit(solution)/shard_map/ppermute | solution.py:402
  607.4 40.6 %collective-permute-start.119 = (bf16[288,2304]{1,0:T(8,128)(2,1)}, bf16[288,2304]{1,0:T(8,128)(2,1)S(1)}, u32[]{:S(2)}, u32[]{:S(2)}) collective-permute-start(bf16[288,2304]{1,0:T(8,128)(2,1)} %add_convert_fusion.2), channel_id=1, source_target_pairs={{0,16},{8,24},{16,0},{24,8},{1,17},{9,25},{17,1},{25,9},{2,18},{10... | collective-permute-start | bytes 3981320 | tf_op jit(solution)/shard_map/ppermute | solution.py:399
  609.0 45.7 %collective-permute-start.82 = (bf16[512,512]{1,0:T(8,128)(2,1)}, bf16[512,512]{1,0:T(8,128)(2,1)S(1)}, u32[]{:S(2)}, u32[]{:S(2)}) collective-permute-start(bf16[512,512]{1,0:T(8,128)(2,1)} %get-tuple-element.110), channel_id=1, source_target_pairs={{1,0},{3,2},{5,4},{7,6},{9,8},{11,10},{13,12},{15,14},{17,16},{19,... | collective-permute-start | bytes 1572872 | tf_op jit(solution)/shard_map/ppermute | solution.py:402
  611.8 17.7 %collective-permute-start.113 = (bf16[4,72,512]{2,1,0:T(8,128)(2,1)S(1)}, bf16[4,72,512]{2,1,0:T(8,128)(2,1)S(1)}, u32[]{:S(2)}, u32[]{:S(2)}) collective-permute-start(bf16[4,72,512]{2,1,0:T(8,128)(2,1)S(1)} %get-tuple-element.189), channel_id=1, source_target_pairs={{0,2},{2,4},{4,6},{6,7},{7,5},{5,3},{3,1},{1,0},{8,10},{10,12},{12... | collective-permute-start | bytes 884744 | tf_op jit(solution)/shard_map/ppermute | solution.py:402
  629.5 22.6 %collective-permute-start.83 = (bf16[512,512]{1,0:T(8,128)(2,1)S(1)}, bf16[512,512]{1,0:T(8,128)(2,1)S(1)}, u32[]{:S(2)}, u32[]{:S(2)}) collective-permute-start(bf16[512,512]{1,0:T(8,128)(2,1)S(1)} %copy-done.66), channel_id=1, source_target_pairs={{1,0},{3,2},{5,4},{7,6},{0,1},{2,3},{4,5},{6,7},{9,8},{11,10},{13,... | collective-permute-start | bytes 1572872 | tf_op jit(solution)/shard_map/ppermute | solution.py:402
  629.5 23.3 %collective-permute-start.85 = (bf16[512,512]{1,0:T(8,128)(2,1)S(1)}, bf16[512,512]{1,0:T(8,128)(2,1)S(1)}, u32[]{:S(2)}, u32[]{:S(2)}) collective-permute-start(bf16[512,512]{1,0:T(8,128)(2,1)S(1)} %add_convert_fusion.4), channel_id=1, source_target_pairs={{2,0},{3,1},{4,2},{5,3},{6,4},{7,5},{10,8},{11,9},{12,10},{13,11},... | collective-permute-start | bytes 1572872 | tf_op jit(solution)/shard_map/ppermute | solution.py:402
  632.7 21.9 %collective-permute-start.115 = (bf16[72,512]{1,0:T(8,128)(2,1)S(1)}, bf16[72,512]{1,0:T(8,128)(2,1)S(1)}, u32[]{:S(2)}, u32[]{:S(2)}) collective-permute-start(bf16[72,512]{1,0:T(8,128)(2,1)S(1)} %get-tuple-element.253), channel_id=1, source_target_pairs={{0,8},{8,0},{16,24},{24,16},{1,9},{9,1},{17,25},{25,17},{2,10},{10... | collective-permute-start | bytes 221192 | tf_op jit(solution)/shard_map/ppermute | solution.py:399
  652.1 49.8 %collective-permute-start.117 = (bf16[72,512]{1,0:T(8,128)(2,1)}, bf16[72,512]{1,0:T(8,128)(2,1)}, u32[]{:S(2)}, u32[]{:S(2)}) collective-permute-start(bf16[72,512]{1,0:T(8,128)(2,1)} %get-tuple-element.251), channel_id=1, source_target_pairs={{0,24},{8,16},{16,8},{24,0},{1,25},{9,17},{17,9},{25,1},{2,26},{10... | collective-permute-start | bytes 221192 | tf_op jit(solution)/shard_map/ppermute | solution.py:399
  689.4 17.6 %collective-permute-start.96 = (bf16[4,72,512]{2,1,0:T(8,128)(2,1)S(1)}, bf16[4,72,512]{2,1,0:T(8,128)(2,1)S(1)}, u32[]{:S(2)}, u32[]{:S(2)}) collective-permute-start(bf16[4,72,512]{2,1,0:T(8,128)(2,1)S(1)} %get-tuple-element.240), channel_id=1, source_target_pairs={{0,2},{2,4},{4,6},{6,7},{7,5},{5,3},{3,1},{1,0},{8,10},{10,12},{12... | collective-permute-start | bytes 884744 | tf_op jit(solution)/shard_map/ppermute | solution.py:402
  690.3 18.3 %collective-permute-start.97 = (bf16[4,72,512]{2,1,0:T(8,128)(2,1)S(1)}, bf16[4,72,512]{2,1,0:T(8,128)(2,1)S(1)}, u32[]{:S(2)}, u32[]{:S(2)}) collective-permute-start(bf16[4,72,512]{2,1,0:T(8,128)(2,1)S(1)} %get-tuple-element.239), channel_id=1, source_target_pairs={{2,0},{4,2},{6,4},{7,6},{5,7},{3,5},{1,3},{0,1},{10,8},{12,10},{14... | collective-permute-start | bytes 884744 | tf_op jit(solution)/shard_map/ppermute | solution.py:402
  (173 other events, 2095.0 us)

commit v4 on v3

--- a/solution.py
+++ b/solution.py
@@ -568,11 +568,10 @@
     blank = jnp.zeros((-2 * gate_weight.shape[0] % 128, width), bf16)
 
     def unit_rows(weight):
+        weight = after(weight, rows_in[2])
         across = flip(weight, 2)
         beside = flip(weight, 1)
         both = flip(after(across, line[reach]), 1)
-        weight, beside = after(weight, rows_in[2]), after(beside, rows_in[2])
-        across = after(across, side[1])
         return jnp.concatenate([weight, across, blank, beside, both, blank], axis=0)
 
     gate_units, up_units, down_units = (
@@ -723,13 +722,14 @@
 
     gain_parts = jnp.stack([first_part, second_part, third_part, fourth_part])
     gain_parts = gain_parts.reshape(4, seq_count, count, own_rows)
-    gain_sums = gain_parts
-    bits = 1
-    while bits < count:
-        pairs = [(i, i ^ bits) for i in range(count)]
-        gain_sums = gain_sums + hop(gain_sums, pairs)
-        bits *= 2
-    gain_sums = lax.dynamic_slice_in_dim(gain_sums, fsdp_rank, 1, 2)[:, :, 0]
+    gain_sums = None
+    for step in range(count):
+        piece = lax.dynamic_slice_in_dim(gain_parts, lax.rem(fsdp_rank + step, count), 1, 2)
+        if step:
+            pairs = [(i, (i + step) % count) for i in range(count)]
+            piece = hop(piece, pairs)
+        gain_sums = piece if gain_sums is None else gain_sums + piece
+    gain_sums = gain_sums[:, :, 0]
     gain_grads = None
     for j in range(seq_count):
         piece = lax.dynamic_slice_in_dim(gain_sums, seq_rank ^ j, 1, 1)[:, 0]

time: 779 us -> 771 us (0.990)
  starting transfers between devices: 126 us -> 137 us
    ppermute x80 -> x84, waiting for transfers between devices: 227 us -> 182 us  [hop(): return lax.ppermute(value, 'fsdp', pairs)]
    ppermute x44, waiting for transfers between devices: 55.6 us -> 94.2 us  [flip(): return lax.ppermute(value, 'seq', [(i, i ^ bits) for i in range(seq_count)])]
    ppermute x80 -> x84, starting transfers between devices: 106 us -> 117 us  [hop(): return lax.ppermute(value, 'fsdp', pairs)]
    unnamed x197 -> x181, local copies, waits for them, and re-layouts: 38.3 us -> 31.9 us
  transfers between devices with their start and end apart: 124 -> 128, of which waited for: 63 -> 61; matrix products, arithmetic and copies ran while one was open for 33% -> 30% of each run, Pallas kernels for 4% -> 4%
where the time goes in v4:
time: 771 us; the launch traced here: 760 us
  waiting for transfers between devices  276 us (36%)
  matrix products  196 us (25%)
  starting transfers between devices  137 us (18%)
  local copies, waits for them, and re-layouts  61.8 us (8%)
  other arithmetic  55.6 us (7%)
  Pallas kernels  29.9 us (4%)
    ppermute x84, waiting for transfers between devices, hop(): return lax.ppermute(value, 'fsdp', pairs)  182 us
    ppermute x84, starting transfers between devices, hop(): return lax.ppermute(value, 'fsdp', pairs)  117 us
    ppermute x44, waiting for transfers between devices, flip(): return lax.ppermute(value, 'seq', [(i, i ^ bits) for i in range(seq_count)])  94.2 us
    dot_general x17, matrix products, contract_cols(): lax.dot_general(left, right, (((1,), (1,)), ((), ())), preferred_element_...  92.4 us
    dot_general x8, matrix products, contract_rows(): lax.dot_general(left, right, (((0,), (0,)), ((), ())), preferred_element_...  35.7 us
    unnamed x181, local copies, waits for them, and re-layouts  31.9 us
    dot_general x5, matrix products, layer(): jnp.dot(hidden, down_units, preferred_element_type=jnp.float32)  21.7 us
    dot_general x5, matrix products, layer(): jnp.dot(gate_delta, gate_units, preferred_element_type=jnp.float32)  21.4 us
  transfers between devices with their start and end apart: 128, of which 61 were waited for; matrix products, arithmetic and copies ran while one was open for 30% of the time, Pallas kernels for 4%

profile of v4, /device:TPU:0, one launch (start us, length us, event | category | flops | bytes accessed | tf_op | source)
XLA Modules:
  0.0 760.1 jit_solution(6583679587223093384)
XLA Ops:
  36.4 10.3 %collective-permute-done.4 = bf16[128,2304]{1,0:T(8,128)(2,1)S(1)} collective-permute-done((bf16[128,2304]{1,0:T(8,128)(2,1)S(1)}, bf16[128,2304]{1,0:T(8,128)(2,1)S(1)}, u32[]{:S(2)}, u32[]{:S(2)}) %collective-permute-start.4) | collective-permute-done | bytes 589856 | tf_op jit(solution)/shard_map/ppermute | solution.py:399
  54.7 8.5 %collective-permute-done.13 = bf16[4,72,1024]{2,1,0:T(8,128)(2,1)S(1)} collective-permute-done((bf16[4,72,1024]{2,1,0:T(8,128)(2,1)S(1)}, bf16[4,72,1024]{2,1,0:T(8,128)(2,1)S(1)}, u32[]{:S(2)}, u32[]{:S(2)}) %collective-permute-start.13) | collective-permute-done | bytes 589856 | tf_op jit(solution)/shard_map/ppermute | solution.py:402
  73.5 5.7 collective-permute-done.15
  86.1 21.1 %collective-permute-done.41 = bf16[288,2304]{1,0:T(8,128)(2,1)S(1)} collective-permute-done((bf16[288,2304]{1,0:T(8,128)(2,1)S(1)}, bf16[288,2304]{1,0:T(8,128)(2,1)S(1)}, u32[]{:S(2)}, u32[]{:S(2)}) %collective-permute-start.41) | collective-permute-done | bytes 1327136 | tf_op jit(solution)/shard_map/ppermute | solution.py:399
  114.3 20.6 %collective-permute-done.44 = bf16[288,2304]{1,0:T(8,128)(2,1)S(1)} collective-permute-done((bf16[288,2304]{1,0:T(8,128)(2,1)S(1)}, bf16[288,2304]{1,0:T(8,128)(2,1)S(1)}, u32[]{:S(2)}, u32[]{:S(2)}) %collective-permute-start.44) | collective-permute-done | bytes 1327136 | tf_op jit(solution)/shard_map/ppermute | solution.py:399
  139.1 6.9 project.1
  158.4 6.2 collective-permute-done.20
  174.8 11.1 %collective-permute-done.31 = bf16[4,72,512]{2,1,0:T(8,128)(2,1)S(1)} collective-permute-done((bf16[4,72,512]{2,1,0:T(8,128)(2,1)S(1)}, bf16[4,72,512]{2,1,0:T(8,128)(2,1)S(1)}, u32[]{:S(2)}, u32[]{:S(2)}) %collective-permute-start.31) | collective-permute-done | bytes 294944 | tf_op jit(solution)/shard_map/ppermute | solution.py:402
  194.5 7.9 %collective-permute-done.23 = bf16[512,512]{1,0:T(8,128)(2,1)S(1)} collective-permute-done((bf16[512,512]{1,0:T(8,128)(2,1)S(1)}, bf16[512,512]{1,0:T(8,128)(2,1)S(1)}, u32[]{:S(2)}, u32[]{:S(2)}) %collective-permute-start.23) | collective-permute-done | bytes 524320 | tf_op jit(solution)/shard_map/ppermute | solution.py:402
  204.2 7.0 attend.1
  226.2 8.1 %collective-permute-done.37 = bf16[128,2304]{1,0:T(8,128)(2,1)S(1)} collective-permute-done((bf16[128,2304]{1,0:T(8,128)(2,1)S(1)}, bf16[128,2304]{1,0:T(8,128)(2,1)S(1)}, u32[]{:S(2)}, u32[]{:S(2)}) %collective-permute-start.37) | collective-permute-done | bytes 589856 | tf_op jit(solution)/shard_map/ppermute | solution.py:399
  267.1 5.6 collective-permute-done.49
  285.3 5.9 collective-permute-done.51
  298.0 6.0 constant_dynamic-update-slice_fusion.49
  304.1 6.4 fusion.181
  310.5 5.6 constant_dynamic-update-slice_fusion.48
  338.4 8.0 %collective-permute-done.57 = bf16[128,2304]{1,0:T(8,128)(2,1)S(1)} collective-permute-done((bf16[128,2304]{1,0:T(8,128)(2,1)S(1)}, bf16[128,2304]{1,0:T(8,128)(2,1)S(1)}, u32[]{:S(2)}, u32[]{:S(2)}) %collective-permute-start.57) | collective-permute-done | bytes 589856 | tf_op jit(solution)/shard_map/ppermute | solution.py:402
  353.4 8.0 %collective-permute-done.59 = bf16[128,2304]{1,0:T(8,128)(2,1)S(1)} collective-permute-done((bf16[128,2304]{1,0:T(8,128)(2,1)S(1)}, bf16[128,2304]{1,0:T(8,128)(2,1)S(1)}, u32[]{:S(2)}, u32[]{:S(2)}) %collective-permute-start.59) | collective-permute-done | bytes 589856 | tf_op jit(solution)/shard_map/ppermute | solution.py:402
  365.3 8.2 %collective-permute-done.61 = bf16[128,2304]{1,0:T(8,128)(2,1)} collective-permute-done((bf16[128,2304]{1,0:T(8,128)(2,1)}, bf16[128,2304]{1,0:T(8,128)(2,1)}, u32[]{:S(2)}, u32[]{:S(2)}) %collective-permute-start.61) | collective-permute-done | bytes 589856 | tf_op jit(solution)/shard_map/ppermute | solution.py:402
  383.3 5.9 constant_dynamic-update-slice_fusion.33
  393.4 6.8 constant_dynamic-update-slice_fusion.32
  490.5 7.8 %collective-permute-done.73 = bf16[128,2304]{1,0:T(8,128)(2,1)S(1)} collective-permute-done((bf16[128,2304]{1,0:T(8,128)(2,1)S(1)}, bf16[128,2304]{1,0:T(8,128)(2,1)S(1)}, u32[]{:S(2)}, u32[]{:S(2)}) %collective-permute-start.73) | collective-permute-done | bytes 589856 | tf_op jit(solution)/shard_map/ppermute | solution.py:402
  507.1 6.3 collective-permute-done.75
  588.5 6.3 collective-permute-start.117
  595.1 7.3 attend_back.5
  618.6 18.4 %collective-permute-done.123 = bf16[288,2304]{1,0:T(8,128)(2,1)S(1)} collective-permute-done((bf16[288,2304]{1,0:T(8,128)(2,1)}, bf16[288,2304]{1,0:T(8,128)(2,1)S(1)}, u32[]{:S(2)}, u32[]{:S(2)}) %collective-permute-start.123) | collective-permute-done | bytes 1327136 | tf_op jit(solution)/shard_map/ppermute | solution.py:399
  645.4 13.1 %collective-permute-done.86 = bf16[512,512]{1,0:T(8,128)(2,1)S(1)} collective-permute-done((bf16[512,512]{1,0:T(8,128)(2,1)S(1)}, bf16[512,512]{1,0:T(8,128)(2,1)S(1)}, u32[]{:S(2)}, u32[]{:S(2)}) %collective-permute-start.86) | collective-permute-done | bytes 524320 | tf_op jit(solution)/shard_map/ppermute | solution.py:402
  666.7 9.3 %fusion.4 = (f32[2304]{0:T(1024)}, bf16[512,2304]{1,0:T(8,128)(2,1)}, f32[512,2304]{1,0:T(8,128)}) fusion(f32[512]{0:T(512)S(1)} %copy-done.46, bf16[128,2304]{1,0:T(8,128)(2,1)S(1)} %copy-done.14, bf16[128,2304]{1,0:T(8,128)(2,1)S(1)} %copy-done.10, bf16[128,2304]{1,0:T(8,128)(2,1)S(1)} %copy-done.12, bf16[128,2304]{1,0:T(8,128)(2,1)S(1)} %copy-done.3, ...), kind=kOutput, calls=%fused_computation.14 | convolution fusion | flops 2433218304 | bytes 15215616 | tf_op jit(solution)/shard_map/dot_general | solution.py:77
  693.5 6.6 collective-permute-done.100
  707.6 10.4 %collective-permute-done.102 = bf16[4,72,1024]{2,1,0:T(8,128)(2,1)S(1)} collective-permute-done((bf16[4,72,1024]{2,1,0:T(8,128)(2,1)S(1)}, bf16[4,72,1024]{2,1,0:T(8,128)(2,1)S(1)}, u32[]{:S(2)}, u32[]{:S(2)}) %collective-permute-start.102) | collective-permute-done | bytes 589856 | tf_op jit(solution)/shard_map/ppermute | solution.py:402
  721.8 11.7 %collective-permute-done.104 = bf16[4,72,1024]{2,1,0:T(8,128)(2,1)S(1)} collective-permute-done((bf16[4,72,1024]{2,1,0:T(8,128)(2,1)S(1)}, bf16[4,72,1024]{2,1,0:T(8,128)(2,1)S(1)}, u32[]{:S(2)}, u32[]{:S(2)}) %collective-permute-start.104) | collective-permute-done | bytes 589856 | tf_op jit(solution)/shard_map/ppermute | solution.py:402
  738.7 10.1 %collective-permute-done.106 = bf16[4,72,1024]{2,1,0:T(8,128)(2,1)S(1)} collective-permute-done((bf16[4,72,1024]{2,1,0:T(8,128)(2,1)S(1)}, bf16[4,72,1024]{2,1,0:T(8,128)(2,1)S(1)}, u32[]{:S(2)}, u32[]{:S(2)}) %collective-permute-start.106) | collective-permute-done | bytes 589856 | tf_op jit(solution)/shard_map/ppermute | solution.py:402
  (635 shorter events, 469.5 us)
Async XLA Ops:
  2.7 26.1 %collective-permute-start = (bf16[72,1024]{1,0:T(8,128)(2,1)S(1)}, bf16[72,1024]{1,0:T(8,128)(2,1)S(1)}, u32[]{:S(2)}, u32[]{:S(2)}) collective-permute-start(bf16[72,1024]{1,0:T(8,128)(2,1)S(1)} %pad_maximum_fusion.7), channel_id=1, source_target_pairs={{0,8},{8,0},{16,24},{24,16},{1,9},{9,1},{17,25},{25,17},{2,10},{10... | collective-permute-start | bytes 442376 | tf_op jit(solution)/shard_map/ppermute | solution.py:399
  3.3 25.6 %collective-permute-start.1 = (bf16[72,1024]{1,0:T(8,128)(2,1)S(1)}, bf16[72,1024]{1,0:T(8,128)(2,1)S(1)}, u32[]{:S(2)}, u32[]{:S(2)}) collective-permute-start(bf16[72,1024]{1,0:T(8,128)(2,1)S(1)} %pad_maximum_fusion.8), channel_id=1, source_target_pairs={{0,16},{8,24},{16,0},{24,8},{1,17},{9,25},{17,1},{25,9},{2,18},{10... | collective-permute-start | bytes 442376 | tf_op jit(solution)/shard_map/ppermute | solution.py:399
  5.9 23.1 %collective-permute-start.2 = (bf16[72,1024]{1,0:T(8,128)(2,1)S(1)}, bf16[72,1024]{1,0:T(8,128)(2,1)S(1)}, u32[]{:S(2)}, u32[]{:S(2)}) collective-permute-start(bf16[72,1024]{1,0:T(8,128)(2,1)S(1)} %pad_maximum_fusion.9), channel_id=1, source_target_pairs={{0,24},{8,16},{16,8},{24,0},{1,25},{9,17},{17,9},{25,1},{2,26},{10... | collective-permute-start | bytes 442376 | tf_op jit(solution)/shard_map/ppermute | solution.py:399
  29.0 18.5 %collective-permute-start.11 = (bf16[4,72,1024]{2,1,0:T(8,128)(2,1)S(1)}, bf16[4,72,1024]{2,1,0:T(8,128)(2,1)S(1)}, u32[]{:S(2)}, u32[]{:S(2)}) collective-permute-start(bf16[4,72,1024]{2,1,0:T(8,128)(2,1)S(1)} %bitcast_dynamic-update-slice_fusion.15), channel_id=1, source_target_pairs={{0,2},{2,4},{4,6},{6,7},{7,5},{5,3},{3,1},{1,0},{8,10},{10,12},{12... | collective-permute-start | bytes 1769480 | tf_op jit(solution)/shard_map/ppermute | solution.py:402
  32.3 17.9 %collective-permute-start.12 = (bf16[4,72,1024]{2,1,0:T(8,128)(2,1)S(1)}, bf16[4,72,1024]{2,1,0:T(8,128)(2,1)S(1)}, u32[]{:S(2)}, u32[]{:S(2)}) collective-permute-start(bf16[4,72,1024]{2,1,0:T(8,128)(2,1)S(1)} %bitcast_dynamic-update-slice_fusion.15), channel_id=1, source_target_pairs={{2,0},{4,2},{6,4},{7,6},{5,7},{3,5},{1,3},{0,1},{10,8},{12,10},{14... | collective-permute-start | bytes 1769480 | tf_op jit(solution)/shard_map/ppermute | solution.py:402
  32.8 21.9 %collective-permute-start.3 = (bf16[128,2304]{1,0:T(8,128)(2,1)S(1)}, bf16[128,2304]{1,0:T(8,128)(2,1)S(1)}, u32[]{:S(2)}, u32[]{:S(2)}) collective-permute-start(bf16[128,2304]{1,0:T(8,128)(2,1)S(1)} %copy-done.2), channel_id=1, source_target_pairs={{0,8},{8,0},{16,24},{24,16},{1,9},{9,1},{17,25},{25,17},{2,10},{10... | collective-permute-start | bytes 1769480 | tf_op jit(solution)/shard_map/ppermute | solution.py:399
  46.8 36.9 %collective-permute-start.38 = (bf16[288,2304]{1,0:T(8,128)(2,1)S(1)}, bf16[288,2304]{1,0:T(8,128)(2,1)}, u32[]{:S(2)}, u32[]{:S(2)}) collective-permute-start(bf16[288,2304]{1,0:T(8,128)(2,1)S(1)} %copy-done.16), channel_id=1, source_target_pairs={{0,16},{8,24},{16,0},{24,8},{1,17},{9,25},{17,1},{25,9},{2,18},{10... | collective-permute-start | bytes 3981320 | tf_op jit(solution)/shard_map/ppermute | solution.py:399
  54.7 55.2 %collective-permute-start.39 = (bf16[288,2304]{1,0:T(8,128)(2,1)S(1)}, bf16[288,2304]{1,0:T(8,128)(2,1)S(1)}, u32[]{:S(2)}, u32[]{:S(2)}) collective-permute-start(bf16[288,2304]{1,0:T(8,128)(2,1)S(1)} %copy-done.16), channel_id=1, source_target_pairs={{0,8},{8,0},{16,24},{24,16},{1,9},{9,1},{17,25},{25,17},{2,10},{10... | collective-permute-start | bytes 3981320 | tf_op jit(solution)/shard_map/ppermute | solution.py:399
  63.2 44.0 %collective-permute-start.41 = (bf16[288,2304]{1,0:T(8,128)(2,1)S(1)}, bf16[288,2304]{1,0:T(8,128)(2,1)S(1)}, u32[]{:S(2)}, u32[]{:S(2)}) collective-permute-start(bf16[288,2304]{1,0:T(8,128)(2,1)S(1)} %copy-done.17), channel_id=1, source_target_pairs={{0,16},{8,24},{16,0},{24,8},{1,17},{9,25},{17,1},{25,9},{2,18},{10... | collective-permute-start | bytes 3981320 | tf_op jit(solution)/shard_map/ppermute | solution.py:399
  79.2 33.8 %collective-permute-start.42 = (bf16[288,2304]{1,0:T(8,128)(2,1)S(1)}, bf16[288,2304]{1,0:T(8,128)(2,1)S(1)}, u32[]{:S(2)}, u32[]{:S(2)}) collective-permute-start(bf16[288,2304]{1,0:T(8,128)(2,1)S(1)} %copy-done.17), channel_id=1, source_target_pairs={{0,8},{8,0},{16,24},{24,16},{1,9},{9,1},{17,25},{25,17},{2,10},{10... | collective-permute-start | bytes 3981320 | tf_op jit(solution)/shard_map/ppermute | solution.py:399
  80.4 54.5 %collective-permute-start.44 = (bf16[288,2304]{1,0:T(8,128)(2,1)S(1)}, bf16[288,2304]{1,0:T(8,128)(2,1)S(1)}, u32[]{:S(2)}, u32[]{:S(2)}) collective-permute-start(bf16[288,2304]{1,0:T(8,128)(2,1)S(1)} %copy-done.18), channel_id=1, source_target_pairs={{0,16},{8,24},{16,0},{24,8},{1,17},{9,25},{17,1},{25,9},{2,18},{10... | collective-permute-start | bytes 3981320 | tf_op jit(solution)/shard_map/ppermute | solution.py:399
  83.6 131.8 %collective-permute-start.45 = (bf16[288,2304]{1,0:T(8,128)(2,1)S(1)}, bf16[288,2304]{1,0:T(8,128)(2,1)}, u32[]{:S(2)}, u32[]{:S(2)}) collective-permute-start(bf16[288,2304]{1,0:T(8,128)(2,1)S(1)} %copy-done.18), channel_id=1, source_target_pairs={{0,8},{8,0},{16,24},{24,16},{1,9},{9,1},{17,25},{25,17},{2,10},{10... | collective-permute-start | bytes 3981320 | tf_op jit(solution)/shard_map/ppermute | solution.py:399
  107.2 28.9 %collective-permute-start.17 = (bf16[4,72,512]{2,1,0:T(8,128)(2,1)S(1)}, bf16[4,72,512]{2,1,0:T(8,128)(2,1)S(1)}, u32[]{:S(2)}, u32[]{:S(2)}) collective-permute-start(bf16[4,72,512]{2,1,0:T(8,128)(2,1)S(1)} %slice.290), channel_id=1, source_target_pairs={{0,2},{2,4},{4,6},{6,7},{7,5},{5,3},{3,1},{1,0},{8,10},{10,12},{12... | collective-permute-start | bytes 884744 | tf_op jit(solution)/shard_map/ppermute | solution.py:402
  110.0 26.2 %collective-permute-start.18 = (bf16[4,72,512]{2,1,0:T(8,128)(2,1)S(1)}, bf16[4,72,512]{2,1,0:T(8,128)(2,1)S(1)}, u32[]{:S(2)}, u32[]{:S(2)}) collective-permute-start(bf16[4,72,512]{2,1,0:T(8,128)(2,1)S(1)} %slice.291), channel_id=1, source_target_pairs={{2,0},{4,2},{6,4},{7,6},{5,7},{3,5},{1,3},{0,1},{10,8},{12,10},{14... | collective-permute-start | bytes 884744 | tf_op jit(solution)/shard_map/ppermute | solution.py:402
  136.2 18.2 %collective-permute-start.27 = (bf16[4,72,512]{2,1,0:T(8,128)(2,1)S(1)}, bf16[4,72,512]{2,1,0:T(8,128)(2,1)S(1)}, u32[]{:S(2)}, u32[]{:S(2)}) collective-permute-start(bf16[4,72,512]{2,1,0:T(8,128)(2,1)S(1)} %bitcast_dynamic-update-slice_fusion.18), channel_id=1, source_target_pairs={{0,2},{2,4},{4,6},{6,7},{7,5},{5,3},{3,1},{1,0},{8,10},{10,12},{12... | collective-permute-start | bytes 884744 | tf_op jit(solution)/shard_map/ppermute | solution.py:402
  136.3 19.7 %collective-permute-start.28 = (bf16[4,72,512]{2,1,0:T(8,128)(2,1)S(1)}, bf16[4,72,512]{2,1,0:T(8,128)(2,1)S(1)}, u32[]{:S(2)}, u32[]{:S(2)}) collective-permute-start(bf16[4,72,512]{2,1,0:T(8,128)(2,1)S(1)} %bitcast_dynamic-update-slice_fusion.18), channel_id=1, source_target_pairs={{2,0},{4,2},{6,4},{7,6},{5,7},{3,5},{1,3},{0,1},{10,8},{12,10},{14... | collective-permute-start | bytes 884744 | tf_op jit(solution)/shard_map/ppermute | solution.py:402
  146.1 18.6 %collective-permute-start.19 = (bf16[512,512]{1,0:T(8,128)(2,1)}, bf16[512,512]{1,0:T(8,128)(2,1)S(1)}, u32[]{:S(2)}, u32[]{:S(2)}) collective-permute-start(bf16[512,512]{1,0:T(8,128)(2,1)} %get-tuple-element.68), channel_id=1, source_target_pairs={{0,1},{2,3},{4,5},{6,7},{8,9},{10,11},{12,13},{14,15},{16,17},{18,... | collective-permute-start | bytes 1572872 | tf_op jit(solution)/shard_map/ppermute | solution.py:402
  156.0 17.3 %collective-permute-start.30 = (bf16[4,72,512]{2,1,0:T(8,128)(2,1)S(1)}, bf16[4,72,512]{2,1,0:T(8,128)(2,1)S(1)}, u32[]{:S(2)}, u32[]{:S(2)}) collective-permute-start(bf16[4,72,512]{2,1,0:T(8,128)(2,1)S(1)} %collective-permute-done.28), channel_id=1, source_target_pairs={{2,0},{4,2},{6,4},{7,6},{5,7},{3,5},{1,3},{0,1},{10,8},{12,10},{14... | collective-permute-start | bytes 884744 | tf_op jit(solution)/shard_map/ppermute | solution.py:402
  164.6 29.8 %collective-permute-start.21 = (bf16[512,512]{1,0:T(8,128)(2,1)S(1)}, bf16[512,512]{1,0:T(8,128)(2,1)S(1)}, u32[]{:S(2)}, u32[]{:S(2)}) collective-permute-start(bf16[512,512]{1,0:T(8,128)(2,1)S(1)} %collective-permute-done.20), channel_id=1, source_target_pairs={{0,1},{2,3},{4,5},{6,7},{1,0},{3,2},{5,4},{7,6},{8,9},{10,11},{12,... | collective-permute-start | bytes 1572872 | tf_op jit(solution)/shard_map/ppermute | solution.py:402
  164.6 24.7 %collective-permute-start.22 = (bf16[512,512]{1,0:T(8,128)(2,1)S(1)}, bf16[512,512]{1,0:T(8,128)(2,1)S(1)}, u32[]{:S(2)}, u32[]{:S(2)}) collective-permute-start(bf16[512,512]{1,0:T(8,128)(2,1)S(1)} %collective-permute-done.20), channel_id=1, source_target_pairs={{0,2},{1,3},{2,4},{3,5},{4,6},{5,7},{8,10},{9,11},{10,12},{11,13},... | collective-permute-start | bytes 1572872 | tf_op jit(solution)/shard_map/ppermute | solution.py:402
  194.5 24.6 %collective-permute-start.40 = (bf16[288,2304]{1,0:T(8,128)(2,1)}, bf16[288,2304]{1,0:T(8,128)(2,1)}, u32[]{:S(2)}, u32[]{:S(2)}) collective-permute-start(bf16[288,2304]{1,0:T(8,128)(2,1)} %collective-permute-done.38), channel_id=1, source_target_pairs={{0,8},{8,0},{16,24},{24,16},{1,9},{9,1},{17,25},{25,17},{2,10},{10... | collective-permute-start | bytes 3981320 | tf_op jit(solution)/shard_map/ppermute | solution.py:399
  459.2 86.1 %collective-permute-start.126 = (bf16[640,2304]{1,0:T(8,128)(2,1)}, bf16[640,2304]{1,0:T(8,128)(2,1)}, u32[]{:S(2)}, u32[]{:S(2)}) collective-permute-start(bf16[640,2304]{1,0:T(8,128)(2,1)} %convolution_convert_fusion), channel_id=1, source_target_pairs={{0,8},{8,0},{16,24},{24,16},{1,9},{9,1},{17,25},{25,17},{2,10},{10... | collective-permute-start | bytes 8847368 | tf_op jit(solution)/shard_map/ppermute | solution.py:399
  479.0 69.6 %collective-permute-start.124 = (bf16[640,2304]{1,0:T(8,128)(2,1)}, bf16[640,2304]{1,0:T(8,128)(2,1)}, u32[]{:S(2)}, u32[]{:S(2)}) collective-permute-start(bf16[640,2304]{1,0:T(8,128)(2,1)} %convolution_convert_fusion.2), channel_id=1, source_target_pairs={{0,8},{8,0},{16,24},{24,16},{1,9},{9,1},{17,25},{25,17},{2,10},{10... | collective-permute-start | bytes 8847368 | tf_op jit(solution)/shard_map/ppermute | solution.py:399
  522.1 36.4 %collective-permute-start.122 = (bf16[640,2304]{1,0:T(8,128)(2,1)}, bf16[640,2304]{1,0:T(8,128)(2,1)}, u32[]{:S(2)}, u32[]{:S(2)}) collective-permute-start(bf16[640,2304]{1,0:T(8,128)(2,1)} %convolution_convert_fusion.4), channel_id=1, source_target_pairs={{0,8},{8,0},{16,24},{24,16},{1,9},{9,1},{17,25},{25,17},{2,10},{10... | collective-permute-start | bytes 8847368 | tf_op jit(solution)/shard_map/ppermute | solution.py:399
  548.4 59.7 %collective-permute-start.127 = (bf16[288,2304]{1,0:T(8,128)(2,1)}, bf16[288,2304]{1,0:T(8,128)(2,1)}, u32[]{:S(2)}, u32[]{:S(2)}) collective-permute-start(bf16[288,2304]{1,0:T(8,128)(2,1)} %add_convert_fusion), channel_id=1, source_target_pairs={{0,16},{8,24},{16,0},{24,8},{1,17},{9,25},{17,1},{25,9},{2,18},{10... | collective-permute-start | bytes 3981320 | tf_op jit(solution)/shard_map/ppermute | solution.py:399
  551.7 63.1 %collective-permute-start.125 = (bf16[288,2304]{1,0:T(8,128)(2,1)}, bf16[288,2304]{1,0:T(8,128)(2,1)S(1)}, u32[]{:S(2)}, u32[]{:S(2)}) collective-permute-start(bf16[288,2304]{1,0:T(8,128)(2,1)} %add_convert_fusion.1), channel_id=1, source_target_pairs={{0,16},{8,24},{16,0},{24,8},{1,17},{9,25},{17,1},{25,9},{2,18},{10... | collective-permute-start | bytes 3981320 | tf_op jit(solution)/shard_map/ppermute | solution.py:399
  578.4 23.9 %collective-permute-start.84 = (bf16[512,512]{1,0:T(8,128)(2,1)}, bf16[512,512]{1,0:T(8,128)(2,1)}, u32[]{:S(2)}, u32[]{:S(2)}) collective-permute-start(bf16[512,512]{1,0:T(8,128)(2,1)} %get-tuple-element.102), channel_id=1, source_target_pairs={{0,1},{2,3},{4,5},{6,7},{8,9},{10,11},{12,13},{14,15},{16,17},{18,... | collective-permute-start | bytes 1572872 | tf_op jit(solution)/shard_map/ppermute | solution.py:402
  602.3 34.7 %collective-permute-start.123 = (bf16[288,2304]{1,0:T(8,128)(2,1)}, bf16[288,2304]{1,0:T(8,128)(2,1)S(1)}, u32[]{:S(2)}, u32[]{:S(2)}) collective-permute-start(bf16[288,2304]{1,0:T(8,128)(2,1)} %add_convert_fusion.2), channel_id=1, source_target_pairs={{0,16},{8,24},{16,0},{24,8},{1,17},{9,25},{17,1},{25,9},{2,18},{10... | collective-permute-start | bytes 3981320 | tf_op jit(solution)/shard_map/ppermute | solution.py:399
  604.0 41.4 %collective-permute-start.82 = (bf16[512,512]{1,0:T(8,128)(2,1)}, bf16[512,512]{1,0:T(8,128)(2,1)S(1)}, u32[]{:S(2)}, u32[]{:S(2)}) collective-permute-start(bf16[512,512]{1,0:T(8,128)(2,1)} %get-tuple-element.98), channel_id=1, source_target_pairs={{1,0},{3,2},{5,4},{7,6},{9,8},{11,10},{13,12},{15,14},{17,16},{19,... | collective-permute-start | bytes 1572872 | tf_op jit(solution)/shard_map/ppermute | solution.py:402
  605.3 35.8 %collective-permute-start.83 = (bf16[512,512]{1,0:T(8,128)(2,1)}, bf16[512,512]{1,0:T(8,128)(2,1)S(1)}, u32[]{:S(2)}, u32[]{:S(2)}) collective-permute-start(bf16[512,512]{1,0:T(8,128)(2,1)} %get-tuple-element.100), channel_id=1, source_target_pairs={{1,0},{3,2},{5,4},{7,6},{0,1},{2,3},{4,5},{6,7},{9,8},{11,10},{13,... | collective-permute-start | bytes 1572872 | tf_op jit(solution)/shard_map/ppermute | solution.py:402
  608.0 33.8 %collective-permute-start.85 = (bf16[512,512]{1,0:T(8,128)(2,1)S(1)}, bf16[512,512]{1,0:T(8,128)(2,1)S(1)}, u32[]{:S(2)}, u32[]{:S(2)}) collective-permute-start(bf16[512,512]{1,0:T(8,128)(2,1)S(1)} %add_convert_fusion.4), channel_id=1, source_target_pairs={{2,0},{3,1},{4,2},{5,3},{6,4},{7,5},{10,8},{11,9},{12,10},{13,11},... | collective-permute-start | bytes 1572872 | tf_op jit(solution)/shard_map/ppermute | solution.py:402
  614.9 28.7 %collective-permute-start.119 = (bf16[72,512]{1,0:T(8,128)(2,1)S(1)}, bf16[72,512]{1,0:T(8,128)(2,1)S(1)}, u32[]{:S(2)}, u32[]{:S(2)}) collective-permute-start(bf16[72,512]{1,0:T(8,128)(2,1)S(1)} %get-tuple-element.241), channel_id=1, source_target_pairs={{0,8},{8,0},{16,24},{24,16},{1,9},{9,1},{17,25},{25,17},{2,10},{10... | collective-permute-start | bytes 221192 | tf_op jit(solution)/shard_map/ppermute | solution.py:399
  (169 other events, 1878.4 us)
